TPU v7x, 128 devices: a whole 4x4x4 slice. The times are simulated.
128 devices in a mesh: segment: 2 (over y_lo), ctx: 8 (over y_hi, z), tp: 8 (over x, core).
Axes of the slice: x: 4, y: 4 (y_hi: 2, y_lo: 2; y = y_hi * 2 + y_lo), z: 4, core: 2. Of those that a mesh axis runs over, the one named last changes fastest.
Arguments:
- stash_inputs: bfloat16 [2, 4, 2048, 3840], P('segment', None, ('ctx', 'tp')), may hold values from -12 to 12
- stash_grads: bfloat16 [2, 4, 2048, 3840], P('segment', None, ('ctx', 'tp')), may hold values from -6 to 6
- plan: int32 [2, 4], P('segment'), may hold values from 0 to 3, each once within a row
- query_weight: bfloat16 [2, 2, 3840, 4096], P('segment', None, None, 'tp'), may hold values from -0.1 to 0.1
- key_weight: bfloat16 [2, 2, 3840, 2048], P('segment', None, None, 'tp'), may hold values from -0.1 to 0.1
- value_weight: bfloat16 [2, 2, 3840, 2048], P('segment', None, None, 'tp'), may hold values from -0.09375 to 0.09375
- out_weight: bfloat16 [2, 2, 4096, 3840], P('segment', None, 'tp'), may hold values from -0.09375 to 0.09375
- input_gain: float32 [2, 2, 3840], P('segment'), may hold values from 0.1 to 1.9
- output_gain: float32 [2, 2, 3840], P('segment'), may hold values from 0.1 to 1.9
- query_gain: float32 [2, 2, 256], P('segment'), may hold values from 0.5 to 6
- key_gain: float32 [2, 2, 256], P('segment'), may hold values from 0.5 to 6
Outputs:
- arrived_act: bfloat16 [2, 2048, 3840], P('segment', ('ctx', 'tp'))
- arrived_grad: bfloat16 [2, 2048, 3840], P('segment', ('ctx', 'tp'))
Inputs may be any that keep to these rules, and one draw needn't show every extreme that they name: `plan`: row s names each of the 4 micro-batches once; its first entry is run forward and its second through its input gradient.
All inputs are finite; a program needn't handle non-finite values.
Results may differ from a plain program's by a relative error of at most 0.019.
The roundings to bfloat16 on the way count: a program that leaves them out, or rounds other values in their place, can miss the bound.
Values may be sent and summed in bfloat16 or wider, within the bound.
A program may use at most 128 MiB of HBM per device.

v0:
```python
import jax
import jax.numpy as jnp
from jax import lax
from jax.sharding import PartitionSpec as P

WINDOW = 1024


epsilon = 1e-06
rope_base = 10000.0
masked_score = -1e30


def sent_to_all(value, axis):
    copies = jnp.broadcast_to(value, (lax.axis_size(axis), *value.shape))
    return lax.all_to_all(copies, axis, split_axis=0, concat_axis=0, tiled=True)


def joined_along(tiles, dim):
    lengths = list(tiles.shape[1:])
    lengths[dim] *= tiles.shape[0]
    return jnp.moveaxis(tiles, 0, dim).reshape(lengths)


def gather_directly(value, axis, dim):
    tiles = sent_to_all(value, axis)
    return joined_along(tiles, dim)


def passed_along(value, axis, by):
    size = lax.axis_size(axis)
    pairs = [(i, i + by) for i in range(size) if 0 <= i + by < size]
    return lax.ppermute(value, axis, pairs)


def cut_along(value, dim, size):
    lengths = value.shape
    tiles = value.reshape(*lengths[:dim], size, lengths[dim] // size, *lengths[dim + 1 :])
    return jnp.moveaxis(tiles, dim, 0)


def summed_on_arrival(value, axis, dim):
    size = lax.axis_size(axis)
    tiles = lax.all_to_all(cut_along(value, dim, size), axis, 0, 0, tiled=True)
    return jnp.sum(tiles.astype(jnp.float32), axis=0)


def swapped(value, axis, apart):
    mask = 2**apart
    pairs = [(source, source ^ mask) for source in range(lax.axis_size(axis))]
    return lax.ppermute(value, axis, pairs)


def rms_scale(operand, gain):
    return operand * lax.rsqrt(jnp.mean(operand * operand, axis=-1, keepdims=True) + epsilon) * gain


def rotate(normed, positions):
    half_width = normed.shape[-1] // 2
    frequency = rope_base ** (
        -(jnp.arange(half_width).astype(normed.dtype) * 2.0 / normed.shape[-1])
    )
    angles = positions.astype(normed.dtype)[:, None] * frequency[None, :]
    cosine = jnp.cos(angles)[:, None, :]
    sines = jnp.sin(angles)[:, None, :]
    front_half = normed[..., :half_width]
    back_half = normed[..., half_width:]
    return jnp.concatenate(
        [front_half * cosine - back_half * sines, back_half * cosine + front_half * sines], axis=-1
    )


def head_norm(raw_heads, gain, positions):
    return rotate(rms_scale(raw_heads, gain), positions)


def take_leg(arrays, leg_index):
    return tuple((lax.dynamic_slice_in_dim(member, leg_index, 1, 0) for member in arrays))


def attend(queries, key_rows, value_rows, query_place, key_place):
    leg_count, row_count, head_count, head_width = queries.shape
    kv_count = key_rows.shape[2]
    grouped = queries.reshape(leg_count, row_count, kv_count, head_count // kv_count, head_width)
    scores = jnp.einsum(
        "ltkgd,lskd->lkgts", grouped, key_rows, preferred_element_type=jnp.float32
    ) * head_width ** (-0.5)
    visible = (
        (key_place[None, :] >= 0)
        & (key_place[None, :] <= query_place[:, None])
        & (key_place[None, :] > query_place[:, None] - WINDOW)
    )
    scores = jnp.where(visible, scores, masked_score)
    highest = jnp.max(scores, axis=-1, keepdims=True)
    raised = jnp.exp(scores - highest)
    weighting = raised / jnp.sum(raised, axis=-1, keepdims=True)
    weighting_low = weighting.astype(jnp.bfloat16)
    context = jnp.einsum(
        "lkgts,lskd->ltkgd", weighting_low, value_rows, preferred_element_type=jnp.float32
    )
    return (
        weighting,
        weighting_low,
        context.astype(jnp.bfloat16).reshape(leg_count, row_count, head_count * head_width),
    )


def attend_back(context_grad, queries, key_rows, value_rows, weighting, weighting_low):
    leg_count, row_count, head_count, head_width = queries.shape
    kv_count = key_rows.shape[2]
    grouped = queries.reshape(leg_count, row_count, kv_count, head_count // kv_count, head_width)
    grad_grouped = context_grad.reshape(
        leg_count, row_count, kv_count, head_count // kv_count, head_width
    )
    weight_grad = jnp.einsum(
        "ltkgd,lskd->lkgts", grad_grouped, value_rows, preferred_element_type=jnp.float32
    )
    score_grad = (
        weighting
        * (weight_grad - jnp.sum(weight_grad * weighting, axis=-1, keepdims=True))
        * head_width ** (-0.5)
    )
    score_grad = score_grad.astype(jnp.bfloat16)
    query_grad = jnp.einsum(
        "lkgts,lskd->ltkgd", score_grad, key_rows, preferred_element_type=jnp.float32
    ).reshape(leg_count, row_count, head_count, head_width)
    key_grad = jnp.einsum(
        "lkgts,ltkgd->lskd", score_grad, grouped, preferred_element_type=jnp.float32
    )
    value_grad = jnp.einsum(
        "lkgts,ltkgd->lskd", weighting_low, grad_grouped, preferred_element_type=jnp.float32
    )
    return (query_grad, key_grad, value_grad)


def forward_front(inputs, query_proj, key_proj, value_proj, in_gain, q_gain, k_gain):
    normed = rms_scale(inputs.astype(jnp.float32), in_gain[:, None, :]).astype(jnp.bfloat16)
    piece = gather_directly(normed, "tp", 1)
    projections = jnp.concatenate(
        [
            jnp.einsum("lrd,ldc->lrc", piece, matrix, preferred_element_type=jnp.float32)
            for matrix in (query_proj, key_proj, value_proj)
        ],
        axis=-1,
    )
    leg_count = projections.shape[0]
    row_count = projections.shape[1]
    head_width = q_gain.shape[-1]
    query_cols = query_proj.shape[-1]
    key_cols = key_proj.shape[-1]
    query_raw = projections[..., :query_cols].reshape(
        leg_count, row_count, query_cols // head_width, head_width
    )
    key_raw = projections[..., query_cols : query_cols + key_cols].reshape(
        leg_count, row_count, key_cols // head_width, head_width
    )
    value_own = (
        projections[..., query_cols + key_cols :]
        .astype(jnp.bfloat16)
        .reshape(leg_count, row_count, key_cols // head_width, head_width)
    )
    block_index = lax.axis_index("ctx")
    query_place = block_index * row_count + jnp.arange(row_count, dtype=jnp.int32)
    queries = head_norm(query_raw, q_gain[:, None, None, :], query_place).astype(jnp.bfloat16)
    key_own = head_norm(key_raw, k_gain[:, None, None, :], query_place).astype(jnp.bfloat16)
    reaches = min(WINDOW // row_count, lax.axis_size("ctx") - 1)
    received = [
        passed_along((key_own, value_own), "ctx", distance) for distance in range(reaches, 0, -1)
    ]
    key_rows = jnp.concatenate([couple[0] for couple in received] + [key_own], axis=1)
    value_rows = jnp.concatenate([couple[1] for couple in received] + [value_own], axis=1)
    key_place = (block_index - reaches) * row_count + jnp.arange(
        (reaches + 1) * row_count, dtype=jnp.int32
    )
    weighting, weighting_low, context = attend(
        queries, key_rows, value_rows, query_place, key_place
    )
    batched = (query_raw, key_raw, queries, key_rows, value_rows, weighting, weighting_low, context)
    return (batched, query_place, reaches)


def scatter_out(context, out_proj):
    summed = summed_on_arrival(
        jnp.einsum("lrc,lcd->rld", context, out_proj, preferred_element_type=jnp.float32).astype(
            jnp.bfloat16
        ),
        "tp",
        0,
    )
    return jnp.swapaxes(summed, 0, 1)


def per_device(
    stash_inputs,
    stash_grads,
    plan,
    query_weight,
    key_weight,
    value_weight,
    out_weight,
    input_gain,
    output_gain,
    query_gain,
    key_gain,
):
    segment_index = lax.axis_index("segment")
    other_index = 1 - segment_index
    forward_batch = plan[0, 0]
    backward_batch = plan[0, 1]
    forward_in = lax.dynamic_slice_in_dim(stash_inputs[0], forward_batch, 1, 0)
    backward_in = lax.dynamic_slice_in_dim(stash_inputs[0], backward_batch, 1, 0)
    incoming = lax.dynamic_slice_in_dim(stash_grads[0], backward_batch, 1, 0)
    stacked = (
        query_weight[0],
        key_weight[0],
        value_weight[0],
        out_weight[0],
        input_gain[0],
        output_gain[0],
        query_gain[0],
        key_gain[0],
    )
    forward_set = take_leg(stacked, segment_index)
    backward_set = take_leg(stacked, other_index)
    joined = jnp.where(
        segment_index == 0,
        jnp.concatenate([forward_in, backward_in], axis=0),
        jnp.concatenate([backward_in, forward_in], axis=0),
    )
    both_parts, query_place, reaches = forward_front(
        joined, stacked[0], stacked[1], stacked[2], stacked[4], stacked[6], stacked[7]
    )
    backward_parts = take_leg(both_parts, other_index)
    both_projected = scatter_out(both_parts[7], stacked[3])
    forward_projected = lax.dynamic_slice_in_dim(both_projected, segment_index, 1, 0)
    backward_projected = lax.dynamic_slice_in_dim(both_projected, other_index, 1, 0)
    forward_out = (
        forward_in.astype(jnp.float32) + rms_scale(forward_projected, forward_set[5][:, None, :])
    ).astype(jnp.bfloat16)
    arrived_act = swapped(forward_out, "segment", 0)
    query_raw, key_raw, queries, key_rows, value_rows, weighting, weighting_low, context = (
        backward_parts
    )
    out_back = backward_set[3]
    post_back = backward_set[5][:, None, :]
    grad_low = jax.vjp(lambda operand: rms_scale(operand, post_back), backward_projected)[1](
        incoming.astype(jnp.float32)
    )[0].astype(jnp.bfloat16)
    context_grad = jnp.einsum(
        "lrd,lcd->lrc",
        gather_directly(grad_low, "tp", 1),
        out_back,
        preferred_element_type=jnp.float32,
    ).astype(jnp.bfloat16)
    query_grad, key_grad_all, value_grad_all = attend_back(
        context_grad, queries, key_rows, value_rows, weighting, weighting_low
    )
    row_count = queries.shape[1]
    key_grad = key_grad_all[:, reaches * row_count :]
    value_grad = value_grad_all[:, reaches * row_count :]
    for distance in range(1, reaches + 1):
        begin_row = (reaches - distance) * row_count
        returned = (
            passed_along(
                key_grad_all[:, begin_row : begin_row + row_count].astype(jnp.bfloat16),
                "ctx",
                -distance,
            ).astype(jnp.float32),
            passed_along(
                value_grad_all[:, begin_row : begin_row + row_count].astype(jnp.bfloat16),
                "ctx",
                -distance,
            ).astype(jnp.float32),
        )
        key_grad = key_grad + returned[0]
        value_grad = value_grad + returned[1]
    q_gain_back = backward_set[6][:, None, None, :]
    k_gain_back = backward_set[7][:, None, None, :]
    query_low = (
        jax.vjp(lambda operand: head_norm(operand, q_gain_back, query_place), query_raw)[1](
            query_grad
        )[0]
        .astype(jnp.bfloat16)
        .reshape(1, row_count, -1)
    )
    key_low = (
        jax.vjp(lambda operand: head_norm(operand, k_gain_back, query_place), key_raw)[1](key_grad)[
            0
        ]
        .astype(jnp.bfloat16)
        .reshape(1, row_count, -1)
    )
    value_low = value_grad.astype(jnp.bfloat16).reshape(1, row_count, -1)
    summed = jnp.einsum(
        "lrc,ldc->rd", query_low, backward_set[0], preferred_element_type=jnp.float32
    )
    summed = summed + jnp.einsum(
        "lrc,ldc->rd", key_low, backward_set[1], preferred_element_type=jnp.float32
    )
    summed = summed + jnp.einsum(
        "lrc,ldc->rd", value_low, backward_set[2], preferred_element_type=jnp.float32
    )
    hidden_grad = summed_on_arrival(summed.astype(jnp.bfloat16), "tp", 0)
    in_gain_back = backward_set[4][0]
    wide_input = backward_in[0].astype(jnp.float32)
    outgoing = (
        incoming[0].astype(jnp.float32)
        + jax.vjp(lambda operand: rms_scale(operand, in_gain_back), wide_input)[1](hidden_grad)[0]
    )
    arrived_grad = swapped(outgoing.astype(jnp.bfloat16)[None], "segment", 0)
    return (arrived_act, arrived_grad)


def solution(mesh):
    return jax.shard_map(
        per_device,
        mesh=mesh,
        in_specs=(
            P("segment", None, ("ctx", "tp"), None),
            P("segment", None, ("ctx", "tp"), None),
            P("segment", None),
            P("segment", None, None, "tp"),
            P("segment", None, None, "tp"),
            P("segment", None, None, "tp"),
            P("segment", None, "tp", None),
            P("segment", None, None),
            P("segment", None, None),
            P("segment", None, None),
            P("segment", None, None),
        ),
        out_specs=(P("segment", ("ctx", "tp"), None), P("segment", ("ctx", "tp"), None)),
        check_vma=False,
    )
```

profile of v0, /device:TPU:72, one launch (start us, length us, event | category | flops | bytes accessed | tf_op | source)
XLA Modules:
  0.0 310.9 jit_solution(5591880686322541963)
XLA Ops:
  8.1 2.3 broadcast_in_dim.20
  10.4 4.5 %all-to-all-start = ((bf16[8,2,32,3840]{3,2,1,0:T(8,128)(2,1)}), bf16[8,2,32,3840]{3,2,1,0:T(8,128)(2,1)}, u32[]{:S(2)}, u32[]{:S(2)}) async-start(bf16[8,2,32,3840]{3,2,1,0:T(8,128)(2,1)} %broadcast_in_dim.20), calls=%async_computation | async-start | bytes 7864320 | tf_op jit(solution)/shard_map/all_to_all | solution.py:16
  16.8 45.0 %all-to-all-done = bf16[8,2,32,3840]{3,2,1,0:T(8,128)(2,1)} async-done(((bf16[8,2,32,3840]{3,2,1,0:T(8,128)(2,1)}), bf16[8,2,32,3840]{3,2,1,0:T(8,128)(2,1)}, u32[]{:S(2)}, u32[]{:S(2)}) %all-to-all-start) | async-done | bytes 3932192 | tf_op jit(solution)/shard_map/all_to_all | solution.py:16
  61.8 2.5 copy.59
  67.0 3.8 %collective-permute-start.3 = (bf16[2,256,1,256]{3,1,0,2:T(8,128)(2,1)}, bf16[2,256,1,256]{3,1,0,2:T(8,128)(2,1)}, u32[]{:S(2)}, u32[]{:S(2)}) collective-permute-start(bf16[2,256,1,256]{3,1,0,2:T(8,128)(2,1)} %fusion.42), channel_id=1, source_target_pairs={{0,8},{8,16},{16,24},{24,32},{32,40},{40,48},{48,56},{1,9},{9,17},... | collective-permute-start | bytes 786440 | tf_op jit(solution)/shard_map/ppermute | solution.py:33
  70.8 3.6 %collective-permute-start.2 = (bf16[2,256,1,256]{3,1,0,2:T(8,128)(2,1)}, bf16[2,256,1,256]{3,1,0,2:T(8,128)(2,1)}, u32[]{:S(2)}, u32[]{:S(2)}) collective-permute-start(bf16[2,256,1,256]{3,1,0,2:T(8,128)(2,1)} %fusion.42), channel_id=1, source_target_pairs={{0,16},{8,24},{16,32},{24,40},{32,48},{40,56},{1,17},{9,25},{17,33... | collective-permute-start | bytes 786440 | tf_op jit(solution)/shard_map/ppermute | solution.py:33
  77.1 5.5 %collective-permute-start.6 = (bf16[2,256,1,256]{1,3,0,2:T(8,128)(2,1)}, bf16[2,256,1,256]{1,3,0,2:T(8,128)(2,1)}, u32[]{:S(2)}, u32[]{:S(2)}) collective-permute-start(bf16[2,256,1,256]{1,3,0,2:T(8,128)(2,1)} %pad_maximum_fusion.2), channel_id=1, source_target_pairs={{0,16},{8,24},{16,32},{24,40},{32,48},{40,56},{1,17},{9,25},{17,33... | collective-permute-start | bytes 786440 | tf_op jit(solution)/shard_map/ppermute | solution.py:33
  82.5 2.0 collective-permute-start.5
  86.5 3.2 %fusion.2 = f32[2,256,512]{2,1,0:T(8,128)} fusion(bf16[2,256,3840]{2,1,0:T(8,128)(2,1)S(1)} %bitcast.227, bf16[1,2,3840,512]{3,2,1,0:T(8,128)(2,1)S(1)} %bitcast.236), kind=kOutput, calls=%fused_computation.2 | convolution fusion | flops 2013265920 | bytes 12845056 | tf_op jit(solution)/shard_map/lrd,ldc->lrc/dot_general | solution.py:141
  94.0 4.8 %collective-permute-done.4 = bf16[2,256,1,256]{1,3,0,2:T(8,128)(2,1)} collective-permute-done((bf16[2,256,1,256]{1,3,0,2:T(8,128)(2,1)}, bf16[2,256,1,256]{1,3,0,2:T(8,128)(2,1)}, u32[]{:S(2)}, u32[]{:S(2)}) %collective-permute-start.4) | collective-permute-done | bytes 262176 | tf_op jit(solution)/shard_map/ppermute | solution.py:33
  98.8 2.9 collective-permute-start.7
  102.7 6.4 %collective-permute-start.1 = (bf16[2,256,1,256]{3,1,0,2:T(8,128)(2,1)}, bf16[2,256,1,256]{3,1,0,2:T(8,128)(2,1)S(1)}, u32[]{:S(2)}, u32[]{:S(2)}) collective-permute-start(bf16[2,256,1,256]{3,1,0,2:T(8,128)(2,1)} %fusion.42), channel_id=1, source_target_pairs={{0,24},{8,32},{16,40},{24,48},{32,56},{1,25},{9,33},{17,41},{25,49... | collective-permute-start | bytes 786440 | tf_op jit(solution)/shard_map/ppermute | solution.py:33
  112.7 5.9 %collective-permute-done = bf16[2,256,1,256]{3,1,0,2:T(8,128)(2,1)S(1)} collective-permute-done((bf16[2,256,1,256]{3,1,0,2:T(8,128)(2,1)}, bf16[2,256,1,256]{3,1,0,2:T(8,128)(2,1)S(1)}, u32[]{:S(2)}, u32[]{:S(2)}) %collective-permute-start) | collective-permute-done | bytes 262176 | tf_op jit(solution)/shard_map/ppermute | solution.py:33
  123.8 3.5 %fusion.111 = (bf16[2,1,2,256,1280]{3,4,2,0,1:T(8,128)(2,1)S(1)}, f32[2,1,2,256,1280]{3,4,2,0,1:T(8,128)}) fusion(f32[2,2,256]{2,1,0:T(2,128)S(1)} %fusion.9, f32[2,1,2,256,1280]{3,4,2,0,1:T(8,128)S(1)} %get-tuple-element.46, f32[2,2,256]{2,1,0:T(2,128)S(1)} %get-tuple-element.45), kind=kLoop, calls=%fused_computation.186 | loop fusion | flops 3932160 | bytes 13115392 | tf_op jit(solution)/shard_map/convert_element_type | solution.py:97
  128.3 2.3 fusion.4
  130.6 2.2 copy.69
  132.9 4.7 %all-to-all-start.1 = ((bf16[8,32,2,3840]{3,1,2,0:T(8,128)(2,1)}), bf16[8,32,2,3840]{3,1,2,0:T(8,128)(2,1)}, u32[]{:S(2)}, u32[]{:S(2)}) async-start(bf16[8,32,2,3840]{3,1,2,0:T(8,128)(2,1)} %copy.69), calls=%async_computation.1 | async-start | bytes 7864320 | tf_op jit(solution)/shard_map/all_to_all | solution.py:44
  137.7 46.7 %all-to-all-done.1 = bf16[8,32,2,3840]{3,1,2,0:T(8,128)(2,1)} async-done(((bf16[8,32,2,3840]{3,1,2,0:T(8,128)(2,1)}), bf16[8,32,2,3840]{3,1,2,0:T(8,128)(2,1)}, u32[]{:S(2)}, u32[]{:S(2)}) %all-to-all-start.1) | async-done | bytes 3932192 | tf_op jit(solution)/shard_map/all_to_all | solution.py:44
  184.4 2.7 convert_reduce_fusion
  191.0 4.3 %all-to-all-start.2 = ((bf16[8,1,32,3840]{3,2,1,0:T(8,128)(2,1)}), bf16[8,1,32,3840]{3,2,1,0:T(8,128)(2,1)}, u32[]{:S(2)}, u32[]{:S(2)}) async-start(bf16[8,1,32,3840]{3,2,1,0:T(8,128)(2,1)} %broadcast_in_dim.24), calls=%async_computation.2 | async-start | bytes 3932160 | tf_op jit(solution)/shard_map/all_to_all | solution.py:16
  197.7 23.4 %all-to-all-done.2 = bf16[8,1,32,3840]{3,2,1,0:T(8,128)(2,1)} async-done(((bf16[8,1,32,3840]{3,2,1,0:T(8,128)(2,1)}), bf16[8,1,32,3840]{3,2,1,0:T(8,128)(2,1)}, u32[]{:S(2)}, u32[]{:S(2)}) %all-to-all-start.2) | async-done | bytes 1966112 | tf_op jit(solution)/shard_map/all_to_all | solution.py:16
  221.1 4.7 %fusion.39 = bf16[256,512]{1,0:T(8,128)(2,1)} fusion(bf16[256,3840]{1,0:T(8,128)(2,1)} %bitcast.36, bf16[1,2,512,3840]{3,2,1,0:T(8,128)(2,1)} %param.17, s32[]{:T(128)S(6)} %select_n.26), kind=kOutput, calls=%fused_computation.46 | convolution fusion | flops 1006764032 | bytes 6160388 | tf_op jit(solution)/shard_map/lrd,lcd->lrc/dot_general | solution.py:249
  227.6 2.1 fusion.118
  229.7 2.3 multiply_reduce_fusion
  235.4 2.1 collective-permute-start.13
  249.3 5.6 %collective-permute-done.11 = bf16[1,256,1,256]{1,3,2,0:T(8,128)(2,1)S(1)} collective-permute-done((bf16[1,256,1,256]{1,3,2,0:T(8,128)(2,1)S(1)}, bf16[1,256,1,256]{1,3,2,0:T(8,128)(2,1)S(1)}, u32[]{:S(2)}, u32[]{:S(2)}) %collective-permute-start.11) | collective-permute-done | bytes 131104 | tf_op jit(solution)/shard_map/ppermute | solution.py:33
  254.9 2.0 collective-permute-start.14
  261.8 4.6 %collective-permute-done.14 = bf16[1,256,1,256]{1,3,2,0:T(8,128)(2,1)S(1)} collective-permute-done((bf16[1,256,1,256]{1,3,2,0:T(8,128)(2,1)S(1)}, bf16[1,256,1,256]{1,3,2,0:T(8,128)(2,1)S(1)}, u32[]{:S(2)}, u32[]{:S(2)}) %collective-permute-start.14) | collective-permute-done | bytes 131104 | tf_op jit(solution)/shard_map/ppermute | solution.py:33
  266.5 2.0 fusion.7
  268.5 4.5 %all-to-all-start.3 = ((bf16[8,32,3840]{2,1,0:T(8,128)(2,1)}), bf16[8,32,3840]{2,1,0:T(8,128)(2,1)}, u32[]{:S(2)}, u32[]{:S(2)}) async-start(bf16[8,32,3840]{2,1,0:T(8,128)(2,1)} %bitcast.230), calls=%async_computation.3 | async-start | bytes 3932160 | tf_op jit(solution)/shard_map/all_to_all | solution.py:44
  274.6 24.1 %all-to-all-done.3 = bf16[8,32,3840]{2,1,0:T(8,128)(2,1)} async-done(((bf16[8,32,3840]{2,1,0:T(8,128)(2,1)}), bf16[8,32,3840]{2,1,0:T(8,128)(2,1)}, u32[]{:S(2)}, u32[]{:S(2)}) %all-to-all-start.3) | async-done | bytes 1966112 | tf_op jit(solution)/shard_map/all_to_all | solution.py:44
  303.5 6.1 %collective-permute-done.17 = bf16[1,32,3840]{2,1,0:T(8,128)(2,1)S(1)} collective-permute-done((bf16[1,32,3840]{2,1,0:T(8,128)(2,1)S(1)}, bf16[1,32,3840]{2,1,0:T(8,128)(2,1)S(1)}, u32[]{:S(2)}, u32[]{:S(2)}) %collective-permute-start.17) | collective-permute-done | bytes 245792 | tf_op jit(solution)/shard_map/ppermute | solution.py:51
  (159 shorter events, 63.0 us)
Async XLA Ops:
  10.4 51.4 %all-to-all-start = ((bf16[8,2,32,3840]{3,2,1,0:T(8,128)(2,1)}), bf16[8,2,32,3840]{3,2,1,0:T(8,128)(2,1)}, u32[]{:S(2)}, u32[]{:S(2)}) async-start(bf16[8,2,32,3840]{3,2,1,0:T(8,128)(2,1)} %broadcast_in_dim.20), calls=%async_computation | async-start | bytes 7864320 | tf_op jit(solution)/shard_map/all_to_all | solution.py:16
  15.5 60.7 %copy-start.4 = (f32[256,128]{0,1:T(8,128)}, f32[256,128]{0,1:T(8,128)S(1)}, u32[]{:S(2)}) copy-start(f32[256,128]{0,1:T(8,128)S(1)} %get-tuple-element.34) | copy-start | bytes 393220
  65.1 21.4 %slice-start.4 = ((s8[7864320]{0:T(1024)(128)(4,1)}), s8[4194304]{0:T(1024)(128)(4,1)S(1)}, s32[]{:S(2)}) async-start(s8[7864320]{0:T(1024)(128)(4,1)} %bitcast.235), calls=%async_computation.8 | async-start | bytes 8388608
  67.0 19.5 %slice-start.5 = ((s8[7864320]{0:T(1024)(128)(4,1)}), s8[3670016]{0:T(1024)(128)(4,1)S(1)}, s32[]{:S(2)}) async-start(s8[7864320]{0:T(1024)(128)(4,1)} %bitcast.235), calls=%async_computation.9 | async-start | bytes 7340032
  67.0 52.6 %collective-permute-start.3 = (bf16[2,256,1,256]{3,1,0,2:T(8,128)(2,1)}, bf16[2,256,1,256]{3,1,0,2:T(8,128)(2,1)}, u32[]{:S(2)}, u32[]{:S(2)}) collective-permute-start(bf16[2,256,1,256]{3,1,0,2:T(8,128)(2,1)} %fusion.42), channel_id=1, source_target_pairs={{0,8},{8,16},{16,24},{24,32},{32,40},{40,48},{48,56},{1,9},{9,17},... | collective-permute-start | bytes 786440 | tf_op jit(solution)/shard_map/ppermute | solution.py:33
  70.8 47.8 %collective-permute-start.2 = (bf16[2,256,1,256]{3,1,0,2:T(8,128)(2,1)}, bf16[2,256,1,256]{3,1,0,2:T(8,128)(2,1)}, u32[]{:S(2)}, u32[]{:S(2)}) collective-permute-start(bf16[2,256,1,256]{3,1,0,2:T(8,128)(2,1)} %fusion.42), channel_id=1, source_target_pairs={{0,16},{8,24},{16,32},{24,40},{32,48},{40,56},{1,17},{9,25},{17,33... | collective-permute-start | bytes 786440 | tf_op jit(solution)/shard_map/ppermute | solution.py:33
  77.1 33.0 %collective-permute-start.6 = (bf16[2,256,1,256]{1,3,0,2:T(8,128)(2,1)}, bf16[2,256,1,256]{1,3,0,2:T(8,128)(2,1)}, u32[]{:S(2)}, u32[]{:S(2)}) collective-permute-start(bf16[2,256,1,256]{1,3,0,2:T(8,128)(2,1)} %pad_maximum_fusion.2), channel_id=1, source_target_pairs={{0,16},{8,24},{16,32},{24,40},{32,48},{40,56},{1,17},{9,25},{17,33... | collective-permute-start | bytes 786440 | tf_op jit(solution)/shard_map/ppermute | solution.py:33
  82.5 20.1 %collective-permute-start.5 = (bf16[2,256,1,256]{1,3,0,2:T(8,128)(2,1)}, bf16[2,256,1,256]{1,3,0,2:T(8,128)(2,1)}, u32[]{:S(2)}, u32[]{:S(2)}) collective-permute-start(bf16[2,256,1,256]{1,3,0,2:T(8,128)(2,1)} %pad_maximum_fusion.2), channel_id=1, source_target_pairs={{0,24},{8,32},{16,40},{24,48},{32,56},{1,25},{9,33},{17,41},{25,49... | collective-permute-start | bytes 786440 | tf_op jit(solution)/shard_map/ppermute | solution.py:33
  84.5 14.3 %collective-permute-start.4 = (bf16[2,256,1,256]{1,3,0,2:T(8,128)(2,1)}, bf16[2,256,1,256]{1,3,0,2:T(8,128)(2,1)}, u32[]{:S(2)}, u32[]{:S(2)}) collective-permute-start(bf16[2,256,1,256]{1,3,0,2:T(8,128)(2,1)} %pad_maximum_fusion.2), channel_id=1, source_target_pairs={{0,32},{8,40},{16,48},{24,56},{1,33},{9,41},{17,49},{25,57},{2,34}... | collective-permute-start | bytes 786440 | tf_op jit(solution)/shard_map/ppermute | solution.py:33
  94.0 27.6 %copy-start.6 = (bf16[2,256,2,128]{3,1,2,0:T(8,128)(2,1)}, bf16[2,256,2,128]{3,1,2,0:T(8,128)(2,1)S(1)}, u32[]{:S(2)}) copy-start(bf16[2,256,2,128]{3,1,2,0:T(8,128)(2,1)S(1)} %get-tuple-element.13) | copy-start | bytes 786436
  94.0 27.6 %copy-start.8 = (bf16[2,256,2,128]{3,1,2,0:T(8,128)(2,1)}, bf16[2,256,2,128]{3,1,2,0:T(8,128)(2,1)S(1)}, u32[]{:S(2)}) copy-start(bf16[2,256,2,128]{3,1,2,0:T(8,128)(2,1)S(1)} %get-tuple-element.14) | copy-start | bytes 786436
  98.8 13.8 %collective-permute-start.7 = (bf16[2,256,1,256]{1,3,0,2:T(8,128)(2,1)}, bf16[2,256,1,256]{1,3,0,2:T(8,128)(2,1)S(1)}, u32[]{:S(2)}, u32[]{:S(2)}) collective-permute-start(bf16[2,256,1,256]{1,3,0,2:T(8,128)(2,1)} %pad_maximum_fusion.2), channel_id=1, source_target_pairs={{0,8},{8,16},{16,24},{24,32},{32,40},{40,48},{48,56},{1,9},{9,17},... | collective-permute-start | bytes 786440 | tf_op jit(solution)/shard_map/ppermute | solution.py:33
  102.7 15.9 %collective-permute-start.1 = (bf16[2,256,1,256]{3,1,0,2:T(8,128)(2,1)}, bf16[2,256,1,256]{3,1,0,2:T(8,128)(2,1)S(1)}, u32[]{:S(2)}, u32[]{:S(2)}) collective-permute-start(bf16[2,256,1,256]{3,1,0,2:T(8,128)(2,1)} %fusion.42), channel_id=1, source_target_pairs={{0,24},{8,32},{16,40},{24,48},{32,56},{1,25},{9,33},{17,41},{25,49... | collective-permute-start | bytes 786440 | tf_op jit(solution)/shard_map/ppermute | solution.py:33
  110.1 8.4 %collective-permute-start = (bf16[2,256,1,256]{3,1,0,2:T(8,128)(2,1)}, bf16[2,256,1,256]{3,1,0,2:T(8,128)(2,1)S(1)}, u32[]{:S(2)}, u32[]{:S(2)}) collective-permute-start(bf16[2,256,1,256]{3,1,0,2:T(8,128)(2,1)} %fusion.42), channel_id=1, source_target_pairs={{0,32},{8,40},{16,48},{24,56},{1,33},{9,41},{17,49},{25,57},{2,34}... | collective-permute-start | bytes 786440 | tf_op jit(solution)/shard_map/ppermute | solution.py:33
  112.6 10.4 %copy-start.15 = (bf16[2,1280,1,256]{1,3,0,2:T(8,128)(2,1)}, bf16[2,1280,1,256]{1,3,0,2:T(8,128)(2,1)S(1)}, u32[]{:S(2)}) copy-start(bf16[2,1280,1,256]{1,3,0,2:T(8,128)(2,1)S(1)} %constant_dynamic-update-slice_fusion.5) | copy-start | bytes 3932164
  132.9 51.5 %all-to-all-start.1 = ((bf16[8,32,2,3840]{3,1,2,0:T(8,128)(2,1)}), bf16[8,32,2,3840]{3,1,2,0:T(8,128)(2,1)}, u32[]{:S(2)}, u32[]{:S(2)}) async-start(bf16[8,32,2,3840]{3,1,2,0:T(8,128)(2,1)} %copy.69), calls=%async_computation.1 | async-start | bytes 7864320 | tf_op jit(solution)/shard_map/all_to_all | solution.py:44
  191.0 30.1 %all-to-all-start.2 = ((bf16[8,1,32,3840]{3,2,1,0:T(8,128)(2,1)}), bf16[8,1,32,3840]{3,2,1,0:T(8,128)(2,1)}, u32[]{:S(2)}, u32[]{:S(2)}) async-start(bf16[8,1,32,3840]{3,2,1,0:T(8,128)(2,1)} %broadcast_in_dim.24), calls=%async_computation.2 | async-start | bytes 3932160 | tf_op jit(solution)/shard_map/all_to_all | solution.py:16
  221.1 11.0 %slice-start = ((s8[5242880]{0:T(1024)(128)(4,1)}), s8[1048576]{0:T(1024)(128)(4,1)S(1)}, s32[]{:S(2)}) async-start(s8[5242880]{0:T(1024)(128)(4,1)} %bitcast.223), calls=%async_computation.4 | async-start | bytes 2097152
  232.1 12.4 %slice-start.6 = ((s8[7864320]{0:T(1024)(128)(4,1)}), s8[4194304]{0:T(1024)(128)(4,1)S(1)}, s32[]{:S(2)}) async-start(s8[7864320]{0:T(1024)(128)(4,1)} %bitcast.237), calls=%async_computation.10 | async-start | bytes 8388608
  235.4 25.1 %collective-permute-start.13 = (bf16[1,256,1,256]{1,3,2,0:T(8,128)(2,1)S(1)}, bf16[1,256,1,256]{1,3,2,0:T(8,128)(2,1)S(1)}, u32[]{:S(2)}, u32[]{:S(2)}) collective-permute-start(bf16[1,256,1,256]{1,3,2,0:T(8,128)(2,1)S(1)} %get-tuple-element.21), channel_id=1, source_target_pairs={{8,0},{16,8},{24,16},{32,24},{40,32},{48,40},{56,48},{9,1},{17,9},... | collective-permute-start | bytes 393224 | tf_op jit(solution)/shard_map/ppermute | solution.py:33
  237.6 8.3 %collective-permute-start.9 = (bf16[1,256,1,256]{1,3,2,0:T(8,128)(2,1)S(1)}, bf16[1,256,1,256]{1,3,2,0:T(8,128)(2,1)S(1)}, u32[]{:S(2)}, u32[]{:S(2)}) collective-permute-start(bf16[1,256,1,256]{1,3,2,0:T(8,128)(2,1)S(1)} %get-tuple-element.25), channel_id=1, source_target_pairs={{8,0},{16,8},{24,16},{32,24},{40,32},{48,40},{56,48},{9,1},{17,9},... | collective-permute-start | bytes 393224 | tf_op jit(solution)/shard_map/ppermute | solution.py:33
  239.5 8.5 %collective-permute-start.12 = (bf16[1,256,1,256]{1,3,2,0:T(8,128)(2,1)S(1)}, bf16[1,256,1,256]{1,3,2,0:T(8,128)(2,1)S(1)}, u32[]{:S(2)}, u32[]{:S(2)}) collective-permute-start(bf16[1,256,1,256]{1,3,2,0:T(8,128)(2,1)S(1)} %get-tuple-element.26), channel_id=1, source_target_pairs={{32,0},{40,8},{48,16},{56,24},{33,1},{41,9},{49,17},{57,25},{34,2}... | collective-permute-start | bytes 393224 | tf_op jit(solution)/shard_map/ppermute | solution.py:33
  240.8 14.1 %collective-permute-start.11 = (bf16[1,256,1,256]{1,3,2,0:T(8,128)(2,1)S(1)}, bf16[1,256,1,256]{1,3,2,0:T(8,128)(2,1)S(1)}, u32[]{:S(2)}, u32[]{:S(2)}) collective-permute-start(bf16[1,256,1,256]{1,3,2,0:T(8,128)(2,1)S(1)} %get-tuple-element.27), channel_id=1, source_target_pairs={{24,0},{32,8},{40,16},{48,24},{56,32},{25,1},{33,9},{41,17},{49,25... | collective-permute-start | bytes 393224 | tf_op jit(solution)/shard_map/ppermute | solution.py:33
  242.3 16.5 %collective-permute-start.10 = (bf16[1,256,1,256]{1,3,2,0:T(8,128)(2,1)S(1)}, bf16[1,256,1,256]{1,3,2,0:T(8,128)(2,1)S(1)}, u32[]{:S(2)}, u32[]{:S(2)}) collective-permute-start(bf16[1,256,1,256]{1,3,2,0:T(8,128)(2,1)S(1)} %get-tuple-element.28), channel_id=1, source_target_pairs={{16,0},{24,8},{32,16},{40,24},{48,32},{56,40},{17,1},{25,9},{33,17... | collective-permute-start | bytes 393224 | tf_op jit(solution)/shard_map/ppermute | solution.py:33
  244.6 15.1 %copy-start.1 = (bf16[1,2,3840,256]{3,2,1,0:T(8,128)(2,1)S(1)}, bf16[1,2,3840,256]{3,2,1,0:T(8,128)(2,1)}, u32[]{:S(2)}) copy-start(bf16[1,2,3840,256]{3,2,1,0:T(8,128)(2,1)} %param.15) | copy-start | bytes 11796484
  245.9 14.6 %collective-permute-start.16 = (bf16[1,256,1,256]{1,3,2,0:T(8,128)(2,1)S(1)}, bf16[1,256,1,256]{1,3,2,0:T(8,128)(2,1)S(1)}, u32[]{:S(2)}, u32[]{:S(2)}) collective-permute-start(bf16[1,256,1,256]{1,3,2,0:T(8,128)(2,1)S(1)} %get-tuple-element.22), channel_id=1, source_target_pairs={{32,0},{40,8},{48,16},{56,24},{33,1},{41,9},{49,17},{57,25},{34,2}... | collective-permute-start | bytes 393224 | tf_op jit(solution)/shard_map/ppermute | solution.py:33
  248.0 13.9 %collective-permute-start.15 = (bf16[1,256,1,256]{1,3,2,0:T(8,128)(2,1)S(1)}, bf16[1,256,1,256]{1,3,2,0:T(8,128)(2,1)S(1)}, u32[]{:S(2)}, u32[]{:S(2)}) collective-permute-start(bf16[1,256,1,256]{1,3,2,0:T(8,128)(2,1)S(1)} %get-tuple-element.23), channel_id=1, source_target_pairs={{24,0},{32,8},{40,16},{48,24},{56,32},{25,1},{33,9},{41,17},{49,25... | collective-permute-start | bytes 393224 | tf_op jit(solution)/shard_map/ppermute | solution.py:33
  254.9 11.5 %collective-permute-start.14 = (bf16[1,256,1,256]{1,3,2,0:T(8,128)(2,1)S(1)}, bf16[1,256,1,256]{1,3,2,0:T(8,128)(2,1)S(1)}, u32[]{:S(2)}, u32[]{:S(2)}) collective-permute-start(bf16[1,256,1,256]{1,3,2,0:T(8,128)(2,1)S(1)} %get-tuple-element.24), channel_id=1, source_target_pairs={{16,0},{24,8},{32,16},{40,24},{48,32},{56,40},{17,1},{25,9},{33,17... | collective-permute-start | bytes 393224 | tf_op jit(solution)/shard_map/ppermute | solution.py:33
  268.5 30.2 %all-to-all-start.3 = ((bf16[8,32,3840]{2,1,0:T(8,128)(2,1)}), bf16[8,32,3840]{2,1,0:T(8,128)(2,1)}, u32[]{:S(2)}, u32[]{:S(2)}) async-start(bf16[8,32,3840]{2,1,0:T(8,128)(2,1)} %bitcast.230), calls=%async_computation.3 | async-start | bytes 3932160 | tf_op jit(solution)/shard_map/all_to_all | solution.py:44
  273.0 27.6 %copy-start.10 = (bf16[1,4,32,3840]{3,2,1,0:T(8,128)(2,1)S(1)}, bf16[1,4,32,3840]{3,2,1,0:T(8,128)(2,1)}, u32[]{:S(2)}) copy-start(bf16[1,4,32,3840]{3,2,1,0:T(8,128)(2,1)} %param.11) | copy-start | bytes 2949124
  273.2 30.3 %collective-permute-start.8 = (bf16[1,32,3840]{2,1,0:T(8,128)(2,1)S(1)}, bf16[1,32,3840]{2,1,0:T(8,128)(2,1)S(1)}, u32[]{:S(2)}, u32[]{:S(2)}) collective-permute-start(bf16[1,32,3840]{2,1,0:T(8,128)(2,1)S(1)} %fusion.69), channel_id=1, source_target_pairs={{0,64},{64,0},{1,65},{65,1},{2,66},{66,2},{3,67},{67,3},{4,68},{68... | collective-permute-start | bytes 737288 | tf_op jit(solution)/shard_map/ppermute | solution.py:51
  302.0 7.5 %collective-permute-start.17 = (bf16[1,32,3840]{2,1,0:T(8,128)(2,1)S(1)}, bf16[1,32,3840]{2,1,0:T(8,128)(2,1)S(1)}, u32[]{:S(2)}, u32[]{:S(2)}) collective-permute-start(bf16[1,32,3840]{2,1,0:T(8,128)(2,1)S(1)} %fusion.58), channel_id=1, source_target_pairs={{0,64},{64,0},{1,65},{65,1},{2,66},{66,2},{3,67},{67,3},{4,68},{68... | collective-permute-start | bytes 737288 | tf_op jit(solution)/shard_map/ppermute | solution.py:51
  (19 other events, 84.1 us)
where the time goes:
time: 313 us; the launch traced here: 311 us
  waiting for transfers between devices  170 us (54%)
  starting transfers between devices  61.8 us (20%)
  local copies, waits for them, and re-layouts  27.4 us (9%)
  matrix products  25.7 us (8%)
  other arithmetic  20.1 us (6%)
  between operations  5.39 us (2%)
    all_to_all x2, waiting for transfers between devices, summed_on_arrival(): tiles = lax.all_to_all(cut_along(value, dim, size), axis, 0, 0, tiled=True)  70.8 us
    all_to_all x2, waiting for transfers between devices, sent_to_all(): return lax.all_to_all(copies, axis, split_axis=0, concat_axis=0, tiled=True)  68.5 us
    ppermute x16, starting transfers between devices, passed_along(): return lax.ppermute(value, axis, pairs)  40.9 us
    ppermute x16, waiting for transfers between devices, passed_along(): return lax.ppermute(value, axis, pairs)  25.1 us
    unnamed x69, local copies, waits for them, and re-layouts  10.3 us
    all_to_all x2, starting transfers between devices, summed_on_arrival(): tiles = lax.all_to_all(cut_along(value, dim, size), axis, 0, 0, tiled=True)  9.12 us
    all_to_all x2, starting transfers between devices, sent_to_all(): return lax.all_to_all(copies, axis, split_axis=0, concat_axis=0, tiled=True)  8.88 us
    dot_general x3, matrix products, forward_front(): jnp.einsum('lrd,ldc->lrc', piece, matrix, preferred_element_type=jnp.floa...  6.78 us
  transfers between devices with their start and end apart: 22, of which 12 were waited for; matrix products, arithmetic and copies ran while one was open for 8% of the time, Pallas kernels for 0%

commit v1 on v0

v1 whole, which is shorter than its diff:
```python
import jax
import jax.numpy as jnp
from jax import lax
from jax.experimental import pallas as pl
from jax.experimental.pallas import tpu as pltpu
from jax.sharding import PartitionSpec as P

WINDOW = 1024
epsilon = 1e-06
rope_base = 10000.0
masked_score = -1e30

D = 3840
ROWS = 32
TOK = 256
HD = 256
NCH = 3
CW = D // NCH
BACK, FWD, GRAD = 0, 1, 2
f32 = jnp.float32
bf16 = jnp.bfloat16
MESH = pl.DeviceIdType.MESH


def dot(a, b):
    return lax.dot_general(a, b, (((1,), (0,)), ((), ())), preferred_element_type=f32)


def dot_nt(a, b):
    return lax.dot_general(a, b, (((1,), (1,)), ((), ())), preferred_element_type=f32)


def dot_tn(a, b):
    return lax.dot_general(a, b, (((0,), (0,)), ((), ())), preferred_element_type=f32)


def rms_of(x):
    return lax.rsqrt(jnp.mean(x * x, axis=-1, keepdims=True) + epsilon)


def rms_back(x, grad, gain):
    g = grad * gain
    r = rms_of(x)
    return r * (g - x * (r * r * jnp.mean(g * x, axis=-1, keepdims=True)))


def rope(y, cosine, sine):
    a, b = y[:, : HD // 2], y[:, HD // 2 :]
    return jnp.concatenate([a * cosine - b * sine, b * cosine + a * sine], axis=-1)


def rope_back(g, cosine, sine):
    a, b = g[:, : HD // 2], g[:, HD // 2 :]
    return jnp.concatenate([a * cosine + b * sine, b * cosine - a * sine], axis=-1)


def kernel(
    plan, cos_ref, sin_ref, ig, og, qg, kg, si, sg, wq_h, wk_h, wv_h, wo_h,
    act_out, grad_out,
    wq, wk, wv, wo, sti, stg, ag, qs, qraw, kraw, kvs, kvrl, cx, pw, pl_s, dss, cgs,
    ps, pr, sb, rl, fr, own, gs, gr, gacc, lq, fo, go,
    lsem, ags, agr, rss, rsr, kss, ksr, gss, gsr, swap_s, swap_r,
):
    s = lax.axis_index("segment")
    p = lax.axis_index("ctx")
    t = lax.axis_index("tp")
    yh, z = p // 4, p % 4
    y = 2 * yh + s
    x, c = t // 2, t % 2
    legs = (1 - s, s)

    def dev(s_=None, p_=None, t_=None):
        return {
            "segment": s if s_ is None else s_,
            "ctx": p if p_ is None else p_,
            "tp": t if t_ is None else t_,
        }

    t_r, t_l = ((x + 1) % 4) * 2 + c, ((x + 3) % 4) * 2 + c
    t_o = ((x + 2) % 4) * 2 + c
    t_p = 2 * x + 1 - c
    right, left, partner = dev(t_=t_r), dev(t_=t_l), dev(t_=t_p)
    z_up, z_dn = dev(p_=4 * yh + (z + 1) % 4), dev(p_=4 * yh + (z + 3) % 4)
    y_u, y_d = (y + 1) % 4, (y + 3) % 4
    y_up = dev(s_=y_u % 2, p_=(y_u // 2) * 4 + z)
    y_dn = dev(s_=y_d % 2, p_=(y_d // 2) * 4 + z)
    other = dev(s_=1 - s)

    barrier = pltpu.get_barrier_semaphore()
    for device in (right, left, partner, z_up, z_dn, y_up, y_dn):
        pl.semaphore_signal(barrier, inc=1, device_id=device, device_id_type=MESH)

    loads = [
        pltpu.make_async_copy(si, sti, lsem.at[0]),
        pltpu.make_async_copy(sg, stg, lsem.at[1]),
    ]
    for j in range(2):
        loads += [
            pltpu.make_async_copy(wq_h.at[legs[j]], wq.at[j], lsem.at[2 + 4 * j]),
            pltpu.make_async_copy(wk_h.at[legs[j]], wk.at[j], lsem.at[3 + 4 * j]),
            pltpu.make_async_copy(wv_h.at[legs[j]], wv.at[j], lsem.at[4 + 4 * j]),
            pltpu.make_async_copy(wo_h.at[legs[j]], wo.at[j], lsem.at[5 + 4 * j]),
        ]
    for load in loads:
        load.start()

    def gain(ref, j):
        return ref[pl.ds(legs[j], 1), :]

    def rcopy(src, dst, ssem, rsem, device):
        return pltpu.make_async_remote_copy(
            src_ref=src, dst_ref=dst, send_sem=ssem, recv_sem=rsem,
            device_id=device, device_id_type=MESH,
        )

    drains = []

    def when(cond, run):
        if cond is None:
            run()
        else:
            pl.when(cond)(run)

    def send(copy, cond=None):
        when(cond, copy.start)
        drains.append((copy, cond))

    def arrive(dst, rsem, cond=None):
        copy = rcopy(dst, dst, swap_s.at[0], rsem, partner)
        when(cond, copy.wait_recv)

    H0, H1 = pl.ds(0, ROWS // 2), pl.ds(ROWS // 2, ROWS // 2)
    halves = (H0, H1)

    def gather_start(j):
        blk = ag.at[j, t]
        send(rcopy(blk.at[H0], blk.at[H0], ags.at[j, 0], agr.at[j, 0], right))
        send(rcopy(blk.at[H1], blk.at[H1], ags.at[j, 1], agr.at[j, 1], left))
        send(rcopy(blk.at[H1], blk.at[H1], ags.at[j, 2], agr.at[j, 2], right))
        send(rcopy(blk.at[H0], blk.at[H0], ags.at[j, 3], agr.at[j, 3], left))
        send(rcopy(blk, blk, ags.at[j, 6], agr.at[j, 6], partner))

    def across(j, place, half, i):
        part = ag.at[j, place, halves[half]]
        send(rcopy(part, part, ags.at[j, i], agr.at[j, i], partner))

    def gather_relay(j):
        a = ag.at[j, t_l, H0]
        arrive(a, agr.at[j, 0])
        send(rcopy(a, a, ags.at[j, 4], agr.at[j, 4], right))
        b = ag.at[j, t_r, H1]
        arrive(b, agr.at[j, 1])
        send(rcopy(b, b, ags.at[j, 5], agr.at[j, 5], left))
        across(j, t_l, 0, 7)
        across(j, t_r, 1, 8)

    def gather_finish(j):
        arrive(ag.at[j, t_l, H1], agr.at[j, 2])
        across(j, t_l, 1, 9)
        arrive(ag.at[j, t_r, H0], agr.at[j, 3])
        across(j, t_r, 0, 10)
        arrive(ag.at[j, t_o, H0], agr.at[j, 4])
        across(j, t_o, 0, 11)
        arrive(ag.at[j, t_o, H1], agr.at[j, 5])
        across(j, t_o, 1, 12)
        u_r, u_l, u_o = t_r + 1 - 2 * c, t_l + 1 - 2 * c, t_o + 1 - 2 * c
        arrive(ag.at[j, t_p], agr.at[j, 6])
        arrive(ag.at[j, u_l, H0], agr.at[j, 7])
        arrive(ag.at[j, u_r, H1], agr.at[j, 8])
        arrive(ag.at[j, u_l, H1], agr.at[j, 9])
        arrive(ag.at[j, u_r, H0], agr.at[j, 10])
        arrive(ag.at[j, u_o, H0], agr.at[j, 11])
        arrive(ag.at[j, u_o, H1], agr.at[j, 12])

    def cols(n):
        return pl.ds(n * CW, CW)

    def rows_of(ref, parity):
        parts = [ref[2 * ((x + k) % 4) + parity] for k in range(4)]
        return jnp.concatenate(parts, axis=0)

    def scatter_first(r, product, lhs_of):
        lhs = lhs_of(1 - c)
        for n in range(NCH):
            ps[r % 2, :, :, cols(n)] = product(lhs, n).astype(bf16).reshape(4, ROWS, CW)
            send(rcopy(ps.at[r % 2, :, :, cols(n)], pr.at[r, :, :, cols(n)],
                       rss.at[r, n, 0], rsr.at[r, n, 0], partner))

    def scatter_second(r, product, lhs_of):
        lhs = lhs_of(c)
        for n in range(NCH):
            arrive(pr.at[r, :, :, cols(n)], rsr.at[r, n, 0])
            total = product(lhs, n).reshape(4, ROWS, CW) + pr[r, :, :, cols(n)].astype(f32)
            own[r, :, cols(n)] = total[0]
            sb[r, :, :, cols(n)] = total[1:].astype(bf16)
            send(rcopy(sb.at[r, 1, H0, cols(n)], rl.at[r, 0, :, cols(n)],
                       rss.at[r, n, 1], rsr.at[r, n, 1], right))
            send(rcopy(sb.at[r, 1, H1, cols(n)], rl.at[r, 1, :, cols(n)],
                       rss.at[r, n, 2], rsr.at[r, n, 2], left))
            send(rcopy(sb.at[r, 0, H1, cols(n)], fr.at[r, 0, H1, cols(n)],
                       rss.at[r, n, 3], rsr.at[r, n, 3], right))
            send(rcopy(sb.at[r, 2, H0, cols(n)], fr.at[r, 1, H0, cols(n)],
                       rss.at[r, n, 4], rsr.at[r, n, 4], left))

    def scatter_relay(r):
        for n in range(NCH):
            arrive(rl.at[r, 0, :, cols(n)], rsr.at[r, n, 1])
            sb[r, 0, H0, cols(n)] = (
                sb[r, 0, H0, cols(n)].astype(f32) + rl[r, 0, :, cols(n)].astype(f32)
            ).astype(bf16)
            send(rcopy(sb.at[r, 0, H0, cols(n)], fr.at[r, 0, H0, cols(n)],
                       rss.at[r, n, 5], rsr.at[r, n, 5], right))
            arrive(rl.at[r, 1, :, cols(n)], rsr.at[r, n, 2])
            sb[r, 2, H1, cols(n)] = (
                sb[r, 2, H1, cols(n)].astype(f32) + rl[r, 1, :, cols(n)].astype(f32)
            ).astype(bf16)
            send(rcopy(sb.at[r, 2, H1, cols(n)], fr.at[r, 1, H1, cols(n)],
                       rss.at[r, n, 6], rsr.at[r, n, 6], left))

    def scatter_finish(r):
        for n in range(NCH):
            arrive(fr.at[r, 0, H1, cols(n)], rsr.at[r, n, 3])
            arrive(fr.at[r, 1, H0, cols(n)], rsr.at[r, n, 4])
            arrive(fr.at[r, 0, H0, cols(n)], rsr.at[r, n, 5])
            arrive(fr.at[r, 1, H1, cols(n)], rsr.at[r, n, 6])
        return own[r] + fr[r, 0].astype(f32) + fr[r, 1].astype(f32)

    hi, lo = yh == 1, yh == 0
    mid = (z == 1) | (z == 2)

    def kv_start(j):
        k, v = kvs.at[j, 0, 0], kvs.at[j, 1, 0]
        send(rcopy(k, kvrl.at[j], kss.at[j, 6, 0], ksr.at[j, 0, 0], y_up), lo)
        send(rcopy(v, kvrl.at[j], kss.at[j, 6, 1], ksr.at[j, 0, 0], y_dn), lo)
        for i in range(2):
            o = kvs.at[j, i, 0]
            send(rcopy(o, kvs.at[j, i, 1], kss.at[j, 1, i], ksr.at[j, 1, i], z_up), z < 3)
            send(rcopy(o, kvs.at[j, i, 3], kss.at[j, 3, i], ksr.at[j, 3, i], z_dn), z == 0)

    relay_k = (y == 1) | (y == 2)
    relay_v = (y == 0) | (y == 3)

    def kv_relay(j):
        arrive(kvrl.at[j], ksr.at[j, 0, 0])
        send(rcopy(kvrl.at[j], kvs.at[j, 0, 4], kss.at[j, 4, 0], ksr.at[j, 4, 0], y_up), relay_k)
        send(rcopy(kvrl.at[j], kvs.at[j, 1, 4], kss.at[j, 4, 1], ksr.at[j, 4, 1], y_dn), relay_v)

    def kv_second(j):
        for i in range(2):
            b1, b4 = kvs.at[j, i, 1], kvs.at[j, i, 4]
            arrive(b1, ksr.at[j, 1, i], mid)
            send(rcopy(b1, kvs.at[j, i, 2], kss.at[j, 2, i], ksr.at[j, 2, i], z_up), mid)
            arrive(b4, ksr.at[j, 4, i], hi)
            send(rcopy(b4, kvs.at[j, i, 3], kss.at[j, 3, i], ksr.at[j, 3, i], z_dn), hi & (z >= 1))
            send(rcopy(b4, kvs.at[j, i, 1], kss.at[j, 1, i], ksr.at[j, 1, i], z_up), hi & (z == 3))

    def kv_third(j):
        for i in range(2):
            b3 = kvs.at[j, i, 3]
            arrive(b3, ksr.at[j, 3, i], hi & mid)
            send(rcopy(b3, kvs.at[j, i, 2], kss.at[j, 5, i], ksr.at[j, 2, i], z_dn), hi & mid)

    def kv_finish(j):
        for i in range(2):
            arrive(kvs.at[j, i, 1], ksr.at[j, 1, i], (z == 3) | (hi & (z == 0)))
            arrive(kvs.at[j, i, 2], ksr.at[j, 2, i], (z >= 2) | hi)
            arrive(kvs.at[j, i, 3], ksr.at[j, 3, i], (z == 3) | (hi & (z == 0)))

    cosine, sine = cos_ref[...], sin_ref[...]

    def project(j):
        for load in loads[2 + 4 * j : 5 + 4 * j]:
            load.wait()
        xn = ag[j].reshape(TOK, D)
        q_gain, k_gain = gain(qg, j), gain(kg, j)
        kr = dot(xn, wk[j])
        kvs[j, 0, 0] = rope(kr * rms_of(kr) * k_gain, cosine, sine).astype(bf16)
        kvs[j, 1, 0] = dot(xn, wv[j]).astype(bf16)
        kv_start(j)
        if j == BACK:
            kraw[...] = kr
        for h in range(2):
            qr = dot(xn, wq[j, :, h * HD : (h + 1) * HD])
            qs[j, h * TOK : (h + 1) * TOK] = rope(
                qr * rms_of(qr) * q_gain, cosine, sine
            ).astype(bf16)
            if j == BACK:
                qraw[h * TOK : (h + 1) * TOK] = qr

    def attention(j, keep):
        @pl.loop(0, 4)
        def _(ci):
            rows = pl.ds(pl.multiple_of(ci * 128, 128), 128)
            sc = dot_nt(qs[j, rows, :], kvs[j, 0].reshape(5 * TOK, HD)) * (HD ** -0.5)
            col = lax.broadcasted_iota(jnp.int32, (1, 5 * TOK), 1)
            back = (col // TOK) * TOK - col % TOK
            back = jnp.where(col // TOK <= p, back, -4 * WINDOW)
            ii = (ci % 2) * 128 + lax.broadcasted_iota(jnp.int32, (128, 1), 0)
            rel = ii + back
            sc = jnp.where((rel >= 0) & (rel < WINDOW), sc, masked_score)
            e = jnp.exp(sc - jnp.max(sc, axis=-1, keepdims=True))
            w = e / jnp.sum(e, axis=-1, keepdims=True)
            low = w.astype(bf16)
            if keep:
                pw[rows, :] = w
                pl_s[rows, :] = low
            out = dot(low, kvs[j, 1].reshape(5 * TOK, HD)).astype(bf16)
            for h in range(2):
                @pl.when(ci // 2 == h)
                def _():
                    cx[j, pl.ds(4 * (ci % 2), 4), :, h * HD : (h + 1) * HD] = out.reshape(
                        4, ROWS, HD
                    )

    def out_product(j):
        return lambda lhs, n: dot(lhs, wo[j, :, n * CW : (n + 1) * CW])

    def hidden_product(lhs, n):
        w_rows = slice(n * CW, (n + 1) * CW)
        total = dot_nt(lhs[:, : 2 * HD], wq[BACK, w_rows, :])
        total += dot_nt(lhs[:, 2 * HD : 3 * HD], wk[BACK, w_rows, :])
        return total + dot_nt(lhs[:, 3 * HD :], wv[BACK, w_rows, :])

    loads[0].wait()
    x_back = sti[plan[0, 1]].astype(f32)
    ag[BACK, t] = (x_back * rms_of(x_back) * gain(ig, BACK)).astype(bf16)
    for j in range(2):
        for d in range(1, 5):
            @pl.when(d > p)
            def _():
                for i in range(2):
                    kvs[j, i, d] = jnp.zeros((TOK, HD), bf16)
    pl.semaphore_wait(barrier, 7)
    gather_start(BACK)
    x_fwd = sti[plan[0, 0]].astype(f32)
    ag[FWD, t] = (x_fwd * rms_of(x_fwd) * gain(ig, FWD)).astype(bf16)
    gather_relay(BACK)
    gather_start(FWD)
    gather_finish(BACK)
    project(BACK)
    gather_relay(FWD)
    kv_relay(BACK)
    gather_finish(FWD)
    kv_second(BACK)
    project(FWD)
    kv_third(BACK)
    kv_relay(FWD)
    kv_finish(BACK)
    attention(BACK, True)
    loads[5].wait()
    before = len(drains)
    scatter_first(BACK, out_product(BACK), lambda par: rows_of(cx.at[BACK], par))
    kv_second(FWD)
    scatter_second(BACK, out_product(BACK), lambda par: rows_of(cx.at[BACK], par))
    scatter_relay(BACK)
    kv_third(FWD)
    projected = scatter_finish(BACK)
    loads[1].wait()
    incoming = stg[plan[0, 1]].astype(f32)
    ag[GRAD, t] = rms_back(projected, incoming, gain(og, BACK)).astype(bf16)
    gather_start(GRAD)
    kv_finish(FWD)
    attention(FWD, False)
    gather_relay(GRAD)
    loads[9].wait()
    scatter_first(FWD, out_product(FWD), lambda par: rows_of(cx.at[FWD], par))
    gather_finish(GRAD)
    scatter_second(FWD, out_product(FWD), lambda par: rows_of(cx.at[FWD], par))

    og_rows = ag[GRAD].reshape(TOK, D)
    for h in range(2):
        cgs[h * TOK : (h + 1) * TOK] = dot_nt(
            og_rows, wo[BACK, h * HD : (h + 1) * HD, :]
        ).astype(bf16)
    q_gain, k_gain = gain(qg, BACK), gain(kg, BACK)

    @pl.loop(0, 4)
    def _(ci):
        rows = pl.ds(pl.multiple_of(ci * 128, 128), 128)
        w = pw[rows, :]
        wg = dot_nt(cgs[rows, :], kvs[BACK, 1].reshape(5 * TOK, HD))
        delta = jnp.sum(w * wg, axis=-1, keepdims=True)
        dss[rows, :] = (w * (wg - delta) * (HD ** -0.5)).astype(bf16)

    scatter_relay(FWD)

    def grad_block(d):
        ds_d = dss[:, d * TOK : (d + 1) * TOK]
        gacc[0, d] = dot_tn(ds_d, qs[BACK])
        gacc[1, d] = dot_tn(pl_s[:, d * TOK : (d + 1) * TOK], cgs[...])

    R1, R2, R3, R4, R5, RR = 0, 1, 2, 3, 4, 5

    def give(d):
        for i in range(2):
            gs[i, d - 1] = gacc[i, d].astype(bf16)

    def g_send(d, e, se, device, cond, i):
        send(rcopy(gs.at[i, d - 1], gr.at[e, i], gss.at[se, i], gsr.at[e, i], device), cond)

    def g_add(e, d, cond):
        for i in range(2):
            arrive(gr.at[e, i], gsr.at[e, i], cond)

            @pl.when(cond)
            def _():
                gacc[i, d] = gacc[i, d] + gr[e, i].astype(f32)

    grad_block(2)
    give(2)
    for i in range(2):
        g_send(2, R2, 0, z_dn, z >= 2, i)
        g_send(2, R5, 1, z_up, hi & (z <= 1), i)
    grad_block(3)
    grad_block(1)
    g_add(R5, 3, hi & mid)
    give(3)
    for i in range(2):
        g_send(3, R3, 2, z_up, (z == 3) | hi, i)
    g_add(R2, 1, mid)
    give(1)
    for i in range(2):
        g_send(1, R1, 3, z_dn, (z >= 1) | hi, i)
    grad_block(4)
    grad_block(0)
    g_add(R3, 4, hi & (z >= 1))
    g_add(R1, 4, hi & (z == 3))
    give(4)
    send(rcopy(gs.at[0, 3], gr.at[RR, 0], gss.at[4, 0], gsr.at[RR, 0], y_dn), hi)
    send(rcopy(gs.at[1, 3], gr.at[RR, 0], gss.at[4, 1], gsr.at[RR, 0], y_up), hi)

    for h in range(2):
        rows = slice(h * TOK, (h + 1) * TOK)
        dq = dot(dss[rows, :], kvs[BACK, 0].reshape(5 * TOK, HD))
        low = rms_back(qraw[rows], rope_back(dq, cosine, sine), q_gain).astype(bf16)
        lq[:, :, h * HD : (h + 1) * HD] = low.reshape(8, ROWS, HD)

    arrive(gr.at[RR, 0], gsr.at[RR, 0])
    send(rcopy(gr.at[RR, 0], gr.at[R4, 0], gss.at[5, 0], gsr.at[R4, 0], y_dn), relay_k)
    send(rcopy(gr.at[RR, 0], gr.at[R4, 1], gss.at[5, 1], gsr.at[R4, 1], y_up), relay_v)

    fwd_proj = scatter_finish(FWD)
    x_fwd = sti[plan[0, 0]].astype(f32)
    fo[...] = (x_fwd + fwd_proj * rms_of(fwd_proj) * gain(og, FWD)).astype(bf16)
    send(rcopy(fo, act_out, swap_s.at[1], swap_r.at[1], other))

    g_add(R1, 0, z < 3)
    g_add(R3, 0, z == 0)
    g_add(R4, 0, lo)
    key_low = rms_back(kraw[...], rope_back(gacc[0, 0], cosine, sine), k_gain).astype(bf16)
    lq[:, :, 2 * HD : 3 * HD] = key_low.reshape(8, ROWS, HD)
    lq[:, :, 3 * HD :] = gacc[1, 0].astype(bf16).reshape(8, ROWS, HD)

    for copy, _ in drains[before : before + NCH]:
        copy.wait_send()
    del drains[before : before + NCH]
    scatter_first(2, hidden_product, lambda par: rows_of(lq, par))
    scatter_second(2, hidden_product, lambda par: rows_of(lq, par))
    scatter_relay(2)
    hidden = scatter_finish(2)
    x_back = sti[plan[0, 1]].astype(f32)
    incoming = stg[plan[0, 1]].astype(f32)
    go[...] = (incoming + rms_back(x_back, hidden, gain(ig, BACK))).astype(bf16)
    send(rcopy(go, grad_out, swap_s.at[2], swap_r.at[2], other))
    arrive(act_out, swap_r.at[1])
    arrive(grad_out, swap_r.at[2])
    for copy, cond in drains:
        when(cond, copy.wait_send)


def per_device(
    stash_inputs, stash_grads, plan, query_weight, key_weight, value_weight, out_weight,
    input_gain, output_gain, query_gain, key_gain,
):
    block = lax.axis_index("ctx")
    positions = (block * TOK + jnp.arange(TOK, dtype=jnp.int32)).astype(f32)
    frequency = rope_base ** (-(jnp.arange(HD // 2).astype(f32) * 2.0 / HD))
    angles = positions[:, None] * frequency[None, :]
    vmem = pl.BlockSpec(memory_space=pltpu.VMEM)
    hbm = pl.BlockSpec(memory_space=pl.ANY)
    smem = pl.BlockSpec(memory_space=pltpu.SMEM)
    V = pltpu.VMEM
    sem = pltpu.SemaphoreType.DMA
    act, grad = pl.pallas_call(
        kernel,
        out_shape=(jax.ShapeDtypeStruct((ROWS, D), bf16),) * 2,
        in_specs=[smem] + [vmem] * 6 + [hbm] * 6,
        out_specs=(hbm, hbm),
        scratch_shapes=[
            V((2, D, 2 * HD), bf16), V((2, D, HD), bf16), V((2, D, HD), bf16), V((2, 2 * HD, D), bf16),
            V((4, ROWS, D), bf16), V((4, ROWS, D), bf16),
            V((3, 8, ROWS, D), bf16),
            V((2, 2 * TOK, HD), bf16), V((2 * TOK, HD), f32), V((TOK, HD), f32),
            V((2, 2, 5, TOK, HD), bf16), V((2, TOK, HD), bf16),
            V((2, 8, ROWS, 2 * HD), bf16),
            V((2 * TOK, 5 * TOK), f32), V((2 * TOK, 5 * TOK), bf16), V((2 * TOK, 5 * TOK), bf16),
            V((2 * TOK, HD), bf16),
            V((2, 4, ROWS, D), bf16), V((3, 4, ROWS, D), bf16), V((3, 3, ROWS, D), bf16),
            V((3, 2, ROWS // 2, D), bf16), V((3, 2, ROWS, D), bf16), V((3, ROWS, D), f32),
            V((2, 4, TOK, HD), bf16), V((6, 2, TOK, HD), bf16), V((2, 5, TOK, HD), f32),
            V((8, ROWS, 4 * HD), bf16),
            V((ROWS, D), bf16), V((ROWS, D), bf16),
            sem((10,)), sem((3, 13)), sem((3, 13)), sem((3, NCH, 7)), sem((3, NCH, 7)),
            sem((2, 7, 2)), sem((2, 5, 2)), sem((6, 2)), sem((6, 2)), sem((3,)), sem((3,)),
        ],
        compiler_params=pltpu.CompilerParams(
            collective_id=0, has_side_effects=True, vmem_limit_bytes=67043328
        ),
    )(
        plan, jnp.cos(angles), jnp.sin(angles), input_gain[0], output_gain[0], query_gain[0],
        key_gain[0], stash_inputs[0], stash_grads[0], query_weight[0], key_weight[0],
        value_weight[0], out_weight[0],
    )
    return act[None], grad[None]


def solution(mesh):
    return jax.shard_map(
        per_device,
        mesh=mesh,
        in_specs=(
            P("segment", None, ("ctx", "tp"), None),
            P("segment", None, ("ctx", "tp"), None),
            P("segment", None),
            P("segment", None, None, "tp"),
            P("segment", None, None, "tp"),
            P("segment", None, None, "tp"),
            P("segment", None, "tp", None),
            P("segment", None, None),
            P("segment", None, None),
            P("segment", None, None),
            P("segment", None, None),
        ),
        out_specs=(P("segment", ("ctx", "tp"), None), P("segment", ("ctx", "tp"), None)),
        check_vma=False,
    )
```

time: 313 us -> 134 us (0.43)
  waiting for transfers between devices: 170 us -> 0 us
  Pallas kernels: 0 us -> 129 us
  starting transfers between devices: 61.8 us -> 0 us
  matrix products: 25.7 us -> 0 us
  local copies, waits for them, and re-layouts: 27.4 us -> 3.31 us
  other arithmetic: 20.1 us -> 1.25 us
  between operations: 5.39 us -> 0.66 us
    all_to_all x4 -> x0, waiting for transfers between devices: 139 us -> none  [the longest x2 70.8 us: summed_on_arrival(): tiles = lax.all_to_all(cut_along(value, dim, size), axis, 0, 0, tiled=True)]
    pallas_call x0 -> x1, Pallas kernels: none -> 129 us  [per_device(): pl.pallas_call(kernel, out_shape=(jax.ShapeDtypeStruct((ROWS, D), bf16),)...]
    ppermute x18 -> x0, starting transfers between devices: 43.8 us -> none  [the longest x16 40.9 us: passed_along(): return lax.ppermute(value, axis, pairs)]
    ppermute x18 -> x0, waiting for transfers between devices: 31.1 us -> none  [the longest x16 25.1 us: passed_along(): return lax.ppermute(value, axis, pairs)]
    dot_general x14 -> x0, matrix products: 25.7 us -> none  [the longest x3 6.78 us: forward_front(): jnp.einsum('lrd,ldc->lrc', piece, matrix, preferred_element_type=jnp.floa...]
    all_to_all x4 -> x0, starting transfers between devices: 18 us -> none  [the longest x2 9.12 us: summed_on_arrival(): tiles = lax.all_to_all(cut_along(value, dim, size), axis, 0, 0, tiled=True)]
    reduce_sum x10 -> x0, other arithmetic: 7.97 us -> none  [the longest x2 4.62 us: summed_on_arrival(): return jnp.sum(tiles.astype(jnp.float32), axis=0)]
    unnamed x69 -> x2, local copies, waits for them, and re-layouts: 10.3 us -> 3.31 us
  transfers between devices with their start and end apart: 22 -> 0, of which waited for: 12 -> 0; matrix products, arithmetic and copies ran while one was open for 8% -> 0% of each run, Pallas kernels for 0% -> 0%
where the time goes in v1:
time: 134 us
  Pallas kernels  129 us (96%)
  local copies, waits for them, and re-layouts  3.31 us (2%)
    pallas_call x1, Pallas kernels, per_device(): pl.pallas_call(kernel, out_shape=(jax.ShapeDtypeStruct((ROWS, D), bf16),)...  129 us
    unnamed x2, local copies, waits for them, and re-layouts  3.31 us

profile of v1, /device:TPU:72, one launch (start us, length us, event | category | flops | bytes accessed | tf_op | source)
XLA Modules:
  0.0 133.8 jit_solution(7685328528818438432)
XLA Ops:
  0.7 1.2 multiply_sine_fusion
  1.9 128.6 %shard_map.122 = (bf16[32,3840]{1,0:T(8,128)(2,1)}, bf16[32,3840]{1,0:T(8,128)(2,1)}) custom-call(s32[1,4]{1,0:T(1,128)} %plan.1, f32[256,128]{1,0:T(8,128)} %get-tuple-element.7.cos_ref, f32[256,128]{1,0:T(8,128)} %get-tuple-element.6.sin_ref, f32[2,3840]{1,0:T(2,128)} %bitcast.20, f32[2,3840]{1,0:T(2,128)} %bitcast.21, f32[2,256]{1,0:T(2,128)} %bitcast.22, ...), custom_call_target="tpu_custom_call" | custom-call | tf_op jit(solution)/shard_map/pallas_call | solution.py:484
  130.5 1.7 %copy.15 = bf16[1,32,3840]{2,1,0:T(8,128)(2,1)} copy(bf16[1,32,3840]{2,1,0:T(8,128)(2,1)} %bitcast.19) | data formatting | bytes 491520
  132.2 1.7 %copy.16 = bf16[1,32,3840]{2,1,0:T(8,128)(2,1)} copy(bf16[1,32,3840]{2,1,0:T(8,128)(2,1)} %bitcast.18) | data formatting | bytes 491520
  (2 shorter events, 0.0 us)

commit v2 on v1

--- a/solution.py
+++ b/solution.py
@@ -55,10 +55,10 @@
 
 
 def kernel(
-    plan, cos_ref, sin_ref, ig, og, qg, kg, si, sg, wq_h, wk_h, wv_h, wo_h,
+    plan, freq, ig, og, qg, kg, si, sg, wq_h, wk_h, wv_h, wo_h,
     act_out, grad_out,
     wq, wk, wv, wo, sti, stg, ag, qs, qraw, kraw, kvs, kvrl, cx, pw, pl_s, dss, cgs,
-    ps, pr, sb, rl, fr, own, gs, gr, gacc, lq, fo, go,
+    ps, pr, sb, rl, fr, own, gs, gr, gacc, lq, fo, go, cos_ref, sin_ref, hq, bo, gb,
     lsem, ags, agr, rss, rsr, kss, ksr, gss, gsr, swap_s, swap_r,
 ):
     s = lax.axis_index("segment")
@@ -179,19 +179,22 @@
         parts = [ref[2 * ((x + k) % 4) + parity] for k in range(4)]
         return jnp.concatenate(parts, axis=0)
 
-    def scatter_first(r, product, lhs_of):
-        lhs = lhs_of(1 - c)
+    def rows_all(ref):
+        return jnp.concatenate([rows_of(ref, 1 - c), rows_of(ref, c)], axis=0)
+
+    def scatter_first(r, product, lhs):
         for n in range(NCH):
-            ps[r % 2, :, :, cols(n)] = product(lhs, n).astype(bf16).reshape(4, ROWS, CW)
+            total = product(lhs, n)
+            ps[r % 2, :, :, cols(n)] = total[: 4 * ROWS].astype(bf16).reshape(4, ROWS, CW)
             send(rcopy(ps.at[r % 2, :, :, cols(n)], pr.at[r, :, :, cols(n)],
                        rss.at[r, n, 0], rsr.at[r, n, 0], partner))
-
-    def scatter_second(r, product, lhs_of):
-        lhs = lhs_of(c)
+            hq[4 * ROWS :, cols(n)] = total[4 * ROWS :]
+
+    def scatter_second(r):
         for n in range(NCH):
             arrive(pr.at[r, :, :, cols(n)], rsr.at[r, n, 0])
-            total = product(lhs, n).reshape(4, ROWS, CW) + pr[r, :, :, cols(n)].astype(f32)
-            own[r, :, cols(n)] = total[0]
+            total = hq[4 * ROWS :, cols(n)].reshape(4, ROWS, CW) + pr[r, :, :, cols(n)].astype(f32)
+            own[r % 2, :, cols(n)] = total[0]
             sb[r, :, :, cols(n)] = total[1:].astype(bf16)
             send(rcopy(sb.at[r, 1, H0, cols(n)], rl.at[r, 0, :, cols(n)],
                        rss.at[r, n, 1], rsr.at[r, n, 1], right))
@@ -217,13 +220,17 @@
             send(rcopy(sb.at[r, 2, H1, cols(n)], fr.at[r, 1, H1, cols(n)],
                        rss.at[r, n, 6], rsr.at[r, n, 6], left))
 
+    def scatter_part(r, n):
+        arrive(fr.at[r, 0, H1, cols(n)], rsr.at[r, n, 3])
+        arrive(fr.at[r, 1, H0, cols(n)], rsr.at[r, n, 4])
+        arrive(fr.at[r, 0, H0, cols(n)], rsr.at[r, n, 5])
+        arrive(fr.at[r, 1, H1, cols(n)], rsr.at[r, n, 6])
+        return own[r % 2, :, cols(n)] + (
+            fr[r, 0, :, cols(n)].astype(f32) + fr[r, 1, :, cols(n)].astype(f32)
+        )
+
     def scatter_finish(r):
-        for n in range(NCH):
-            arrive(fr.at[r, 0, H1, cols(n)], rsr.at[r, n, 3])
-            arrive(fr.at[r, 1, H0, cols(n)], rsr.at[r, n, 4])
-            arrive(fr.at[r, 0, H0, cols(n)], rsr.at[r, n, 5])
-            arrive(fr.at[r, 1, H1, cols(n)], rsr.at[r, n, 6])
-        return own[r] + fr[r, 0].astype(f32) + fr[r, 1].astype(f32)
+        return jnp.concatenate([scatter_part(r, n) for n in range(NCH)], axis=-1)
 
     hi, lo = yh == 1, yh == 0
     mid = (z == 1) | (z == 2)
@@ -266,9 +273,8 @@
             arrive(kvs.at[j, i, 2], ksr.at[j, 2, i], (z >= 2) | hi)
             arrive(kvs.at[j, i, 3], ksr.at[j, 3, i], (z == 3) | (hi & (z == 0)))
 
-    cosine, sine = cos_ref[...], sin_ref[...]
-
     def project(j):
+        cosine, sine = cos_ref[...], sin_ref[...]
         for load in loads[2 + 4 * j : 5 + 4 * j]:
             load.wait()
         xn = ag[j].reshape(TOK, D)
@@ -317,23 +323,25 @@
 
     def hidden_product(lhs, n):
         w_rows = slice(n * CW, (n + 1) * CW)
-        total = dot_nt(lhs[:, : 2 * HD], wq[BACK, w_rows, :])
-        total += dot_nt(lhs[:, 2 * HD : 3 * HD], wk[BACK, w_rows, :])
+        total = hq[:, cols(n)] + dot_nt(lhs[:, 2 * HD : 3 * HD], wk[BACK, w_rows, :])
         return total + dot_nt(lhs[:, 3 * HD :], wv[BACK, w_rows, :])
 
     loads[0].wait()
     x_back = sti[plan[0, 1]].astype(f32)
     ag[BACK, t] = (x_back * rms_of(x_back) * gain(ig, BACK)).astype(bf16)
+    pl.semaphore_wait(barrier, 7)
+    gather_start(BACK)
+    x_fwd = sti[plan[0, 0]].astype(f32)
+    ag[FWD, t] = (x_fwd * rms_of(x_fwd) * gain(ig, FWD)).astype(bf16)
     for j in range(2):
         for d in range(1, 5):
             @pl.when(d > p)
             def _():
                 for i in range(2):
                     kvs[j, i, d] = jnp.zeros((TOK, HD), bf16)
-    pl.semaphore_wait(barrier, 7)
-    gather_start(BACK)
-    x_fwd = sti[plan[0, 0]].astype(f32)
-    ag[FWD, t] = (x_fwd * rms_of(x_fwd) * gain(ig, FWD)).astype(bf16)
+    angles = (p * TOK + lax.broadcasted_iota(jnp.int32, (TOK, HD // 2), 0)).astype(f32) * freq[...]
+    cos_ref[...] = jnp.cos(angles)
+    sin_ref[...] = jnp.sin(angles)
     gather_relay(BACK)
     gather_start(FWD)
     gather_finish(BACK)
@@ -349,9 +357,9 @@
     attention(BACK, True)
     loads[5].wait()
     before = len(drains)
-    scatter_first(BACK, out_product(BACK), lambda par: rows_of(cx.at[BACK], par))
+    scatter_first(BACK, out_product(BACK), rows_all(cx.at[BACK]))
     kv_second(FWD)
-    scatter_second(BACK, out_product(BACK), lambda par: rows_of(cx.at[BACK], par))
+    scatter_second(BACK)
     scatter_relay(BACK)
     kv_third(FWD)
     projected = scatter_finish(BACK)
@@ -359,13 +367,20 @@
     incoming = stg[plan[0, 1]].astype(f32)
     ag[GRAD, t] = rms_back(projected, incoming, gain(og, BACK)).astype(bf16)
     gather_start(GRAD)
+    go[...] = sti[plan[0, 1]]
+    fo[...] = stg[plan[0, 1]]
+    ahead = (
+        rcopy(go, bo.at[0], swap_s.at[2], swap_r.at[2], other),
+        rcopy(fo, bo.at[1], swap_s.at[0], swap_r.at[0], other),
+    )
+    for copy in ahead:
+        copy.start()
     kv_finish(FWD)
     attention(FWD, False)
     gather_relay(GRAD)
     loads[9].wait()
-    scatter_first(FWD, out_product(FWD), lambda par: rows_of(cx.at[FWD], par))
+    scatter_first(FWD, out_product(FWD), rows_all(cx.at[FWD]))
     gather_finish(GRAD)
-    scatter_second(FWD, out_product(FWD), lambda par: rows_of(cx.at[FWD], par))
 
     og_rows = ag[GRAD].reshape(TOK, D)
     for h in range(2):
@@ -373,6 +388,63 @@
             og_rows, wo[BACK, h * HD : (h + 1) * HD, :]
         ).astype(bf16)
     q_gain, k_gain = gain(qg, BACK), gain(kg, BACK)
+
+    R1, R2, R3, R4, R5, RR = 0, 1, 2, 3, 4, 5
+
+    def grad_block(i, d):
+        if i == 0:
+            gacc[0, d] = dot_tn(dss[:, d * TOK : (d + 1) * TOK], qs[BACK])
+        else:
+            gacc[1, d] = dot_tn(pl_s[:, d * TOK : (d + 1) * TOK], cgs[...])
+
+    def g_send(d, e, se, device, cond, i):
+        send(rcopy(gs.at[i, d - 1], gr.at[e, i], gss.at[se, i], gsr.at[e, i], device), cond)
+
+    def g_add(e, d, cond, i):
+        arrive(gr.at[e, i], gsr.at[e, i], cond)
+
+        @pl.when(cond)
+        def _():
+            gacc[i, d] = gacc[i, d] + gr[e, i].astype(f32)
+
+    def give(i, d):
+        gs[i, d - 1] = gacc[i, d].astype(bf16)
+
+    def g_second(i, cond):
+        g_send(3, R3, 2, z_up, cond & ((z == 3) | hi), i)
+        g_send(1, R1, 3, z_dn, cond & ((z >= 1) | hi), i)
+
+    def g_first(i):
+        grad_block(i, 2)
+        give(i, 2)
+        g_send(2, R2, 0, z_dn, z >= 2, i)
+        g_send(2, R5, 1, z_up, hi & (z <= 1), i)
+        grad_block(i, 3)
+        give(i, 3)
+        grad_block(i, 1)
+        give(i, 1)
+        g_second(i, ~mid)
+        grad_block(i, 4)
+        grad_block(i, 0)
+
+    def g_middle(i):
+        g_add(R5, 3, hi & mid, i)
+        g_add(R2, 1, mid, i)
+
+        @pl.when(mid)
+        def _():
+            give(i, 3)
+            give(i, 1)
+        g_second(i, mid)
+
+    def g_third(i):
+        g_add(R3, 4, hi & (z >= 1), i)
+        g_add(R1, 4, hi & (z == 3), i)
+        give(i, 4)
+        send(rcopy(gs.at[i, 3], gr.at[RR, 0], gss.at[4, i], gsr.at[RR, 0],
+                   y_up if i else y_dn), hi)
+
+    g_first(1)
 
     @pl.loop(0, 4)
     def _(ci):
@@ -382,100 +454,77 @@
         delta = jnp.sum(w * wg, axis=-1, keepdims=True)
         dss[rows, :] = (w * (wg - delta) * (HD ** -0.5)).astype(bf16)
 
-    scatter_relay(FWD)
-
-    def grad_block(d):
-        ds_d = dss[:, d * TOK : (d + 1) * TOK]
-        gacc[0, d] = dot_tn(ds_d, qs[BACK])
-        gacc[1, d] = dot_tn(pl_s[:, d * TOK : (d + 1) * TOK], cgs[...])
-
-    R1, R2, R3, R4, R5, RR = 0, 1, 2, 3, 4, 5
-
-    def give(d):
-        for i in range(2):
-            gs[i, d - 1] = gacc[i, d].astype(bf16)
-
-    def g_send(d, e, se, device, cond, i):
-        send(rcopy(gs.at[i, d - 1], gr.at[e, i], gss.at[se, i], gsr.at[e, i], device), cond)
-
-    def g_add(e, d, cond):
-        for i in range(2):
-            arrive(gr.at[e, i], gsr.at[e, i], cond)
-
-            @pl.when(cond)
-            def _():
-                gacc[i, d] = gacc[i, d] + gr[e, i].astype(f32)
-
-    grad_block(2)
-    give(2)
-    for i in range(2):
-        g_send(2, R2, 0, z_dn, z >= 2, i)
-        g_send(2, R5, 1, z_up, hi & (z <= 1), i)
-    grad_block(3)
-    grad_block(1)
-    g_add(R5, 3, hi & mid)
-    give(3)
-    for i in range(2):
-        g_send(3, R3, 2, z_up, (z == 3) | hi, i)
-    g_add(R2, 1, mid)
-    give(1)
-    for i in range(2):
-        g_send(1, R1, 3, z_dn, (z >= 1) | hi, i)
-    grad_block(4)
-    grad_block(0)
-    g_add(R3, 4, hi & (z >= 1))
-    g_add(R1, 4, hi & (z == 3))
-    give(4)
-    send(rcopy(gs.at[0, 3], gr.at[RR, 0], gss.at[4, 0], gsr.at[RR, 0], y_dn), hi)
-    send(rcopy(gs.at[1, 3], gr.at[RR, 0], gss.at[4, 1], gsr.at[RR, 0], y_up), hi)
+    g_first(0)
+    g_middle(1)
+    scatter_second(FWD)
+    g_middle(0)
+    g_third(1)
+    g_third(0)
 
     for h in range(2):
         rows = slice(h * TOK, (h + 1) * TOK)
         dq = dot(dss[rows, :], kvs[BACK, 0].reshape(5 * TOK, HD))
-        low = rms_back(qraw[rows], rope_back(dq, cosine, sine), q_gain).astype(bf16)
+        low = rms_back(
+            qraw[rows], rope_back(dq, cos_ref[...], sin_ref[...]), q_gain
+        ).astype(bf16)
         lq[:, :, h * HD : (h + 1) * HD] = low.reshape(8, ROWS, HD)
+    query_low = rows_all(lq)[:, : 2 * HD]
+    for n in range(NCH):
+        hq[:, cols(n)] = dot_nt(query_low, wq[BACK, n * CW : (n + 1) * CW, :])
 
     arrive(gr.at[RR, 0], gsr.at[RR, 0])
     send(rcopy(gr.at[RR, 0], gr.at[R4, 0], gss.at[5, 0], gsr.at[R4, 0], y_dn), relay_k)
     send(rcopy(gr.at[RR, 0], gr.at[R4, 1], gss.at[5, 1], gsr.at[R4, 1], y_up), relay_v)
-
+    for copy in ahead:
+        copy.wait_send()
+    scatter_relay(FWD)
+    for i in (1, 0):
+        g_add(R1, 0, z < 3, i)
+        g_add(R3, 0, z == 0, i)
+        g_add(R4, 0, lo, i)
+    key_low = rms_back(
+        kraw[...], rope_back(gacc[0, 0], cos_ref[...], sin_ref[...]), k_gain
+    ).astype(bf16)
+    lq[:, :, 2 * HD : 3 * HD] = key_low.reshape(8, ROWS, HD)
+    lq[:, :, 3 * HD :] = gacc[1, 0].astype(bf16).reshape(8, ROWS, HD)
+
+    for copy, _ in drains[before : before + NCH]:
+        copy.wait_send()
+    del drains[before : before + NCH]
+    scatter_first(2, hidden_product, rows_all(lq))
+    scatter_second(2)
     fwd_proj = scatter_finish(FWD)
     x_fwd = sti[plan[0, 0]].astype(f32)
     fo[...] = (x_fwd + fwd_proj * rms_of(fwd_proj) * gain(og, FWD)).astype(bf16)
     send(rcopy(fo, act_out, swap_s.at[1], swap_r.at[1], other))
-
-    g_add(R1, 0, z < 3)
-    g_add(R3, 0, z == 0)
-    g_add(R4, 0, lo)
-    key_low = rms_back(kraw[...], rope_back(gacc[0, 0], cosine, sine), k_gain).astype(bf16)
-    lq[:, :, 2 * HD : 3 * HD] = key_low.reshape(8, ROWS, HD)
-    lq[:, :, 3 * HD :] = gacc[1, 0].astype(bf16).reshape(8, ROWS, HD)
-
-    for copy, _ in drains[before : before + NCH]:
-        copy.wait_send()
-    del drains[before : before + NCH]
-    scatter_first(2, hidden_product, lambda par: rows_of(lq, par))
-    scatter_second(2, hidden_product, lambda par: rows_of(lq, par))
     scatter_relay(2)
-    hidden = scatter_finish(2)
-    x_back = sti[plan[0, 1]].astype(f32)
-    incoming = stg[plan[0, 1]].astype(f32)
-    go[...] = (incoming + rms_back(x_back, hidden, gain(ig, BACK))).astype(bf16)
-    send(rcopy(go, grad_out, swap_s.at[2], swap_r.at[2], other))
+    for n in range(NCH):
+        hidden = scatter_part(2, n)
+        gb[0, :, cols(n)] = (hidden * ig[pl.ds(legs[BACK], 1), cols(n)]).astype(bf16)
+        send(rcopy(gb.at[0, :, cols(n)], gb.at[1, :, cols(n)],
+                   swap_s.at[3 + n], swap_r.at[3 + n], other))
+    arrive(bo.at[0], swap_r.at[2])
+    arrive(bo.at[1], swap_r.at[0])
+    x_other = bo[0].astype(f32)
+    scale = rms_of(x_other)
+    for n in range(NCH):
+        arrive(gb.at[1, :, cols(n)], swap_r.at[3 + n])
+    g = gb[1].astype(f32)
+    centred = g - x_other * (scale * scale * jnp.mean(g * x_other, axis=-1, keepdims=True))
+    go[...] = (bo[1].astype(f32) + scale * centred).astype(bf16)
+    final = pltpu.make_async_copy(go, grad_out, lsem.at[10])
+    final.start()
     arrive(act_out, swap_r.at[1])
-    arrive(grad_out, swap_r.at[2])
     for copy, cond in drains:
         when(cond, copy.wait_send)
+    final.wait()
 
 
 def per_device(
     stash_inputs, stash_grads, plan, query_weight, key_weight, value_weight, out_weight,
     input_gain, output_gain, query_gain, key_gain,
 ):
-    block = lax.axis_index("ctx")
-    positions = (block * TOK + jnp.arange(TOK, dtype=jnp.int32)).astype(f32)
     frequency = rope_base ** (-(jnp.arange(HD // 2).astype(f32) * 2.0 / HD))
-    angles = positions[:, None] * frequency[None, :]
     vmem = pl.BlockSpec(memory_space=pltpu.VMEM)
     hbm = pl.BlockSpec(memory_space=pl.ANY)
     smem = pl.BlockSpec(memory_space=pltpu.SMEM)
@@ -484,7 +533,7 @@
     act, grad = pl.pallas_call(
         kernel,
         out_shape=(jax.ShapeDtypeStruct((ROWS, D), bf16),) * 2,
-        in_specs=[smem] + [vmem] * 6 + [hbm] * 6,
+        in_specs=[smem] + [vmem] * 5 + [hbm] * 6,
         out_specs=(hbm, hbm),
         scratch_shapes=[
             V((2, D, 2 * HD), bf16), V((2, D, HD), bf16), V((2, D, HD), bf16), V((2, 2 * HD, D), bf16),
@@ -496,18 +545,19 @@
             V((2 * TOK, 5 * TOK), f32), V((2 * TOK, 5 * TOK), bf16), V((2 * TOK, 5 * TOK), bf16),
             V((2 * TOK, HD), bf16),
             V((2, 4, ROWS, D), bf16), V((3, 4, ROWS, D), bf16), V((3, 3, ROWS, D), bf16),
-            V((3, 2, ROWS // 2, D), bf16), V((3, 2, ROWS, D), bf16), V((3, ROWS, D), f32),
+            V((3, 2, ROWS // 2, D), bf16), V((3, 2, ROWS, D), bf16), V((2, ROWS, D), f32),
             V((2, 4, TOK, HD), bf16), V((6, 2, TOK, HD), bf16), V((2, 5, TOK, HD), f32),
             V((8, ROWS, 4 * HD), bf16),
-            V((ROWS, D), bf16), V((ROWS, D), bf16),
-            sem((10,)), sem((3, 13)), sem((3, 13)), sem((3, NCH, 7)), sem((3, NCH, 7)),
-            sem((2, 7, 2)), sem((2, 5, 2)), sem((6, 2)), sem((6, 2)), sem((3,)), sem((3,)),
+            V((ROWS, D), bf16), V((ROWS, D), bf16), V((TOK, HD // 2), f32), V((TOK, HD // 2), f32),
+            V((2 * 4 * ROWS, D), f32), V((2, ROWS, D), bf16), V((2, ROWS, D), bf16),
+            sem((11,)), sem((3, 13)), sem((3, 13)), sem((3, NCH, 7)), sem((3, NCH, 7)),
+            sem((2, 7, 2)), sem((2, 5, 2)), sem((6, 2)), sem((6, 2)), sem((3 + NCH,)), sem((3 + NCH,)),
         ],
         compiler_params=pltpu.CompilerParams(
             collective_id=0, has_side_effects=True, vmem_limit_bytes=67043328
         ),
     )(
-        plan, jnp.cos(angles), jnp.sin(angles), input_gain[0], output_gain[0], query_gain[0],
+        plan, frequency[None, :], input_gain[0], output_gain[0], query_gain[0],
         key_gain[0], stash_inputs[0], stash_grads[0], query_weight[0], key_weight[0],
         value_weight[0], out_weight[0],
     )

time: 134 us -> 122 us (0.910)
  Pallas kernels: 129 us -> 117 us
    pallas_call x1, Pallas kernels: 129 us -> 117 us  [per_device(): pl.pallas_call(kernel, out_shape=(jax.ShapeDtypeStruct((ROWS, D), bf16),)...]
where the time goes in v2:
time: 122 us; the launch traced here: 121 us
  Pallas kernels  117 us (96%)
  local copies, waits for them, and re-layouts  3.31 us (3%)
    pallas_call x1, Pallas kernels, per_device(): pl.pallas_call(kernel, out_shape=(jax.ShapeDtypeStruct((ROWS, D), bf16),)...  117 us
    unnamed x2, local copies, waits for them, and re-layouts  3.31 us

profile of v2, /device:TPU:72, one launch (start us, length us, event | category | flops | bytes accessed | tf_op | source)
XLA Modules:
  0.0 121.4 jit_solution(13579853540202834744)
XLA Ops:
  0.6 0.5 negate_power_fusion.freq
  1.2 116.9 %shard_map.122 = (bf16[32,3840]{1,0:T(8,128)(2,1)}, bf16[32,3840]{1,0:T(8,128)(2,1)}) custom-call(s32[1,4]{1,0:T(1,128)} %plan.1, f32[1,128]{1,0:T(1,128)} %negate_power_fusion.freq, f32[2,3840]{1,0:T(2,128)} %bitcast.20, f32[2,3840]{1,0:T(2,128)} %bitcast.21, f32[2,256]{1,0:T(2,128)} %bitcast.22, f32[2,256]{1,0:T(2,128)} %bitcast.23, ...), custom_call_target="tpu_custom_call" | custom-call | tf_op jit(solution)/shard_map/pallas_call | solution.py:533
  118.1 1.7 %copy.15 = bf16[1,32,3840]{2,1,0:T(8,128)(2,1)} copy(bf16[1,32,3840]{2,1,0:T(8,128)(2,1)} %bitcast.19) | data formatting | bytes 491520
  119.7 1.7 %copy.16 = bf16[1,32,3840]{2,1,0:T(8,128)(2,1)} copy(bf16[1,32,3840]{2,1,0:T(8,128)(2,1)} %bitcast.18) | data formatting | bytes 491520

commit v3 on v2

--- a/solution.py
+++ b/solution.py
@@ -57,7 +57,7 @@
 def kernel(
     plan, freq, ig, og, qg, kg, si, sg, wq_h, wk_h, wv_h, wo_h,
     act_out, grad_out,
-    wq, wk, wv, wo, sti, stg, ag, qs, qraw, kraw, kvs, kvrl, cx, pw, pl_s, dss, cgs,
+    wq, wk, wv, wo, sti, stg, ag, qs, qraw, kraw, kvs, kvrl, grr, cx, pw, pl_s, dss, cgs,
     ps, pr, sb, rl, fr, own, gs, gr, gacc, lq, fo, go, cos_ref, sin_ref, hq, bo, gb,
     lsem, ags, agr, rss, rsr, kss, ksr, gss, gsr, swap_s, swap_r,
 ):
@@ -81,13 +81,14 @@
     t_p = 2 * x + 1 - c
     right, left, partner = dev(t_=t_r), dev(t_=t_l), dev(t_=t_p)
     z_up, z_dn = dev(p_=4 * yh + (z + 1) % 4), dev(p_=4 * yh + (z + 3) % 4)
+    z_op = dev(p_=4 * yh + (z + 2) % 4)
     y_u, y_d = (y + 1) % 4, (y + 3) % 4
     y_up = dev(s_=y_u % 2, p_=(y_u // 2) * 4 + z)
     y_dn = dev(s_=y_d % 2, p_=(y_d // 2) * 4 + z)
     other = dev(s_=1 - s)
 
     barrier = pltpu.get_barrier_semaphore()
-    for device in (right, left, partner, z_up, z_dn, y_up, y_dn):
+    for device in (right, left, partner, z_up, z_dn, z_op, y_up, y_dn):
         pl.semaphore_signal(barrier, inc=1, device_id=device, device_id_type=MESH)
 
     loads = [
@@ -235,26 +236,34 @@
     hi, lo = yh == 1, yh == 0
     mid = (z == 1) | (z == 2)
 
-    def kv_start(j):
-        k, v = kvs.at[j, 0, 0], kvs.at[j, 1, 0]
-        send(rcopy(k, kvrl.at[j], kss.at[j, 6, 0], ksr.at[j, 0, 0], y_up), lo)
-        send(rcopy(v, kvrl.at[j], kss.at[j, 6, 1], ksr.at[j, 0, 0], y_dn), lo)
+    relay_k = (y == 1) | (y == 2)
+    relay_v = (y == 0) | (y == 3)
+
+    def kv_near(j):
         for i in range(2):
             o = kvs.at[j, i, 0]
             send(rcopy(o, kvs.at[j, i, 1], kss.at[j, 1, i], ksr.at[j, 1, i], z_up), z < 3)
             send(rcopy(o, kvs.at[j, i, 3], kss.at[j, 3, i], ksr.at[j, 3, i], z_dn), z == 0)
-
-    relay_k = (y == 1) | (y == 2)
-    relay_v = (y == 0) | (y == 3)
+            send(rcopy(o, kvs.at[j, i, 2], kss.at[j, 5, i], ksr.at[j, 2, i], z_op), lo & (z >= 2))
+
+    def kv_cross(j):
+        k, v = kvs.at[j, 0, 0], kvs.at[j, 1, 0]
+        send(rcopy(k, kvrl.at[j, 0], kss.at[j, 6, 0], ksr.at[j, 0, 0], y_up), lo)
+        send(rcopy(v, kvrl.at[j, 0], kss.at[j, 6, 1], ksr.at[j, 0, 0], y_dn), lo)
 
     def kv_relay(j):
-        arrive(kvrl.at[j], ksr.at[j, 0, 0])
-        send(rcopy(kvrl.at[j], kvs.at[j, 0, 4], kss.at[j, 4, 0], ksr.at[j, 4, 0], y_up), relay_k)
-        send(rcopy(kvrl.at[j], kvs.at[j, 1, 4], kss.at[j, 4, 1], ksr.at[j, 4, 1], y_dn), relay_v)
+        b = kvrl.at[j, 0]
+        arrive(b, ksr.at[j, 0, 0])
+        send(rcopy(b, kvs.at[j, 0, 4], kss.at[j, 4, 0], ksr.at[j, 4, 0], y_up), relay_k)
+        send(rcopy(b, kvs.at[j, 1, 4], kss.at[j, 4, 1], ksr.at[j, 4, 1], y_dn), relay_v)
 
     def kv_second(j):
+        low = z <= 1
         for i in range(2):
-            b1, b4 = kvs.at[j, i, 1], kvs.at[j, i, 4]
+            b1, b2, b4 = (kvs.at[j, i, d] for d in (1, 2, 4))
+            arrive(b2, ksr.at[j, 2, i], lo & low)
+            send(rcopy(b2, kvrl.at[j, 1], kss.at[j, 0, i], ksr.at[j, 5, 0],
+                       y_dn if i else y_up), lo & low)
             arrive(b1, ksr.at[j, 1, i], mid)
             send(rcopy(b1, kvs.at[j, i, 2], kss.at[j, 2, i], ksr.at[j, 2, i], z_up), mid)
             arrive(b4, ksr.at[j, 4, i], hi)
@@ -262,16 +271,17 @@
             send(rcopy(b4, kvs.at[j, i, 1], kss.at[j, 1, i], ksr.at[j, 1, i], z_up), hi & (z == 3))
 
     def kv_third(j):
-        for i in range(2):
-            b3 = kvs.at[j, i, 3]
-            arrive(b3, ksr.at[j, 3, i], hi & mid)
-            send(rcopy(b3, kvs.at[j, i, 2], kss.at[j, 5, i], ksr.at[j, 2, i], z_dn), hi & mid)
+        low = z <= 1
+        b = kvrl.at[j, 1]
+        arrive(b, ksr.at[j, 5, 0], low)
+        send(rcopy(b, kvs.at[j, 0, 2], kss.at[j, 7, 0], ksr.at[j, 2, 0], y_up), low & relay_k)
+        send(rcopy(b, kvs.at[j, 1, 2], kss.at[j, 7, 1], ksr.at[j, 2, 1], y_dn), low & relay_v)
 
     def kv_finish(j):
         for i in range(2):
             arrive(kvs.at[j, i, 1], ksr.at[j, 1, i], (z == 3) | (hi & (z == 0)))
             arrive(kvs.at[j, i, 2], ksr.at[j, 2, i], (z >= 2) | hi)
-            arrive(kvs.at[j, i, 3], ksr.at[j, 3, i], (z == 3) | (hi & (z == 0)))
+            arrive(kvs.at[j, i, 3], ksr.at[j, 3, i], (z == 3) | hi)
 
     def project(j):
         cosine, sine = cos_ref[...], sin_ref[...]
@@ -282,7 +292,9 @@
         kr = dot(xn, wk[j])
         kvs[j, 0, 0] = rope(kr * rms_of(kr) * k_gain, cosine, sine).astype(bf16)
         kvs[j, 1, 0] = dot(xn, wv[j]).astype(bf16)
-        kv_start(j)
+        if j == BACK:
+            kv_cross(j)
+        kv_near(j)
         if j == BACK:
             kraw[...] = kr
         for h in range(2):
@@ -329,12 +341,12 @@
     loads[0].wait()
     x_back = sti[plan[0, 1]].astype(f32)
     ag[BACK, t] = (x_back * rms_of(x_back) * gain(ig, BACK)).astype(bf16)
-    pl.semaphore_wait(barrier, 7)
+    pl.semaphore_wait(barrier, 8)
     gather_start(BACK)
     x_fwd = sti[plan[0, 0]].astype(f32)
     ag[FWD, t] = (x_fwd * rms_of(x_fwd) * gain(ig, FWD)).astype(bf16)
     for j in range(2):
-        for d in range(1, 5):
+        for d in (1, 3, 4):
             @pl.when(d > p)
             def _():
                 for i in range(2):
@@ -352,6 +364,7 @@
     kv_second(BACK)
     project(FWD)
     kv_third(BACK)
+    kv_cross(FWD)
     kv_relay(FWD)
     kv_finish(BACK)
     attention(BACK, True)
@@ -389,60 +402,65 @@
         ).astype(bf16)
     q_gain, k_gain = gain(qg, BACK), gain(kg, BACK)
 
-    R1, R2, R3, R4, R5, RR = 0, 1, 2, 3, 4, 5
+    R1, R2, R3, R4, R5, RR, RS = 0, 1, 2, 3, 4, 5, 6
+    OWN, ONE, FOUR = 0, 1, 2
 
     def grad_block(i, d):
         if i == 0:
-            gacc[0, d] = dot_tn(dss[:, d * TOK : (d + 1) * TOK], qs[BACK])
-        else:
-            gacc[1, d] = dot_tn(pl_s[:, d * TOK : (d + 1) * TOK], cgs[...])
+            return dot_tn(dss[:, d * TOK : (d + 1) * TOK], qs[BACK])
+        return dot_tn(pl_s[:, d * TOK : (d + 1) * TOK], cgs[...])
 
     def g_send(d, e, se, device, cond, i):
         send(rcopy(gs.at[i, d - 1], gr.at[e, i], gss.at[se, i], gsr.at[e, i], device), cond)
 
-    def g_add(e, d, cond, i):
+    def g_add(e, k, cond, i):
         arrive(gr.at[e, i], gsr.at[e, i], cond)
 
         @pl.when(cond)
         def _():
-            gacc[i, d] = gacc[i, d] + gr[e, i].astype(f32)
-
-    def give(i, d):
-        gs[i, d - 1] = gacc[i, d].astype(bf16)
-
-    def g_second(i, cond):
-        g_send(3, R3, 2, z_up, cond & ((z == 3) | hi), i)
-        g_send(1, R1, 3, z_dn, cond & ((z >= 1) | hi), i)
+            gacc[i, k] = gacc[i, k] + gr[e, i].astype(f32)
 
     def g_first(i):
-        grad_block(i, 2)
-        give(i, 2)
+        gs[i, 1] = grad_block(i, 2).astype(bf16)
+        send(rcopy(gs.at[i, 1], grr.at[1], gss.at[1, i], gsr.at[RS, 0],
+                   y_up if i else y_dn), hi & (z <= 1))
         g_send(2, R2, 0, z_dn, z >= 2, i)
-        g_send(2, R5, 1, z_up, hi & (z <= 1), i)
-        grad_block(i, 3)
-        give(i, 3)
-        grad_block(i, 1)
-        give(i, 1)
-        g_second(i, ~mid)
-        grad_block(i, 4)
-        grad_block(i, 0)
+        gs[i, 2] = grad_block(i, 3).astype(bf16)
+        g_send(3, R3, 2, z_up, (z == 3) | hi, i)
+        gacc[i, ONE] = grad_block(i, 1)
+        gs[i, 0] = gacc[i, ONE].astype(bf16)
+        g_send(1, R1, 3, z_dn, (z == 3) | (hi & (z == 0)), i)
+        gacc[i, FOUR] = grad_block(i, 4)
+        gacc[i, OWN] = grad_block(i, 0)
 
     def g_middle(i):
-        g_add(R5, 3, hi & mid, i)
-        g_add(R2, 1, mid, i)
+        g_add(R2, ONE, mid, i)
 
         @pl.when(mid)
         def _():
-            give(i, 3)
-            give(i, 1)
-        g_second(i, mid)
+            gs[i, 0] = gacc[i, ONE].astype(bf16)
+        g_send(1, R1, 3, z_dn, mid, i)
 
     def g_third(i):
-        g_add(R3, 4, hi & (z >= 1), i)
-        g_add(R1, 4, hi & (z == 3), i)
-        give(i, 4)
-        send(rcopy(gs.at[i, 3], gr.at[RR, 0], gss.at[4, i], gsr.at[RR, 0],
+        g_add(R3, FOUR, hi & (z >= 1), i)
+        g_add(R1, FOUR, hi & (z == 3), i)
+        gs[i, 3] = gacc[i, FOUR].astype(bf16)
+        send(rcopy(gs.at[i, 3], grr.at[0], gss.at[4, i], gsr.at[RR, 0],
                    y_up if i else y_dn), hi)
+
+    def g_relay(i, far):
+        cond, device = (relay_v, y_up) if i else (relay_k, y_dn)
+        if far:
+            cond = cond & (z <= 1)
+        buf, rsem = grr.at[far], gsr.at[RS if far else RR, 0]
+        e = R5 if far else R4
+        arrive(buf, rsem, cond)
+        send(rcopy(buf, gr.at[e, i], gss.at[6 if far else 5, i], gsr.at[e, i], device), cond)
+
+    def g_forward(i):
+        cond = lo & (z <= 1)
+        arrive(gr.at[R5, i], gsr.at[R5, i], cond)
+        send(rcopy(gr.at[R5, i], gr.at[R5, i], gss.at[7, i], gsr.at[R5, i], z_op), cond)
 
     g_first(1)
 
@@ -456,10 +474,12 @@
 
     g_first(0)
     g_middle(1)
+    g_third(1)
+    g_relay(1, 1)
     scatter_second(FWD)
     g_middle(0)
-    g_third(1)
     g_third(0)
+    g_relay(0, 1)
 
     for h in range(2):
         rows = slice(h * TOK, (h + 1) * TOK)
@@ -472,16 +492,18 @@
     for n in range(NCH):
         hq[:, cols(n)] = dot_nt(query_low, wq[BACK, n * CW : (n + 1) * CW, :])
 
-    arrive(gr.at[RR, 0], gsr.at[RR, 0])
-    send(rcopy(gr.at[RR, 0], gr.at[R4, 0], gss.at[5, 0], gsr.at[R4, 0], y_dn), relay_k)
-    send(rcopy(gr.at[RR, 0], gr.at[R4, 1], gss.at[5, 1], gsr.at[R4, 1], y_up), relay_v)
+    g_forward(1)
+    g_relay(1, 0)
+    g_forward(0)
+    g_relay(0, 0)
     for copy in ahead:
         copy.wait_send()
     scatter_relay(FWD)
     for i in (1, 0):
-        g_add(R1, 0, z < 3, i)
-        g_add(R3, 0, z == 0, i)
-        g_add(R4, 0, lo, i)
+        g_add(R1, OWN, z < 3, i)
+        g_add(R3, OWN, z == 0, i)
+        g_add(R4, OWN, lo, i)
+        g_add(R5, OWN, lo & (z >= 2), i)
     key_low = rms_back(
         kraw[...], rope_back(gacc[0, 0], cos_ref[...], sin_ref[...]), k_gain
     ).astype(bf16)
@@ -540,18 +562,18 @@
             V((4, ROWS, D), bf16), V((4, ROWS, D), bf16),
             V((3, 8, ROWS, D), bf16),
             V((2, 2 * TOK, HD), bf16), V((2 * TOK, HD), f32), V((TOK, HD), f32),
-            V((2, 2, 5, TOK, HD), bf16), V((2, TOK, HD), bf16),
+            V((2, 2, 5, TOK, HD), bf16), V((2, 2, TOK, HD), bf16), V((2, TOK, HD), bf16),
             V((2, 8, ROWS, 2 * HD), bf16),
             V((2 * TOK, 5 * TOK), f32), V((2 * TOK, 5 * TOK), bf16), V((2 * TOK, 5 * TOK), bf16),
             V((2 * TOK, HD), bf16),
             V((2, 4, ROWS, D), bf16), V((3, 4, ROWS, D), bf16), V((3, 3, ROWS, D), bf16),
             V((3, 2, ROWS // 2, D), bf16), V((3, 2, ROWS, D), bf16), V((2, ROWS, D), f32),
-            V((2, 4, TOK, HD), bf16), V((6, 2, TOK, HD), bf16), V((2, 5, TOK, HD), f32),
+            V((2, 4, TOK, HD), bf16), V((5, 2, TOK, HD), bf16), V((2, 3, TOK, HD), f32),
             V((8, ROWS, 4 * HD), bf16),
             V((ROWS, D), bf16), V((ROWS, D), bf16), V((TOK, HD // 2), f32), V((TOK, HD // 2), f32),
             V((2 * 4 * ROWS, D), f32), V((2, ROWS, D), bf16), V((2, ROWS, D), bf16),
             sem((11,)), sem((3, 13)), sem((3, 13)), sem((3, NCH, 7)), sem((3, NCH, 7)),
-            sem((2, 7, 2)), sem((2, 5, 2)), sem((6, 2)), sem((6, 2)), sem((3 + NCH,)), sem((3 + NCH,)),
+            sem((2, 8, 2)), sem((2, 6, 2)), sem((8, 2)), sem((7, 2)), sem((3 + NCH,)), sem((3 + NCH,)),
         ],
         compiler_params=pltpu.CompilerParams(
             collective_id=0, has_side_effects=True, vmem_limit_bytes=67043328

time: 122 us -> 120 us (0.984)
  Pallas kernels: 117 us -> 115 us
    pallas_call x1, Pallas kernels: 117 us -> 115 us  [per_device(): pl.pallas_call(kernel, out_shape=(jax.ShapeDtypeStruct((ROWS, D), bf16),)...]
where the time goes in v3:
time: 120 us; the launch traced here: 119 us
  Pallas kernels  115 us (96%)
  local copies, waits for them, and re-layouts  3.31 us (3%)
    pallas_call x1, Pallas kernels, per_device(): pl.pallas_call(kernel, out_shape=(jax.ShapeDtypeStruct((ROWS, D), bf16),)...  115 us
    unnamed x2, local copies, waits for them, and re-layouts  3.31 us

profile of v3, /device:TPU:72, one launch (start us, length us, event | category | flops | bytes accessed | tf_op | source)
XLA Modules:
  0.0 119.0 jit_solution(3291624064849949308)
XLA Ops:
  0.6 0.5 negate_power_fusion.freq
  1.2 114.6 %shard_map.122 = (bf16[32,3840]{1,0:T(8,128)(2,1)}, bf16[32,3840]{1,0:T(8,128)(2,1)}) custom-call(s32[1,4]{1,0:T(1,128)} %plan.1, f32[1,128]{1,0:T(1,128)} %negate_power_fusion.freq, f32[2,3840]{1,0:T(2,128)} %bitcast.20, f32[2,3840]{1,0:T(2,128)} %bitcast.21, f32[2,256]{1,0:T(2,128)} %bitcast.22, f32[2,256]{1,0:T(2,128)} %bitcast.23, ...), custom_call_target="tpu_custom_call" | custom-call | tf_op jit(solution)/shard_map/pallas_call | solution.py:555
  115.7 1.7 %copy.15 = bf16[1,32,3840]{2,1,0:T(8,128)(2,1)} copy(bf16[1,32,3840]{2,1,0:T(8,128)(2,1)} %bitcast.19) | data formatting | bytes 491520
  117.4 1.7 %copy.16 = bf16[1,32,3840]{2,1,0:T(8,128)(2,1)} copy(bf16[1,32,3840]{2,1,0:T(8,128)(2,1)} %bitcast.18) | data formatting | bytes 491520

commit v4 on v3

--- a/solution.py
+++ b/solution.py
@@ -1,3 +1,5 @@
+import math
+
 import jax
 import jax.numpy as jnp
 from jax import lax
@@ -14,7 +16,7 @@
 ROWS = 32
 TOK = 256
 HD = 256
-NCH = 3
+NCH = 5
 CW = D // NCH
 BACK, FWD, GRAD = 0, 1, 2
 f32 = jnp.float32
@@ -55,10 +57,10 @@
 
 
 def kernel(
-    plan, freq, ig, og, qg, kg, si, sg, wq_h, wk_h, wv_h, wo_h,
+    plan, ig_h, og_h, qg_h, kg_h, si, sg, wq_h, wk_h, wv_h, wo_h,
     act_out, grad_out,
     wq, wk, wv, wo, sti, stg, ag, qs, qraw, kraw, kvs, kvrl, grr, cx, pw, pl_s, dss, cgs,
-    ps, pr, sb, rl, fr, own, gs, gr, gacc, lq, fo, go, cos_ref, sin_ref, hq, bo, gb,
+    ps, pr, sb, rl, fr, own, gs, gr, gacc, lq, fo, go, cos_ref, sin_ref, hq, bo, gb, ig, og, qg, kg, tops, sums,
     lsem, ags, agr, rss, rsr, kss, ksr, gss, gsr, swap_s, swap_r,
 ):
     s = lax.axis_index("segment")
@@ -102,7 +104,11 @@
             pltpu.make_async_copy(wv_h.at[legs[j]], wv.at[j], lsem.at[4 + 4 * j]),
             pltpu.make_async_copy(wo_h.at[legs[j]], wo.at[j], lsem.at[5 + 4 * j]),
         ]
-    for load in loads:
+    small = [
+        pltpu.make_async_copy(src, dst, lsem.at[11 + k])
+        for k, (src, dst) in enumerate(((ig_h, ig), (og_h, og), (qg_h, qg), (kg_h, kg)))
+    ]
+    for load in loads[:1] + small + loads[1:]:
         load.start()
 
     def gain(ref, j):
@@ -239,12 +245,15 @@
     relay_k = (y == 1) | (y == 2)
     relay_v = (y == 0) | (y == 3)
 
+    TH = (pl.ds(0, TOK // 2), pl.ds(TOK // 2, TOK // 2))
+
     def kv_near(j):
         for i in range(2):
             o = kvs.at[j, i, 0]
             send(rcopy(o, kvs.at[j, i, 1], kss.at[j, 1, i], ksr.at[j, 1, i], z_up), z < 3)
             send(rcopy(o, kvs.at[j, i, 3], kss.at[j, 3, i], ksr.at[j, 3, i], z_dn), z == 0)
-            send(rcopy(o, kvs.at[j, i, 2], kss.at[j, 5, i], ksr.at[j, 2, i], z_op), lo & (z >= 2))
+            send(rcopy(o, kvs.at[j, i, 2], kss.at[j, 5, i], ksr.at[j, 2, i], z_op), lo & (z == 3))
+            send(rcopy(o, kvs.at[j, i, 3], kss.at[j, 3, i], ksr.at[j, 3, i], z_dn), lo & (z == 1))
 
     def kv_cross(j):
         k, v = kvs.at[j, 0, 0], kvs.at[j, 1, 0]
@@ -259,29 +268,57 @@
 
     def kv_second(j):
         low = z <= 1
+        far = jnp.maximum(3 - z, 2)
         for i in range(2):
-            b1, b2, b4 = (kvs.at[j, i, d] for d in (1, 2, 4))
-            arrive(b2, ksr.at[j, 2, i], lo & low)
+            b1, b2, b4 = (kvs.at[j, i, d] for d in (1, far, 4))
+            arrive(b2, ksr.at[j, far, i], lo & low)
             send(rcopy(b2, kvrl.at[j, 1], kss.at[j, 0, i], ksr.at[j, 5, 0],
                        y_dn if i else y_up), lo & low)
             arrive(b1, ksr.at[j, 1, i], mid)
             send(rcopy(b1, kvs.at[j, i, 2], kss.at[j, 2, i], ksr.at[j, 2, i], z_up), mid)
             arrive(b4, ksr.at[j, 4, i], hi)
-            send(rcopy(b4, kvs.at[j, i, 3], kss.at[j, 3, i], ksr.at[j, 3, i], z_dn), hi & (z >= 1))
+            if i == 0:
+                send(rcopy(b4, kvs.at[j, 0, 3], kss.at[j, 3, 0], ksr.at[j, 3, 0], z_dn), hi & (z >= 2))
+            else:
+                send(rcopy(b4, kvs.at[j, 1, 3], kss.at[j, 3, 1], ksr.at[j, 3, 1], z_dn), hi & (z == 3))
+                for q in range(2):
+                    send(rcopy(b4.at[TH[q]], kvs.at[j, 1, 3, TH[q]], kss.at[j, 8, q],
+                               ksr.at[j, 6, q], z_dn), hi & (z == 2))
             send(rcopy(b4, kvs.at[j, i, 1], kss.at[j, 1, i], ksr.at[j, 1, i], z_up), hi & (z == 3))
 
     def kv_third(j):
         low = z <= 1
         b = kvrl.at[j, 1]
         arrive(b, ksr.at[j, 5, 0], low)
-        send(rcopy(b, kvs.at[j, 0, 2], kss.at[j, 7, 0], ksr.at[j, 2, 0], y_up), low & relay_k)
-        send(rcopy(b, kvs.at[j, 1, 2], kss.at[j, 7, 1], ksr.at[j, 2, 1], y_dn), low & relay_v)
-
-    def kv_finish(j):
+        far = jnp.maximum(3 - z, 2)
+        send(rcopy(b, kvs.at[j, 0, far], kss.at[j, 7, 0], ksr.at[j, far, 0], y_up), low & relay_k)
+        send(rcopy(b, kvs.at[j, 1, far], kss.at[j, 7, 1], ksr.at[j, far, 1], y_dn), low & relay_v)
+
+    def kv_fourth(j):
+        cond = hi & (z == 1)
+        b3 = kvs.at[j, 0, 3]
+        arrive(b3, ksr.at[j, 3, 0], cond)
+        send(rcopy(b3, kvs.at[j, 0, 2], kss.at[j, 5, 0], ksr.at[j, 2, 0], z_dn), cond)
+        for q in range(2):
+            b3 = kvs.at[j, 1, 3, TH[q]]
+            arrive(b3, ksr.at[j, 6, q], cond)
+            send(rcopy(b3, kvs.at[j, 1, 2, TH[q]], kss.at[j, 9, q], ksr.at[j, 7, q], z_dn), cond)
+
+    def kv_near_in(j):
         for i in range(2):
             arrive(kvs.at[j, i, 1], ksr.at[j, 1, i], (z == 3) | (hi & (z == 0)))
-            arrive(kvs.at[j, i, 2], ksr.at[j, 2, i], (z >= 2) | hi)
-            arrive(kvs.at[j, i, 3], ksr.at[j, 3, i], (z == 3) | hi)
+            arrive(kvs.at[j, i, 3], ksr.at[j, 3, i], (z == 3) | (hi & (z != 1)))
+
+    def kv_far_in(j):
+        four = hi & (z == 0)
+        arrive(kvs.at[j, 0, 2], ksr.at[j, 2, 0], (z >= 2) | hi)
+        arrive(kvs.at[j, 1, 2], ksr.at[j, 2, 1], (z >= 2) | (hi & (z == 1)))
+        for q in range(2):
+            arrive(kvs.at[j, 1, 2, TH[q]], ksr.at[j, 7, q], four)
+
+    def kv_finish(j):
+        kv_near_in(j)
+        kv_far_in(j)
 
     def project(j):
         cosine, sine = cos_ref[...], sin_ref[...]
@@ -305,30 +342,67 @@
             if j == BACK:
                 qraw[h * TOK : (h + 1) * TOK] = qr
 
-    def attention(j, keep):
+    def visible(ci, first, count):
+        col = first * TOK + lax.broadcasted_iota(jnp.int32, (1, count * TOK), 1)
+        back = (col // TOK) * TOK - col % TOK
+        back = jnp.where(col // TOK <= p, back, -4 * WINDOW)
+        rel = (ci % 2) * 128 + lax.broadcasted_iota(jnp.int32, (128, 1), 0) + back
+        return (rel >= 0) & (rel < WINDOW)
+
+    def scores(j, ci, rows, first, count):
+        keys = kvs[j, 0, first : first + count].reshape(count * TOK, HD)
+        sc = dot_nt(qs[j, rows, :], keys) * (HD ** -0.5)
+        return jnp.where(visible(ci, first, count), sc, masked_score)
+
+    def chunk_rows(ci):
+        return pl.ds(pl.multiple_of(ci * 128, 128), 128)
+
+    def weigh(j, ci, low):
+        out = dot(low, kvs[j, 1].reshape(5 * TOK, HD)).astype(bf16)
+        for h in range(2):
+            @pl.when(ci // 2 == h)
+            def _():
+                cx[j, pl.ds(4 * (ci % 2), 4), :, h * HD : (h + 1) * HD] = out.reshape(4, ROWS, HD)
+
+    def attend_near():
         @pl.loop(0, 4)
         def _(ci):
-            rows = pl.ds(pl.multiple_of(ci * 128, 128), 128)
-            sc = dot_nt(qs[j, rows, :], kvs[j, 0].reshape(5 * TOK, HD)) * (HD ** -0.5)
-            col = lax.broadcasted_iota(jnp.int32, (1, 5 * TOK), 1)
-            back = (col // TOK) * TOK - col % TOK
-            back = jnp.where(col // TOK <= p, back, -4 * WINDOW)
-            ii = (ci % 2) * 128 + lax.broadcasted_iota(jnp.int32, (128, 1), 0)
-            rel = ii + back
-            sc = jnp.where((rel >= 0) & (rel < WINDOW), sc, masked_score)
+            rows = chunk_rows(ci)
+            sa, sb_ = scores(BACK, ci, rows, 0, 2), scores(BACK, ci, rows, 3, 2)
+            top = jnp.maximum(
+                jnp.max(sa, axis=-1, keepdims=True), jnp.max(sb_, axis=-1, keepdims=True)
+            )
+            ea, eb = jnp.exp(sa - top), jnp.exp(sb_ - top)
+            pw[rows, : 2 * TOK] = ea
+            pw[rows, 3 * TOK :] = eb
+            tops[rows, :] = top
+            sums[rows, :] = jnp.sum(ea, axis=-1, keepdims=True) + jnp.sum(eb, axis=-1, keepdims=True)
+
+    def attend_far():
+        @pl.loop(0, 4)
+        def _(ci):
+            rows = chunk_rows(ci)
+            sc = scores(BACK, ci, rows, 2, 1)
+            top = jnp.maximum(tops[rows, :], jnp.max(sc, axis=-1, keepdims=True))
+            e = jnp.exp(sc - top)
+            near = jnp.exp(tops[rows, :] - top)
+            inverse = 1.0 / (sums[rows, :] * near + jnp.sum(e, axis=-1, keepdims=True))
+            near = near * inverse
+            w = jnp.concatenate(
+                [pw[rows, : 2 * TOK] * near, e * inverse, pw[rows, 3 * TOK :] * near], axis=-1
+            )
+            low = w.astype(bf16)
+            pw[rows, :] = w
+            pl_s[rows, :] = low
+            weigh(BACK, ci, low)
+
+    def attention(j):
+        @pl.loop(0, 4)
+        def _(ci):
+            sc = scores(j, ci, chunk_rows(ci), 0, 5)
             e = jnp.exp(sc - jnp.max(sc, axis=-1, keepdims=True))
-            w = e / jnp.sum(e, axis=-1, keepdims=True)
-            low = w.astype(bf16)
-            if keep:
-                pw[rows, :] = w
-                pl_s[rows, :] = low
-            out = dot(low, kvs[j, 1].reshape(5 * TOK, HD)).astype(bf16)
-            for h in range(2):
-                @pl.when(ci // 2 == h)
-                def _():
-                    cx[j, pl.ds(4 * (ci % 2), 4), :, h * HD : (h + 1) * HD] = out.reshape(
-                        4, ROWS, HD
-                    )
+            w = e * (1.0 / jnp.sum(e, axis=-1, keepdims=True))
+            weigh(j, ci, w.astype(bf16))
 
     def out_product(j):
         return lambda lhs, n: dot(lhs, wo[j, :, n * CW : (n + 1) * CW])
@@ -339,6 +413,8 @@
         return total + dot_nt(lhs[:, 3 * HD :], wv[BACK, w_rows, :])
 
     loads[0].wait()
+    for load in small:
+        load.wait()
     x_back = sti[plan[0, 1]].astype(f32)
     ag[BACK, t] = (x_back * rms_of(x_back) * gain(ig, BACK)).astype(bf16)
     pl.semaphore_wait(barrier, 8)
@@ -346,12 +422,14 @@
     x_fwd = sti[plan[0, 0]].astype(f32)
     ag[FWD, t] = (x_fwd * rms_of(x_fwd) * gain(ig, FWD)).astype(bf16)
     for j in range(2):
-        for d in (1, 3, 4):
-            @pl.when(d > p)
+        for d in range(1, 5):
+            @pl.when((d > p) & (d + p != 3))
             def _():
                 for i in range(2):
                     kvs[j, i, d] = jnp.zeros((TOK, HD), bf16)
-    angles = (p * TOK + lax.broadcasted_iota(jnp.int32, (TOK, HD // 2), 0)).astype(f32) * freq[...]
+    angles = (p * TOK + lax.broadcasted_iota(jnp.int32, (TOK, HD // 2), 0)).astype(f32)
+    pair = lax.broadcasted_iota(jnp.int32, (1, HD // 2), 1).astype(f32)
+    angles = angles * jnp.exp(pair * (-2.0 * math.log(rope_base) / HD))
     cos_ref[...] = jnp.cos(angles)
     sin_ref[...] = jnp.sin(angles)
     gather_relay(BACK)
@@ -365,9 +443,12 @@
     project(FWD)
     kv_third(BACK)
     kv_cross(FWD)
+    kv_fourth(BACK)
+    kv_near_in(BACK)
+    attend_near()
     kv_relay(FWD)
-    kv_finish(BACK)
-    attention(BACK, True)
+    kv_far_in(BACK)
+    attend_far()
     loads[5].wait()
     before = len(drains)
     scatter_first(BACK, out_product(BACK), rows_all(cx.at[BACK]))
@@ -375,6 +456,7 @@
     scatter_second(BACK)
     scatter_relay(BACK)
     kv_third(FWD)
+    kv_fourth(FWD)
     projected = scatter_finish(BACK)
     loads[1].wait()
     incoming = stg[plan[0, 1]].astype(f32)
@@ -389,7 +471,7 @@
     for copy in ahead:
         copy.start()
     kv_finish(FWD)
-    attention(FWD, False)
+    attention(FWD)
     gather_relay(GRAD)
     loads[9].wait()
     scatter_first(FWD, out_product(FWD), rows_all(cx.at[FWD]))
@@ -546,8 +628,6 @@
     stash_inputs, stash_grads, plan, query_weight, key_weight, value_weight, out_weight,
     input_gain, output_gain, query_gain, key_gain,
 ):
-    frequency = rope_base ** (-(jnp.arange(HD // 2).astype(f32) * 2.0 / HD))
-    vmem = pl.BlockSpec(memory_space=pltpu.VMEM)
     hbm = pl.BlockSpec(memory_space=pl.ANY)
     smem = pl.BlockSpec(memory_space=pltpu.SMEM)
     V = pltpu.VMEM
@@ -555,7 +635,7 @@
     act, grad = pl.pallas_call(
         kernel,
         out_shape=(jax.ShapeDtypeStruct((ROWS, D), bf16),) * 2,
-        in_specs=[smem] + [vmem] * 5 + [hbm] * 6,
+        in_specs=[smem] + [hbm] * 10,
         out_specs=(hbm, hbm),
         scratch_shapes=[
             V((2, D, 2 * HD), bf16), V((2, D, HD), bf16), V((2, D, HD), bf16), V((2, 2 * HD, D), bf16),
@@ -572,14 +652,16 @@
             V((8, ROWS, 4 * HD), bf16),
             V((ROWS, D), bf16), V((ROWS, D), bf16), V((TOK, HD // 2), f32), V((TOK, HD // 2), f32),
             V((2 * 4 * ROWS, D), f32), V((2, ROWS, D), bf16), V((2, ROWS, D), bf16),
-            sem((11,)), sem((3, 13)), sem((3, 13)), sem((3, NCH, 7)), sem((3, NCH, 7)),
-            sem((2, 8, 2)), sem((2, 6, 2)), sem((8, 2)), sem((7, 2)), sem((3 + NCH,)), sem((3 + NCH,)),
+            V((2, D), f32), V((2, D), f32), V((2, HD), f32), V((2, HD), f32),
+            V((2 * TOK, 1), f32), V((2 * TOK, 1), f32),
+            sem((15,)), sem((3, 13)), sem((3, 13)), sem((3, NCH, 7)), sem((3, NCH, 7)),
+            sem((2, 10, 2)), sem((2, 8, 2)), sem((8, 2)), sem((7, 2)), sem((3 + NCH,)), sem((3 + NCH,)),
         ],
         compiler_params=pltpu.CompilerParams(
             collective_id=0, has_side_effects=True, vmem_limit_bytes=67043328
         ),
     )(
-        plan, frequency[None, :], input_gain[0], output_gain[0], query_gain[0],
+        plan, input_gain[0], output_gain[0], query_gain[0],
         key_gain[0], stash_inputs[0], stash_grads[0], query_weight[0], key_weight[0],
         value_weight[0], out_weight[0],
     )

time: 120 us -> 115 us (0.958)
  Pallas kernels: 115 us -> 111 us
    pallas_call x1, Pallas kernels: 115 us -> 111 us  [per_device(): pl.pallas_call(kernel, out_shape=(jax.ShapeDtypeStruct((ROWS, D), bf16),)...]
where the time goes in v4:
time: 115 us
  Pallas kernels  111 us (97%)
  local copies, waits for them, and re-layouts  3.31 us (3%)
    pallas_call x1, Pallas kernels, per_device(): pl.pallas_call(kernel, out_shape=(jax.ShapeDtypeStruct((ROWS, D), bf16),)...  111 us
    unnamed x2, local copies, waits for them, and re-layouts  3.31 us

profile of v4, /device:TPU:72, one launch (start us, length us, event | category | flops | bytes accessed | tf_op | source)
XLA Modules:
  0.0 114.8 jit_solution(1187539621718864420)
XLA Ops:
  0.6 110.9 %shard_map.122 = (bf16[32,3840]{1,0:T(8,128)(2,1)}, bf16[32,3840]{1,0:T(8,128)(2,1)}) custom-call(s32[1,4]{1,0:T(1,128)} %plan.1, f32[2,3840]{1,0:T(2,128)} %bitcast.20, f32[2,3840]{1,0:T(2,128)} %bitcast.21, f32[2,256]{1,0:T(2,128)} %bitcast.22, f32[2,256]{1,0:T(2,128)} %bitcast.23, bf16[4,32,3840]{2,1,0:T(8,128)(2,1)} %bitcast.16, ...), custom_call_target="tpu_custom_call" | custom-call | tf_op jit(solution)/shard_map/pallas_call | solution.py:635
  111.5 1.7 %copy.15 = bf16[1,32,3840]{2,1,0:T(8,128)(2,1)} copy(bf16[1,32,3840]{2,1,0:T(8,128)(2,1)} %bitcast.19) | data formatting | bytes 491520
  113.2 1.7 %copy.16 = bf16[1,32,3840]{2,1,0:T(8,128)(2,1)} copy(bf16[1,32,3840]{2,1,0:T(8,128)(2,1)} %bitcast.18) | data formatting | bytes 491520

commit v5 on v4

--- a/solution.py
+++ b/solution.py
@@ -189,42 +189,59 @@
     def rows_all(ref):
         return jnp.concatenate([rows_of(ref, 1 - c), rows_of(ref, c)], axis=0)
 
-    def scatter_first(r, product, lhs):
+    def sent(r, first, last):
+        for key in [k for k in flying if k[0] == r and first <= k[1] <= last]:
+            for copy in flying.pop(key):
+                copy.wait_send()
+
+    flying = {}
+
+    def send_sum(r, i, copy):
+        copy.start()
+        flying.setdefault((r, i), []).append(copy)
+
+    def scatter_first(r, product, lhs, then=None):
+        if r:
+            sent(r - 1, 0, 0)
         for n in range(NCH):
+            if then and n >= 3:
+                then(n - 3)
             total = product(lhs, n)
-            ps[r % 2, :, :, cols(n)] = total[: 4 * ROWS].astype(bf16).reshape(4, ROWS, CW)
-            send(rcopy(ps.at[r % 2, :, :, cols(n)], pr.at[r, :, :, cols(n)],
+            ps[:, :, cols(n)] = total[: 4 * ROWS].astype(bf16).reshape(4, ROWS, CW)
+            send_sum(r, 0, rcopy(ps.at[:, :, cols(n)], pr.at[r, :, :, cols(n)],
                        rss.at[r, n, 0], rsr.at[r, n, 0], partner))
             hq[4 * ROWS :, cols(n)] = total[4 * ROWS :]
 
-    def scatter_second(r):
-        for n in range(NCH):
+    def scatter_second(r, numbers=range(NCH)):
+        if r == 2 and 0 in numbers:
+            sent(0, 1, 6)
+        for n in numbers:
             arrive(pr.at[r, :, :, cols(n)], rsr.at[r, n, 0])
             total = hq[4 * ROWS :, cols(n)].reshape(4, ROWS, CW) + pr[r, :, :, cols(n)].astype(f32)
             own[r % 2, :, cols(n)] = total[0]
-            sb[r, :, :, cols(n)] = total[1:].astype(bf16)
-            send(rcopy(sb.at[r, 1, H0, cols(n)], rl.at[r, 0, :, cols(n)],
+            sb[r % 2, :, :, cols(n)] = total[1:].astype(bf16)
+            send_sum(r, 1, rcopy(sb.at[r % 2, 1, H0, cols(n)], rl.at[r, 0, :, cols(n)],
                        rss.at[r, n, 1], rsr.at[r, n, 1], right))
-            send(rcopy(sb.at[r, 1, H1, cols(n)], rl.at[r, 1, :, cols(n)],
+            send_sum(r, 2, rcopy(sb.at[r % 2, 1, H1, cols(n)], rl.at[r, 1, :, cols(n)],
                        rss.at[r, n, 2], rsr.at[r, n, 2], left))
-            send(rcopy(sb.at[r, 0, H1, cols(n)], fr.at[r, 0, H1, cols(n)],
+            send_sum(r, 3, rcopy(sb.at[r % 2, 0, H1, cols(n)], fr.at[r, 0, H1, cols(n)],
                        rss.at[r, n, 3], rsr.at[r, n, 3], right))
-            send(rcopy(sb.at[r, 2, H0, cols(n)], fr.at[r, 1, H0, cols(n)],
+            send_sum(r, 4, rcopy(sb.at[r % 2, 2, H0, cols(n)], fr.at[r, 1, H0, cols(n)],
                        rss.at[r, n, 4], rsr.at[r, n, 4], left))
 
     def scatter_relay(r):
         for n in range(NCH):
             arrive(rl.at[r, 0, :, cols(n)], rsr.at[r, n, 1])
-            sb[r, 0, H0, cols(n)] = (
-                sb[r, 0, H0, cols(n)].astype(f32) + rl[r, 0, :, cols(n)].astype(f32)
+            sb[r % 2, 0, H0, cols(n)] = (
+                sb[r % 2, 0, H0, cols(n)].astype(f32) + rl[r, 0, :, cols(n)].astype(f32)
             ).astype(bf16)
-            send(rcopy(sb.at[r, 0, H0, cols(n)], fr.at[r, 0, H0, cols(n)],
+            send_sum(r, 5, rcopy(sb.at[r % 2, 0, H0, cols(n)], fr.at[r, 0, H0, cols(n)],
                        rss.at[r, n, 5], rsr.at[r, n, 5], right))
             arrive(rl.at[r, 1, :, cols(n)], rsr.at[r, n, 2])
-            sb[r, 2, H1, cols(n)] = (
-                sb[r, 2, H1, cols(n)].astype(f32) + rl[r, 1, :, cols(n)].astype(f32)
+            sb[r % 2, 2, H1, cols(n)] = (
+                sb[r % 2, 2, H1, cols(n)].astype(f32) + rl[r, 1, :, cols(n)].astype(f32)
             ).astype(bf16)
-            send(rcopy(sb.at[r, 2, H1, cols(n)], fr.at[r, 1, H1, cols(n)],
+            send_sum(r, 6, rcopy(sb.at[r % 2, 2, H1, cols(n)], fr.at[r, 1, H1, cols(n)],
                        rss.at[r, n, 6], rsr.at[r, n, 6], left))
 
     def scatter_part(r, n):
@@ -277,13 +294,10 @@
             arrive(b1, ksr.at[j, 1, i], mid)
             send(rcopy(b1, kvs.at[j, i, 2], kss.at[j, 2, i], ksr.at[j, 2, i], z_up), mid)
             arrive(b4, ksr.at[j, 4, i], hi)
-            if i == 0:
-                send(rcopy(b4, kvs.at[j, 0, 3], kss.at[j, 3, 0], ksr.at[j, 3, 0], z_dn), hi & (z >= 2))
-            else:
-                send(rcopy(b4, kvs.at[j, 1, 3], kss.at[j, 3, 1], ksr.at[j, 3, 1], z_dn), hi & (z == 3))
-                for q in range(2):
-                    send(rcopy(b4.at[TH[q]], kvs.at[j, 1, 3, TH[q]], kss.at[j, 8, q],
-                               ksr.at[j, 6, q], z_dn), hi & (z == 2))
+            send(rcopy(b4, kvs.at[j, i, 3], kss.at[j, 3, i], ksr.at[j, 3, i], z_dn), hi & (z == 3))
+            for q in range(2):
+                send(rcopy(b4.at[TH[q]], kvs.at[j, i, 3, TH[q]], kss.at[j, 8 + i, q],
+                           ksr.at[j, 6 + i, q], z_dn), hi & (z == 2))
             send(rcopy(b4, kvs.at[j, i, 1], kss.at[j, 1, i], ksr.at[j, 1, i], z_up), hi & (z == 3))
 
     def kv_third(j):
@@ -296,13 +310,12 @@
 
     def kv_fourth(j):
         cond = hi & (z == 1)
-        b3 = kvs.at[j, 0, 3]
-        arrive(b3, ksr.at[j, 3, 0], cond)
-        send(rcopy(b3, kvs.at[j, 0, 2], kss.at[j, 5, 0], ksr.at[j, 2, 0], z_dn), cond)
-        for q in range(2):
-            b3 = kvs.at[j, 1, 3, TH[q]]
-            arrive(b3, ksr.at[j, 6, q], cond)
-            send(rcopy(b3, kvs.at[j, 1, 2, TH[q]], kss.at[j, 9, q], ksr.at[j, 7, q], z_dn), cond)
+        for i in range(2):
+            for q in range(2):
+                b3 = kvs.at[j, i, 3, TH[q]]
+                arrive(b3, ksr.at[j, 6 + i, q], cond)
+                send(rcopy(b3, kvs.at[j, i, 2, TH[q]], kss.at[j, 10 + i, q],
+                           ksr.at[j, 8 + i, q], z_dn), cond)
 
     def kv_near_in(j):
         for i in range(2):
@@ -311,10 +324,10 @@
 
     def kv_far_in(j):
         four = hi & (z == 0)
-        arrive(kvs.at[j, 0, 2], ksr.at[j, 2, 0], (z >= 2) | hi)
-        arrive(kvs.at[j, 1, 2], ksr.at[j, 2, 1], (z >= 2) | (hi & (z == 1)))
-        for q in range(2):
-            arrive(kvs.at[j, 1, 2, TH[q]], ksr.at[j, 7, q], four)
+        for i in range(2):
+            arrive(kvs.at[j, i, 2], ksr.at[j, 2, i], (z >= 2) | (hi & (z == 1)))
+            for q in range(2):
+                arrive(kvs.at[j, i, 2, TH[q]], ksr.at[j, 8 + i, q], four)
 
     def kv_finish(j):
         kv_near_in(j)
@@ -336,73 +349,82 @@
             kraw[...] = kr
         for h in range(2):
             qr = dot(xn, wq[j, :, h * HD : (h + 1) * HD])
-            qs[j, h * TOK : (h + 1) * TOK] = rope(
-                qr * rms_of(qr) * q_gain, cosine, sine
-            ).astype(bf16)
+            query = rope(qr * rms_of(qr) * q_gain, cosine, sine).astype(bf16)
+            qs[j, h * TOK : (h + 1) * TOK] = query * jnp.asarray(HD ** -0.5, bf16)
             if j == BACK:
                 qraw[h * TOK : (h + 1) * TOK] = qr
 
-    def visible(ci, first, count):
-        col = first * TOK + lax.broadcasted_iota(jnp.int32, (1, count * TOK), 1)
-        back = (col // TOK) * TOK - col % TOK
-        back = jnp.where(col // TOK <= p, back, -4 * WINDOW)
-        rel = (ci % 2) * 128 + lax.broadcasted_iota(jnp.int32, (128, 1), 0) + back
-        return (rel >= 0) & (rel < WINDOW)
-
-    def scores(j, ci, rows, first, count):
-        keys = kvs[j, 0, first : first + count].reshape(count * TOK, HD)
-        sc = dot_nt(qs[j, rows, :], keys) * (HD ** -0.5)
-        return jnp.where(visible(ci, first, count), sc, masked_score)
+    def score(j, ci, d):
+        sc = dot_nt(qs[j, chunk_rows(ci), :], kvs[j, 0, d])
+        if d in (0, 4):
+            ii = lax.broadcasted_iota(jnp.int32, (TOK, TOK), 0)
+            ahead_by = ii - lax.broadcasted_iota(jnp.int32, (TOK, TOK), 1)
+            if d == 0:
+                return jnp.where(ahead_by >= 0, sc, masked_score)
+            return jnp.where(ahead_by < jnp.where(p >= 4, 0, -TOK), sc, masked_score)
+        return sc + jnp.where(p >= d, 0.0, masked_score)
+
+    def top_of(scs):
+        top = jnp.max(scs[0], axis=-1, keepdims=True)
+        for sc in scs[1:]:
+            top = jnp.maximum(top, jnp.max(sc, axis=-1, keepdims=True))
+        return top
+
+    def sum_of(es):
+        total = es[0]
+        for e in es[1:]:
+            total = total + e
+        return jnp.sum(total, axis=-1, keepdims=True)
 
     def chunk_rows(ci):
-        return pl.ds(pl.multiple_of(ci * 128, 128), 128)
+        return slice(ci * TOK, (ci + 1) * TOK)
 
     def weigh(j, ci, low):
         out = dot(low, kvs[j, 1].reshape(5 * TOK, HD)).astype(bf16)
-        for h in range(2):
-            @pl.when(ci // 2 == h)
-            def _():
-                cx[j, pl.ds(4 * (ci % 2), 4), :, h * HD : (h + 1) * HD] = out.reshape(4, ROWS, HD)
+        cx[j, :, :, ci * HD : (ci + 1) * HD] = out.reshape(8, ROWS, HD)
+
+    near_blocks = (0, 1, 3, 4)
+
+    def block_cols(d):
+        return slice(d * TOK, (d + 1) * TOK)
 
     def attend_near():
-        @pl.loop(0, 4)
-        def _(ci):
+        for ci in range(2):
             rows = chunk_rows(ci)
-            sa, sb_ = scores(BACK, ci, rows, 0, 2), scores(BACK, ci, rows, 3, 2)
-            top = jnp.maximum(
-                jnp.max(sa, axis=-1, keepdims=True), jnp.max(sb_, axis=-1, keepdims=True)
-            )
-            ea, eb = jnp.exp(sa - top), jnp.exp(sb_ - top)
-            pw[rows, : 2 * TOK] = ea
-            pw[rows, 3 * TOK :] = eb
+            scs = [score(BACK, ci, d) for d in near_blocks]
+            top = top_of(scs)
+            es = [jnp.exp(sc - top) for sc in scs]
+            for d, e in zip(near_blocks, es):
+                pw[rows, block_cols(d)] = e
             tops[rows, :] = top
-            sums[rows, :] = jnp.sum(ea, axis=-1, keepdims=True) + jnp.sum(eb, axis=-1, keepdims=True)
+            sums[rows, :] = sum_of(es)
 
     def attend_far():
-        @pl.loop(0, 4)
-        def _(ci):
+        for ci in range(2):
             rows = chunk_rows(ci)
-            sc = scores(BACK, ci, rows, 2, 1)
+            sc = score(BACK, ci, 2)
             top = jnp.maximum(tops[rows, :], jnp.max(sc, axis=-1, keepdims=True))
             e = jnp.exp(sc - top)
+            pw[rows, block_cols(2)] = e
             near = jnp.exp(tops[rows, :] - top)
-            inverse = 1.0 / (sums[rows, :] * near + jnp.sum(e, axis=-1, keepdims=True))
-            near = near * inverse
-            w = jnp.concatenate(
-                [pw[rows, : 2 * TOK] * near, e * inverse, pw[rows, 3 * TOK :] * near], axis=-1
-            )
-            low = w.astype(bf16)
-            pw[rows, :] = w
-            pl_s[rows, :] = low
-            weigh(BACK, ci, low)
+            far = 1.0 / (sums[rows, :] * near + jnp.sum(e, axis=-1, keepdims=True))
+            near = near * far
+            tops[rows, :] = near
+            sums[rows, :] = far
+            lows = []
+            for d in range(5):
+                w = e * far if d == 2 else pw[rows, block_cols(d)] * near
+                lows.append(w.astype(bf16))
+                pl_s[rows, block_cols(d)] = lows[d]
+            weigh(BACK, ci, jnp.concatenate(lows, axis=-1))
 
     def attention(j):
-        @pl.loop(0, 4)
-        def _(ci):
-            sc = scores(j, ci, chunk_rows(ci), 0, 5)
-            e = jnp.exp(sc - jnp.max(sc, axis=-1, keepdims=True))
-            w = e * (1.0 / jnp.sum(e, axis=-1, keepdims=True))
-            weigh(j, ci, w.astype(bf16))
+        for ci in range(2):
+            scs = [score(j, ci, d) for d in range(5)]
+            top = top_of(scs)
+            es = [jnp.exp(sc - top) for sc in scs]
+            inverse = 1.0 / sum_of(es)
+            weigh(j, ci, jnp.concatenate([(e * inverse).astype(bf16) for e in es], axis=-1))
 
     def out_product(j):
         return lambda lhs, n: dot(lhs, wo[j, :, n * CW : (n + 1) * CW])
@@ -450,10 +472,10 @@
     kv_far_in(BACK)
     attend_far()
     loads[5].wait()
-    before = len(drains)
-    scatter_first(BACK, out_product(BACK), rows_all(cx.at[BACK]))
+    scatter_first(BACK, out_product(BACK), rows_all(cx.at[BACK]),
+                  lambda n: scatter_second(BACK, (n,)))
+    scatter_second(BACK, range(NCH - 3, NCH))
     kv_second(FWD)
-    scatter_second(BACK)
     scatter_relay(BACK)
     kv_third(FWD)
     kv_fourth(FWD)
@@ -546,13 +568,14 @@
 
     g_first(1)
 
-    @pl.loop(0, 4)
-    def _(ci):
-        rows = pl.ds(pl.multiple_of(ci * 128, 128), 128)
-        w = pw[rows, :]
-        wg = dot_nt(cgs[rows, :], kvs[BACK, 1].reshape(5 * TOK, HD))
-        delta = jnp.sum(w * wg, axis=-1, keepdims=True)
-        dss[rows, :] = (w * (wg - delta) * (HD ** -0.5)).astype(bf16)
+    for ci in range(2):
+        rows = chunk_rows(ci)
+        near, far = tops[rows, :], sums[rows, :]
+        ws = [pw[rows, block_cols(d)] * (far if d == 2 else near) for d in range(5)]
+        wgs = [dot_nt(cgs[rows, :], kvs[BACK, 1, d]) for d in range(5)]
+        delta = sum_of([w * wg for w, wg in zip(ws, wgs)])
+        for d in range(5):
+            dss[rows, block_cols(d)] = (ws[d] * (wgs[d] - delta)).astype(bf16)
 
     g_first(0)
     g_middle(1)
@@ -565,7 +588,7 @@
 
     for h in range(2):
         rows = slice(h * TOK, (h + 1) * TOK)
-        dq = dot(dss[rows, :], kvs[BACK, 0].reshape(5 * TOK, HD))
+        dq = dot(dss[rows, :], kvs[BACK, 0].reshape(5 * TOK, HD)) * (HD ** -0.5)
         low = rms_back(
             qraw[rows], rope_back(dq, cos_ref[...], sin_ref[...]), q_gain
         ).astype(bf16)
@@ -592,11 +615,8 @@
     lq[:, :, 2 * HD : 3 * HD] = key_low.reshape(8, ROWS, HD)
     lq[:, :, 3 * HD :] = gacc[1, 0].astype(bf16).reshape(8, ROWS, HD)
 
-    for copy, _ in drains[before : before + NCH]:
-        copy.wait_send()
-    del drains[before : before + NCH]
-    scatter_first(2, hidden_product, rows_all(lq))
-    scatter_second(2)
+    scatter_first(2, hidden_product, rows_all(lq), lambda n: scatter_second(2, (n,)))
+    scatter_second(2, range(NCH - 3, NCH))
     fwd_proj = scatter_finish(FWD)
     x_fwd = sti[plan[0, 0]].astype(f32)
     fo[...] = (x_fwd + fwd_proj * rms_of(fwd_proj) * gain(og, FWD)).astype(bf16)
@@ -621,7 +641,24 @@
     arrive(act_out, swap_r.at[1])
     for copy, cond in drains:
         when(cond, copy.wait_send)
+    for r in range(3):
+        sent(r, 0, 6)
     final.wait()
+
+
+def hand_on(act_in, grad_in, act_out, grad_out, held, lsem):
+    pairs = ((act_in, act_out), (grad_in, grad_out))
+    ins = [pltpu.make_async_copy(src, held.at[k], lsem.at[k]) for k, (src, _) in enumerate(pairs)]
+    outs = [
+        pltpu.make_async_copy(held.at[k], dst, lsem.at[2 + k]) for k, (_, dst) in enumerate(pairs)
+    ]
+    for copy in ins:
+        copy.start()
+    for taken, given in zip(ins, outs):
+        taken.wait()
+        given.start()
+    for copy in outs:
+        copy.wait()
 
 
 def per_device(
@@ -646,7 +683,7 @@
             V((2, 8, ROWS, 2 * HD), bf16),
             V((2 * TOK, 5 * TOK), f32), V((2 * TOK, 5 * TOK), bf16), V((2 * TOK, 5 * TOK), bf16),
             V((2 * TOK, HD), bf16),
-            V((2, 4, ROWS, D), bf16), V((3, 4, ROWS, D), bf16), V((3, 3, ROWS, D), bf16),
+            V((4, ROWS, D), bf16), V((3, 4, ROWS, D), bf16), V((2, 3, ROWS, D), bf16),
             V((3, 2, ROWS // 2, D), bf16), V((3, 2, ROWS, D), bf16), V((2, ROWS, D), f32),
             V((2, 4, TOK, HD), bf16), V((5, 2, TOK, HD), bf16), V((2, 3, TOK, HD), f32),
             V((8, ROWS, 4 * HD), bf16),
@@ -655,7 +692,7 @@
             V((2, D), f32), V((2, D), f32), V((2, HD), f32), V((2, HD), f32),
             V((2 * TOK, 1), f32), V((2 * TOK, 1), f32),
             sem((15,)), sem((3, 13)), sem((3, 13)), sem((3, NCH, 7)), sem((3, NCH, 7)),
-            sem((2, 10, 2)), sem((2, 8, 2)), sem((8, 2)), sem((7, 2)), sem((3 + NCH,)), sem((3 + NCH,)),
+            sem((2, 12, 2)), sem((2, 10, 2)), sem((8, 2)), sem((7, 2)), sem((3 + NCH,)), sem((3 + NCH,)),
         ],
         compiler_params=pltpu.CompilerParams(
             collective_id=0, has_side_effects=True, vmem_limit_bytes=67043328
@@ -665,6 +702,13 @@
         key_gain[0], stash_inputs[0], stash_grads[0], query_weight[0], key_weight[0],
         value_weight[0], out_weight[0],
     )
+    act, grad = pl.pallas_call(
+        hand_on,
+        out_shape=(jax.ShapeDtypeStruct((ROWS, D), bf16),) * 2,
+        in_specs=[hbm, hbm],
+        out_specs=(hbm, hbm),
+        scratch_shapes=[V((2, ROWS, D), bf16), sem((4,))],
+    )(act, grad)
     return act[None], grad[None]
 
 

time: 115 us -> 111 us (0.965)
  the two profiles are of different devices: /device:TPU:72 before, /device:TPU:96 now
where the time goes in v5:
time: 111 us
  Pallas kernels  110 us (99%)
    pallas_call x1, Pallas kernels, per_device(): pl.pallas_call(kernel, out_shape=(jax.ShapeDtypeStruct((ROWS, D), bf16),)...  108 us

profile of v5, /device:TPU:96, one launch (start us, length us, event | category | flops | bytes accessed | tf_op | source)
XLA Modules:
  0.0 111.1 jit_solution(5441290444548844888)
XLA Ops:
  0.6 108.5 %shard_map.122 = (bf16[32,3840]{1,0:T(8,128)(2,1)}, bf16[32,3840]{1,0:T(8,128)(2,1)}) custom-call(s32[1,4]{1,0:T(1,128)} %plan.1, f32[2,3840]{1,0:T(2,128)} %bitcast.18, f32[2,3840]{1,0:T(2,128)} %bitcast.19, f32[2,256]{1,0:T(2,128)} %bitcast.20, f32[2,256]{1,0:T(2,128)} %bitcast.21, bf16[4,32,3840]{2,1,0:T(8,128)(2,1)} %bitcast.16, ...), custom_call_target="tpu_custom_call" | custom-call | tf_op jit(solution)/shard_map/pallas_call | solution.py:672
  109.1 1.8 %shard_map.123 = (bf16[32,3840]{1,0:T(8,128)(2,1)}, bf16[32,3840]{1,0:T(8,128)(2,1)}) custom-call(bf16[32,3840]{1,0:T(8,128)(2,1)} %get-tuple-element.6.act_in, bf16[32,3840]{1,0:T(8,128)(2,1)} %get-tuple-element.7.grad_in), custom_call_target="tpu_custom_call" | custom-call | tf_op jit(solution)/shard_map/pallas_call | solution.py:705

commit v6 on v5

--- a/solution.py
+++ b/solution.py
@@ -61,7 +61,7 @@
     act_out, grad_out,
     wq, wk, wv, wo, sti, stg, ag, qs, qraw, kraw, kvs, kvrl, grr, cx, pw, pl_s, dss, cgs,
     ps, pr, sb, rl, fr, own, gs, gr, gacc, lq, fo, go, cos_ref, sin_ref, hq, bo, gb, ig, og, qg, kg, tops, sums,
-    lsem, ags, agr, rss, rsr, kss, ksr, gss, gsr, swap_s, swap_r,
+    lsem, ags, agr, rss, rsr, kss, ksr, gss, gsr, gsc, gcr, gsx, gsh, gsy, gsz, swap_s, swap_r,
 ):
     s = lax.axis_index("segment")
     p = lax.axis_index("ctx")
@@ -132,6 +132,23 @@
         when(cond, copy.start)
         drains.append((copy, cond))
 
+    def launch(copy, cond=None):
+        when(cond, copy.start)
+
+    def owe(ref, ssem, cond=None):
+        drains.append((rcopy(ref, ref, ssem, swap_r.at[0], partner), cond))
+
+    def flush(first, last):
+        groups = {}
+        for copy, cond in drains[first:last]:
+            groups.setdefault(id(cond), (cond, []))[1].append(copy)
+        for cond, copies in groups.values():
+            def run(copies=copies):
+                for copy in copies:
+                    copy.wait_send()
+            when(cond, run)
+        del drains[first:last]
+
     def arrive(dst, rsem, cond=None):
         copy = rcopy(dst, dst, swap_s.at[0], rsem, partner)
         when(cond, copy.wait_recv)
@@ -141,43 +158,37 @@
 
     def gather_start(j):
         blk = ag.at[j, t]
-        send(rcopy(blk.at[H0], blk.at[H0], ags.at[j, 0], agr.at[j, 0], right))
-        send(rcopy(blk.at[H1], blk.at[H1], ags.at[j, 1], agr.at[j, 1], left))
-        send(rcopy(blk.at[H1], blk.at[H1], ags.at[j, 2], agr.at[j, 2], right))
-        send(rcopy(blk.at[H0], blk.at[H0], ags.at[j, 3], agr.at[j, 3], left))
-        send(rcopy(blk, blk, ags.at[j, 6], agr.at[j, 6], partner))
-
-    def across(j, place, half, i):
+        launch(rcopy(blk.at[H0], blk.at[H0], ags.at[j], agr.at[j, 0], right))
+        launch(rcopy(blk.at[H1], blk.at[H1], ags.at[j], agr.at[j, 1], left))
+        launch(rcopy(blk.at[H1], blk.at[H1], ags.at[j], agr.at[j, 2], right))
+        launch(rcopy(blk.at[H0], blk.at[H0], ags.at[j], agr.at[j, 3], left))
+        launch(rcopy(blk, blk, ags.at[j], agr.at[j, 6], partner))
+
+    def across(j, place, half):
         part = ag.at[j, place, halves[half]]
-        send(rcopy(part, part, ags.at[j, i], agr.at[j, i], partner))
+        launch(rcopy(part, part, ags.at[j], agr.at[j, 6], partner))
 
     def gather_relay(j):
         a = ag.at[j, t_l, H0]
         arrive(a, agr.at[j, 0])
-        send(rcopy(a, a, ags.at[j, 4], agr.at[j, 4], right))
+        launch(rcopy(a, a, ags.at[j], agr.at[j, 4], right))
         b = ag.at[j, t_r, H1]
         arrive(b, agr.at[j, 1])
-        send(rcopy(b, b, ags.at[j, 5], agr.at[j, 5], left))
-        across(j, t_l, 0, 7)
-        across(j, t_r, 1, 8)
+        launch(rcopy(b, b, ags.at[j], agr.at[j, 5], left))
+        across(j, t_l, 0)
+        across(j, t_r, 1)
 
     def gather_finish(j):
         arrive(ag.at[j, t_l, H1], agr.at[j, 2])
-        across(j, t_l, 1, 9)
+        across(j, t_l, 1)
         arrive(ag.at[j, t_r, H0], agr.at[j, 3])
-        across(j, t_r, 0, 10)
+        across(j, t_r, 0)
         arrive(ag.at[j, t_o, H0], agr.at[j, 4])
-        across(j, t_o, 0, 11)
+        across(j, t_o, 0)
         arrive(ag.at[j, t_o, H1], agr.at[j, 5])
-        across(j, t_o, 1, 12)
-        u_r, u_l, u_o = t_r + 1 - 2 * c, t_l + 1 - 2 * c, t_o + 1 - 2 * c
-        arrive(ag.at[j, t_p], agr.at[j, 6])
-        arrive(ag.at[j, u_l, H0], agr.at[j, 7])
-        arrive(ag.at[j, u_r, H1], agr.at[j, 8])
-        arrive(ag.at[j, u_l, H1], agr.at[j, 9])
-        arrive(ag.at[j, u_r, H0], agr.at[j, 10])
-        arrive(ag.at[j, u_o, H0], agr.at[j, 11])
-        arrive(ag.at[j, u_o, H1], agr.at[j, 12])
+        across(j, t_o, 1)
+        arrive(ag.at[j, pl.ds(0, 4)], agr.at[j, 6])
+        owe(ag.at[j, pl.ds(0, 7)], ags.at[j])
 
     def cols(n):
         return pl.ds(n * CW, CW)
@@ -190,15 +201,21 @@
         return jnp.concatenate([rows_of(ref, 1 - c), rows_of(ref, c)], axis=0)
 
     def sent(r, first, last):
-        for key in [k for k in flying if k[0] == r and first <= k[1] <= last]:
-            for copy in flying.pop(key):
-                copy.wait_send()
-
-    flying = {}
+        b = r % 2
+        parts = (
+            ps, sb.at[b, 1, H0], sb.at[b, 1, H1], sb.at[b, 0, H1],
+            sb.at[b, 2, H0], sb.at[b, 0, H0], sb.at[b, 2, H1],
+        )
+        for i in range(first, last + 1):
+            if (r, i) in flying:
+                flying.remove((r, i))
+                rcopy(parts[i], parts[i], rss.at[r, i], swap_r.at[0], partner).wait_send()
+
+    flying = set()
 
     def send_sum(r, i, copy):
         copy.start()
-        flying.setdefault((r, i), []).append(copy)
+        flying.add((r, i))
 
     def scatter_first(r, product, lhs, then=None):
         if r:
@@ -209,7 +226,7 @@
             total = product(lhs, n)
             ps[:, :, cols(n)] = total[: 4 * ROWS].astype(bf16).reshape(4, ROWS, CW)
             send_sum(r, 0, rcopy(ps.at[:, :, cols(n)], pr.at[r, :, :, cols(n)],
-                       rss.at[r, n, 0], rsr.at[r, n, 0], partner))
+                       rss.at[r, 0], rsr.at[r, n, 0], partner))
             hq[4 * ROWS :, cols(n)] = total[4 * ROWS :]
 
     def scatter_second(r, numbers=range(NCH)):
@@ -221,13 +238,13 @@
             own[r % 2, :, cols(n)] = total[0]
             sb[r % 2, :, :, cols(n)] = total[1:].astype(bf16)
             send_sum(r, 1, rcopy(sb.at[r % 2, 1, H0, cols(n)], rl.at[r, 0, :, cols(n)],
-                       rss.at[r, n, 1], rsr.at[r, n, 1], right))
+                       rss.at[r, 1], rsr.at[r, n, 1], right))
             send_sum(r, 2, rcopy(sb.at[r % 2, 1, H1, cols(n)], rl.at[r, 1, :, cols(n)],
-                       rss.at[r, n, 2], rsr.at[r, n, 2], left))
+                       rss.at[r, 2], rsr.at[r, n, 2], left))
             send_sum(r, 3, rcopy(sb.at[r % 2, 0, H1, cols(n)], fr.at[r, 0, H1, cols(n)],
-                       rss.at[r, n, 3], rsr.at[r, n, 3], right))
+                       rss.at[r, 3], rsr.at[r, n, 3], right))
             send_sum(r, 4, rcopy(sb.at[r % 2, 2, H0, cols(n)], fr.at[r, 1, H0, cols(n)],
-                       rss.at[r, n, 4], rsr.at[r, n, 4], left))
+                       rss.at[r, 4], rsr.at[r, n, 3], left))
 
     def scatter_relay(r):
         for n in range(NCH):
@@ -236,19 +253,16 @@
                 sb[r % 2, 0, H0, cols(n)].astype(f32) + rl[r, 0, :, cols(n)].astype(f32)
             ).astype(bf16)
             send_sum(r, 5, rcopy(sb.at[r % 2, 0, H0, cols(n)], fr.at[r, 0, H0, cols(n)],
-                       rss.at[r, n, 5], rsr.at[r, n, 5], right))
+                       rss.at[r, 5], rsr.at[r, n, 3], right))
             arrive(rl.at[r, 1, :, cols(n)], rsr.at[r, n, 2])
             sb[r % 2, 2, H1, cols(n)] = (
                 sb[r % 2, 2, H1, cols(n)].astype(f32) + rl[r, 1, :, cols(n)].astype(f32)
             ).astype(bf16)
             send_sum(r, 6, rcopy(sb.at[r % 2, 2, H1, cols(n)], fr.at[r, 1, H1, cols(n)],
-                       rss.at[r, n, 6], rsr.at[r, n, 6], left))
+                       rss.at[r, 6], rsr.at[r, n, 3], left))
 
     def scatter_part(r, n):
-        arrive(fr.at[r, 0, H1, cols(n)], rsr.at[r, n, 3])
-        arrive(fr.at[r, 1, H0, cols(n)], rsr.at[r, n, 4])
-        arrive(fr.at[r, 0, H0, cols(n)], rsr.at[r, n, 5])
-        arrive(fr.at[r, 1, H1, cols(n)], rsr.at[r, n, 6])
+        arrive(fr.at[r, :, :, cols(n)], rsr.at[r, n, 3])
         return own[r % 2, :, cols(n)] + (
             fr[r, 0, :, cols(n)].astype(f32) + fr[r, 1, :, cols(n)].astype(f32)
         )
@@ -267,21 +281,27 @@
     def kv_near(j):
         for i in range(2):
             o = kvs.at[j, i, 0]
-            send(rcopy(o, kvs.at[j, i, 1], kss.at[j, 1, i], ksr.at[j, 1, i], z_up), z < 3)
-            send(rcopy(o, kvs.at[j, i, 3], kss.at[j, 3, i], ksr.at[j, 3, i], z_dn), z == 0)
-            send(rcopy(o, kvs.at[j, i, 2], kss.at[j, 5, i], ksr.at[j, 2, i], z_op), lo & (z == 3))
-            send(rcopy(o, kvs.at[j, i, 3], kss.at[j, 3, i], ksr.at[j, 3, i], z_dn), lo & (z == 1))
+            launch(rcopy(o, kvs.at[j, i, 1], kss.at[j, 1], ksr.at[j, 1, i], z_up), z < 3)
+            launch(rcopy(o, kvs.at[j, i, 3], kss.at[j, 3], ksr.at[j, 3, i], z_dn), z == 0)
+            launch(rcopy(o, kvs.at[j, i, 2], kss.at[j, 5], ksr.at[j, 2, i], z_op), lo & (z == 3))
+            launch(rcopy(o, kvs.at[j, i, 3], kss.at[j, 3], ksr.at[j, 3, i], z_dn), lo & (z == 1))
+        both = kvs.at[j, :, 0]
+        owe(both, kss.at[j, 1], z < 3)
+        owe(both, kss.at[j, 3], (z == 0) | (lo & (z == 1)))
+        owe(both, kss.at[j, 5], lo & (z == 3))
 
     def kv_cross(j):
         k, v = kvs.at[j, 0, 0], kvs.at[j, 1, 0]
-        send(rcopy(k, kvrl.at[j, 0], kss.at[j, 6, 0], ksr.at[j, 0, 0], y_up), lo)
-        send(rcopy(v, kvrl.at[j, 0], kss.at[j, 6, 1], ksr.at[j, 0, 0], y_dn), lo)
+        launch(rcopy(k, kvrl.at[j, 0], kss.at[j, 6], ksr.at[j, 0, 0], y_up), lo)
+        launch(rcopy(v, kvrl.at[j, 0], kss.at[j, 6], ksr.at[j, 0, 0], y_dn), lo)
+        owe(kvs.at[j, :, 0], kss.at[j, 6], lo)
 
     def kv_relay(j):
         b = kvrl.at[j, 0]
         arrive(b, ksr.at[j, 0, 0])
-        send(rcopy(b, kvs.at[j, 0, 4], kss.at[j, 4, 0], ksr.at[j, 4, 0], y_up), relay_k)
-        send(rcopy(b, kvs.at[j, 1, 4], kss.at[j, 4, 1], ksr.at[j, 4, 1], y_dn), relay_v)
+        launch(rcopy(b, kvs.at[j, 0, 4], kss.at[j, 4], ksr.at[j, 4, 0], y_up), relay_k)
+        launch(rcopy(b, kvs.at[j, 1, 4], kss.at[j, 4], ksr.at[j, 4, 1], y_dn), relay_v)
+        owe(b, kss.at[j, 4])
 
     def kv_second(j):
         low = z <= 1
@@ -289,24 +309,31 @@
         for i in range(2):
             b1, b2, b4 = (kvs.at[j, i, d] for d in (1, far, 4))
             arrive(b2, ksr.at[j, far, i], lo & low)
-            send(rcopy(b2, kvrl.at[j, 1], kss.at[j, 0, i], ksr.at[j, 5, 0],
+            launch(rcopy(b2, kvrl.at[j, 1], kss.at[j, 0], ksr.at[j, 5, 0],
                        y_dn if i else y_up), lo & low)
             arrive(b1, ksr.at[j, 1, i], mid)
-            send(rcopy(b1, kvs.at[j, i, 2], kss.at[j, 2, i], ksr.at[j, 2, i], z_up), mid)
+            launch(rcopy(b1, kvs.at[j, i, 2], kss.at[j, 2], ksr.at[j, 2, i], z_up), mid)
             arrive(b4, ksr.at[j, 4, i], hi)
-            send(rcopy(b4, kvs.at[j, i, 3], kss.at[j, 3, i], ksr.at[j, 3, i], z_dn), hi & (z == 3))
+            launch(rcopy(b4, kvs.at[j, i, 3], kss.at[j, 10], ksr.at[j, 3, i], z_dn), hi & (z == 3))
             for q in range(2):
-                send(rcopy(b4.at[TH[q]], kvs.at[j, i, 3, TH[q]], kss.at[j, 8 + i, q],
+                launch(rcopy(b4.at[TH[q]], kvs.at[j, i, 3, TH[q]], kss.at[j, 8],
                            ksr.at[j, 6 + i, q], z_dn), hi & (z == 2))
-            send(rcopy(b4, kvs.at[j, i, 1], kss.at[j, 1, i], ksr.at[j, 1, i], z_up), hi & (z == 3))
+            launch(rcopy(b4, kvs.at[j, i, 1], kss.at[j, 11], ksr.at[j, 1, i], z_up), hi & (z == 3))
+        both = kvs.at[j, :, 0]
+        owe(both, kss.at[j, 0], lo & low)
+        owe(both, kss.at[j, 2], mid)
+        owe(both, kss.at[j, 10], hi & (z == 3))
+        owe(both, kss.at[j, 8], hi & (z == 2))
+        owe(both, kss.at[j, 11], hi & (z == 3))
 
     def kv_third(j):
         low = z <= 1
         b = kvrl.at[j, 1]
         arrive(b, ksr.at[j, 5, 0], low)
         far = jnp.maximum(3 - z, 2)
-        send(rcopy(b, kvs.at[j, 0, far], kss.at[j, 7, 0], ksr.at[j, far, 0], y_up), low & relay_k)
-        send(rcopy(b, kvs.at[j, 1, far], kss.at[j, 7, 1], ksr.at[j, far, 1], y_dn), low & relay_v)
+        launch(rcopy(b, kvs.at[j, 0, far], kss.at[j, 7], ksr.at[j, far, 0], y_up), low & relay_k)
+        launch(rcopy(b, kvs.at[j, 1, far], kss.at[j, 7], ksr.at[j, far, 1], y_dn), low & relay_v)
+        owe(b, kss.at[j, 7], low)
 
     def kv_fourth(j):
         cond = hi & (z == 1)
@@ -314,8 +341,10 @@
             for q in range(2):
                 b3 = kvs.at[j, i, 3, TH[q]]
                 arrive(b3, ksr.at[j, 6 + i, q], cond)
-                send(rcopy(b3, kvs.at[j, i, 2, TH[q]], kss.at[j, 10 + i, q],
+                launch(rcopy(b3, kvs.at[j, i, 2, TH[q]], kss.at[j, 9],
                            ksr.at[j, 8 + i, q], z_dn), cond)
+        owe(kvs.at[j, :, 0], kss.at[j, 9], cond)
+
 
     def kv_near_in(j):
         for i in range(2):
@@ -506,7 +535,7 @@
         ).astype(bf16)
     q_gain, k_gain = gain(qg, BACK), gain(kg, BACK)
 
-    R1, R2, R3, R4, R5, RR, RS = 0, 1, 2, 3, 4, 5, 6
+    R1, R2, R3, R4, R5 = 0, 1, 2, 3, 4
     OWN, ONE, FOUR = 0, 1, 2
 
     def grad_block(i, d):
@@ -524,10 +553,44 @@
         def _():
             gacc[i, k] = gacc[i, k] + gr[e, i].astype(f32)
 
+    def g_cross(i, d, far, cond):
+        for h, device in enumerate((y_dn, y_up)):
+            send(rcopy(gs.at[i, d - 1, TH[h]], grr.at[far, i], gsc.at[far, i, h],
+                       gcr.at[far, i], device), cond)
+
+    def g_relay(i, far):
+        cond = z <= 1 if far else None
+        e = R5 if far else R4
+        buf = grr.at[far, i]
+        arrive(buf, gcr.at[far, i], cond)
+        for h, (role, device) in enumerate(((relay_k, y_dn), (relay_v, y_up))):
+            send(rcopy(buf, gr.at[e, i, TH[h]], gsx.at[far, i], gsh.at[far, i, h], device),
+                 role & cond if far else role)
+
+    def g_halves(i, far, cond):
+        for h in range(2):
+            arrive(gr.at[R5 if far else R4, i, TH[h]], gsh.at[far, i, h], cond)
+
+    def g_forward(i):
+        cond = lo & (z <= 1)
+        g_halves(i, 1, cond)
+        ahead_cond = cond if i else lo & (z == 1)
+        send(rcopy(gr.at[R5, i], gr.at[R5, i], gss.at[7, i], gsr.at[R5, i], z_op), ahead_cond)
+        if i == 0:
+            for h in range(2):
+                send(rcopy(gr.at[R5, 0, TH[h]], gr.at[R3, 0, TH[h]], gsz.at[h], gsy.at[0, h], z_up),
+                     lo & (z == 0))
+
+    def g_forward_again():
+        cond = lo & (z == 1)
+        for h in range(2):
+            part = gr.at[R3, 0, TH[h]]
+            arrive(part, gsy.at[0, h], cond)
+            send(rcopy(part, gr.at[R5, 0, TH[h]], gsz.at[h], gsy.at[1, h], z_up), cond)
+
     def g_first(i):
         gs[i, 1] = grad_block(i, 2).astype(bf16)
-        send(rcopy(gs.at[i, 1], grr.at[1], gss.at[1, i], gsr.at[RS, 0],
-                   y_up if i else y_dn), hi & (z <= 1))
+        g_cross(i, 2, 1, hi & (z <= 1))
         g_send(2, R2, 0, z_dn, z >= 2, i)
         gs[i, 2] = grad_block(i, 3).astype(bf16)
         g_send(3, R3, 2, z_up, (z == 3) | hi, i)
@@ -549,23 +612,9 @@
         g_add(R3, FOUR, hi & (z >= 1), i)
         g_add(R1, FOUR, hi & (z == 3), i)
         gs[i, 3] = gacc[i, FOUR].astype(bf16)
-        send(rcopy(gs.at[i, 3], grr.at[0], gss.at[4, i], gsr.at[RR, 0],
-                   y_up if i else y_dn), hi)
-
-    def g_relay(i, far):
-        cond, device = (relay_v, y_up) if i else (relay_k, y_dn)
-        if far:
-            cond = cond & (z <= 1)
-        buf, rsem = grr.at[far], gsr.at[RS if far else RR, 0]
-        e = R5 if far else R4
-        arrive(buf, rsem, cond)
-        send(rcopy(buf, gr.at[e, i], gss.at[6 if far else 5, i], gsr.at[e, i], device), cond)
-
-    def g_forward(i):
-        cond = lo & (z <= 1)
-        arrive(gr.at[R5, i], gsr.at[R5, i], cond)
-        send(rcopy(gr.at[R5, i], gr.at[R5, i], gss.at[7, i], gsr.at[R5, i], z_op), cond)
-
+        g_cross(i, 4, 0, hi)
+
+    early = len(drains)
     g_first(1)
 
     for ci in range(2):
@@ -579,12 +628,12 @@
 
     g_first(0)
     g_middle(1)
+    g_relay(1, 1)
     g_third(1)
-    g_relay(1, 1)
     scatter_second(FWD)
     g_middle(0)
+    g_relay(0, 1)
     g_third(0)
-    g_relay(0, 1)
 
     for h in range(2):
         rows = slice(h * TOK, (h + 1) * TOK)
@@ -601,14 +650,31 @@
     g_relay(1, 0)
     g_forward(0)
     g_relay(0, 0)
+    g_forward_again()
     for copy in ahead:
         copy.wait_send()
     scatter_relay(FWD)
+    flush(0, early)
+    sent(0, 0, 6)
+    sent(1, 0, 4)
     for i in (1, 0):
         g_add(R1, OWN, z < 3, i)
         g_add(R3, OWN, z == 0, i)
-        g_add(R4, OWN, lo, i)
-        g_add(R5, OWN, lo & (z >= 2), i)
+        g_halves(i, 0, lo)
+
+        @pl.when(lo)
+        def _():
+            gacc[i, OWN] = gacc[i, OWN] + gr[R4, i].astype(f32)
+        if i:
+            g_add(R5, OWN, lo & (z >= 2), i)
+        else:
+            for h in range(2):
+                arrive(gr.at[R5, 0, TH[h]], gsy.at[1, h], lo & (z == 2))
+            arrive(gr.at[R5, 0], gsr.at[R5, 0], lo & (z == 3))
+
+            @pl.when(lo & (z >= 2))
+            def _():
+                gacc[0, OWN] = gacc[0, OWN] + gr[R5, 0].astype(f32)
     key_low = rms_back(
         kraw[...], rope_back(gacc[0, 0], cos_ref[...], sin_ref[...]), k_gain
     ).astype(bf16)
@@ -622,6 +688,9 @@
     fo[...] = (x_fwd + fwd_proj * rms_of(fwd_proj) * gain(og, FWD)).astype(bf16)
     send(rcopy(fo, act_out, swap_s.at[1], swap_r.at[1], other))
     scatter_relay(2)
+    flush(0, len(drains))
+    sent(1, 0, 6)
+    sent(2, 0, 4)
     for n in range(NCH):
         hidden = scatter_part(2, n)
         gb[0, :, cols(n)] = (hidden * ig[pl.ds(legs[BACK], 1), cols(n)]).astype(bf16)
@@ -639,10 +708,8 @@
     final = pltpu.make_async_copy(go, grad_out, lsem.at[10])
     final.start()
     arrive(act_out, swap_r.at[1])
-    for copy, cond in drains:
-        when(cond, copy.wait_send)
-    for r in range(3):
-        sent(r, 0, 6)
+    flush(0, len(drains))
+    sent(2, 0, 6)
     final.wait()
 
 
@@ -679,7 +746,7 @@
             V((4, ROWS, D), bf16), V((4, ROWS, D), bf16),
             V((3, 8, ROWS, D), bf16),
             V((2, 2 * TOK, HD), bf16), V((2 * TOK, HD), f32), V((TOK, HD), f32),
-            V((2, 2, 5, TOK, HD), bf16), V((2, 2, TOK, HD), bf16), V((2, TOK, HD), bf16),
+            V((2, 2, 5, TOK, HD), bf16), V((2, 2, TOK, HD), bf16), V((2, 2, TOK // 2, HD), bf16),
             V((2, 8, ROWS, 2 * HD), bf16),
             V((2 * TOK, 5 * TOK), f32), V((2 * TOK, 5 * TOK), bf16), V((2 * TOK, 5 * TOK), bf16),
             V((2 * TOK, HD), bf16),
@@ -691,8 +758,9 @@
             V((2 * 4 * ROWS, D), f32), V((2, ROWS, D), bf16), V((2, ROWS, D), bf16),
             V((2, D), f32), V((2, D), f32), V((2, HD), f32), V((2, HD), f32),
             V((2 * TOK, 1), f32), V((2 * TOK, 1), f32),
-            sem((15,)), sem((3, 13)), sem((3, 13)), sem((3, NCH, 7)), sem((3, NCH, 7)),
-            sem((2, 12, 2)), sem((2, 10, 2)), sem((8, 2)), sem((7, 2)), sem((3 + NCH,)), sem((3 + NCH,)),
+            sem((15,)), sem((3,)), sem((3, 7)), sem((3, 7)), sem((3, NCH, 4)),
+            sem((2, 12)), sem((2, 10, 2)), sem((8, 2)), sem((5, 2)),
+            sem((2, 2, 2)), sem((2, 2)), sem((2, 2)), sem((2, 2, 2)), sem((2, 2)), sem((2,)), sem((3 + NCH,)), sem((3 + NCH,)),
         ],
         compiler_params=pltpu.CompilerParams(
             collective_id=0, has_side_effects=True, vmem_limit_bytes=67043328

time: 111 us -> 108 us (0.973)
  the two profiles are of different devices: /device:TPU:96 before, /device:TPU:72 now
where the time goes in v6:
time: 108 us; the launch traced here: 107 us
  Pallas kernels  107 us (99%)
    pallas_call x1, Pallas kernels, per_device(): pl.pallas_call(kernel, out_shape=(jax.ShapeDtypeStruct((ROWS, D), bf16),)...  105 us

profile of v6, /device:TPU:72, one launch (start us, length us, event | category | flops | bytes accessed | tf_op | source)
XLA Modules:
  0.0 107.4 jit_solution(12275874870112051333)
XLA Ops:
  0.6 104.8 %shard_map.122 = (bf16[32,3840]{1,0:T(8,128)(2,1)}, bf16[32,3840]{1,0:T(8,128)(2,1)}) custom-call(s32[1,4]{1,0:T(1,128)} %plan.1, f32[2,3840]{1,0:T(2,128)} %bitcast.18, f32[2,3840]{1,0:T(2,128)} %bitcast.19, f32[2,256]{1,0:T(2,128)} %bitcast.20, f32[2,256]{1,0:T(2,128)} %bitcast.21, bf16[4,32,3840]{2,1,0:T(8,128)(2,1)} %bitcast.16, ...), custom_call_target="tpu_custom_call" | custom-call | tf_op jit(solution)/shard_map/pallas_call | solution.py:739
  105.5 1.8 %shard_map.123 = (bf16[32,3840]{1,0:T(8,128)(2,1)}, bf16[32,3840]{1,0:T(8,128)(2,1)}) custom-call(bf16[32,3840]{1,0:T(8,128)(2,1)} %get-tuple-element.6.act_in, bf16[32,3840]{1,0:T(8,128)(2,1)} %get-tuple-element.7.grad_in), custom_call_target="tpu_custom_call" | custom-call | tf_op jit(solution)/shard_map/pallas_call | solution.py:773

commit v7 on v6

--- a/solution.py
+++ b/solution.py
@@ -58,9 +58,9 @@
 
 def kernel(
     plan, ig_h, og_h, qg_h, kg_h, si, sg, wq_h, wk_h, wv_h, wo_h,
-    act_out, grad_out,
+    act_out, g_out, xi_out,
     wq, wk, wv, wo, sti, stg, ag, qs, qraw, kraw, kvs, kvrl, grr, cx, pw, pl_s, dss, cgs,
-    ps, pr, sb, rl, fr, own, gs, gr, gacc, lq, fo, go, cos_ref, sin_ref, hq, bo, gb, ig, og, qg, kg, tops, sums,
+    ps, pr, sb, rl, fr, own, gs, gr, gacc, lq, fo, go, cos_ref, sin_ref, hq, gb, ig, og, qg, kg, tops, sums,
     lsem, ags, agr, rss, rsr, kss, ksr, gss, gsr, gsc, gcr, gsx, gsh, gsy, gsz, swap_s, swap_r,
 ):
     s = lax.axis_index("segment")
@@ -229,6 +229,12 @@
                        rss.at[r, 0], rsr.at[r, n, 0], partner))
             hq[4 * ROWS :, cols(n)] = total[4 * ROWS :]
 
+    def send_direct(r, n):
+        send_sum(r, 3, rcopy(sb.at[r % 2, 0, H1, cols(n)], fr.at[r, 0, H1, cols(n)],
+                             rss.at[r, 3], rsr.at[r, n, 3], right))
+        send_sum(r, 4, rcopy(sb.at[r % 2, 2, H0, cols(n)], fr.at[r, 1, H0, cols(n)],
+                             rss.at[r, 4], rsr.at[r, n, 3], left))
+
     def scatter_second(r, numbers=range(NCH)):
         if r == 2 and 0 in numbers:
             sent(0, 1, 6)
@@ -241,10 +247,8 @@
                        rss.at[r, 1], rsr.at[r, n, 1], right))
             send_sum(r, 2, rcopy(sb.at[r % 2, 1, H1, cols(n)], rl.at[r, 1, :, cols(n)],
                        rss.at[r, 2], rsr.at[r, n, 2], left))
-            send_sum(r, 3, rcopy(sb.at[r % 2, 0, H1, cols(n)], fr.at[r, 0, H1, cols(n)],
-                       rss.at[r, 3], rsr.at[r, n, 3], right))
-            send_sum(r, 4, rcopy(sb.at[r % 2, 2, H0, cols(n)], fr.at[r, 1, H0, cols(n)],
-                       rss.at[r, 4], rsr.at[r, n, 3], left))
+            if r == 1:
+                send_direct(r, n)
 
     def scatter_relay(r):
         for n in range(NCH):
@@ -260,6 +264,8 @@
             ).astype(bf16)
             send_sum(r, 6, rcopy(sb.at[r % 2, 2, H1, cols(n)], fr.at[r, 1, H1, cols(n)],
                        rss.at[r, 6], rsr.at[r, n, 3], left))
+            if r != 1:
+                send_direct(r, n)
 
     def scatter_part(r, n):
         arrive(fr.at[r, :, :, cols(n)], rsr.at[r, n, 3])
@@ -335,15 +341,15 @@
         launch(rcopy(b, kvs.at[j, 1, far], kss.at[j, 7], ksr.at[j, far, 1], y_dn), low & relay_v)
         owe(b, kss.at[j, 7], low)
 
-    def kv_fourth(j):
+    def kv_fourth(j, pieces=((0, 0), (0, 1), (1, 0), (1, 1))):
         cond = hi & (z == 1)
-        for i in range(2):
-            for q in range(2):
-                b3 = kvs.at[j, i, 3, TH[q]]
-                arrive(b3, ksr.at[j, 6 + i, q], cond)
-                launch(rcopy(b3, kvs.at[j, i, 2, TH[q]], kss.at[j, 9],
-                           ksr.at[j, 8 + i, q], z_dn), cond)
-        owe(kvs.at[j, :, 0], kss.at[j, 9], cond)
+        for i, q in pieces:
+            b3 = kvs.at[j, i, 3, TH[q]]
+            arrive(b3, ksr.at[j, 6 + i, q], cond)
+            launch(rcopy(b3, kvs.at[j, i, 2, TH[q]], kss.at[j, 9],
+                         ksr.at[j, 8 + i, q], z_dn), cond)
+        if (1, 1) in pieces:
+            owe(kvs.at[j, :, 0], kss.at[j, 9], cond)
 
 
     def kv_near_in(j):
@@ -492,9 +498,10 @@
     gather_finish(FWD)
     kv_second(BACK)
     project(FWD)
+    kv_fourth(BACK, ((0, 0),))
     kv_third(BACK)
     kv_cross(FWD)
-    kv_fourth(BACK)
+    kv_fourth(BACK, ((0, 1), (1, 0), (1, 1)))
     kv_near_in(BACK)
     attend_near()
     kv_relay(FWD)
@@ -516,8 +523,8 @@
     go[...] = sti[plan[0, 1]]
     fo[...] = stg[plan[0, 1]]
     ahead = (
-        rcopy(go, bo.at[0], swap_s.at[2], swap_r.at[2], other),
-        rcopy(fo, bo.at[1], swap_s.at[0], swap_r.at[0], other),
+        rcopy(go, xi_out.at[0], swap_s.at[2], swap_r.at[2], other),
+        rcopy(fo, xi_out.at[1], swap_s.at[0], swap_r.at[0], other),
     )
     for copy in ahead:
         copy.start()
@@ -649,14 +656,18 @@
     g_forward(1)
     g_relay(1, 0)
     g_forward(0)
+    scatter_relay(FWD)
     g_relay(0, 0)
     g_forward_again()
     for copy in ahead:
         copy.wait_send()
-    scatter_relay(FWD)
     flush(0, early)
     sent(0, 0, 6)
     sent(1, 0, 4)
+    fwd_proj = scatter_finish(FWD)
+    x_fwd = sti[plan[0, 0]].astype(f32)
+    fo[...] = (x_fwd + fwd_proj * rms_of(fwd_proj) * gain(og, FWD)).astype(bf16)
+    send(rcopy(fo, act_out, swap_s.at[1], swap_r.at[1], other))
     for i in (1, 0):
         g_add(R1, OWN, z < 3, i)
         g_add(R3, OWN, z == 0, i)
@@ -683,47 +694,45 @@
 
     scatter_first(2, hidden_product, rows_all(lq), lambda n: scatter_second(2, (n,)))
     scatter_second(2, range(NCH - 3, NCH))
-    fwd_proj = scatter_finish(FWD)
-    x_fwd = sti[plan[0, 0]].astype(f32)
-    fo[...] = (x_fwd + fwd_proj * rms_of(fwd_proj) * gain(og, FWD)).astype(bf16)
-    send(rcopy(fo, act_out, swap_s.at[1], swap_r.at[1], other))
     scatter_relay(2)
     flush(0, len(drains))
     sent(1, 0, 6)
-    sent(2, 0, 4)
+    sent(2, 0, 2)
     for n in range(NCH):
         hidden = scatter_part(2, n)
-        gb[0, :, cols(n)] = (hidden * ig[pl.ds(legs[BACK], 1), cols(n)]).astype(bf16)
-        send(rcopy(gb.at[0, :, cols(n)], gb.at[1, :, cols(n)],
+        gb[:, cols(n)] = (hidden * ig[pl.ds(legs[BACK], 1), cols(n)]).astype(bf16)
+        send(rcopy(gb.at[:, cols(n)], g_out.at[:, cols(n)],
                    swap_s.at[3 + n], swap_r.at[3 + n], other))
-    arrive(bo.at[0], swap_r.at[2])
-    arrive(bo.at[1], swap_r.at[0])
-    x_other = bo[0].astype(f32)
-    scale = rms_of(x_other)
+    arrive(xi_out.at[0], swap_r.at[2])
+    arrive(xi_out.at[1], swap_r.at[0])
     for n in range(NCH):
-        arrive(gb.at[1, :, cols(n)], swap_r.at[3 + n])
-    g = gb[1].astype(f32)
-    centred = g - x_other * (scale * scale * jnp.mean(g * x_other, axis=-1, keepdims=True))
-    go[...] = (bo[1].astype(f32) + scale * centred).astype(bf16)
-    final = pltpu.make_async_copy(go, grad_out, lsem.at[10])
-    final.start()
+        arrive(g_out.at[:, cols(n)], swap_r.at[3 + n])
     arrive(act_out, swap_r.at[1])
     flush(0, len(drains))
     sent(2, 0, 6)
-    final.wait()
-
-
-def hand_on(act_in, grad_in, act_out, grad_out, held, lsem):
-    pairs = ((act_in, act_out), (grad_in, grad_out))
-    ins = [pltpu.make_async_copy(src, held.at[k], lsem.at[k]) for k, (src, _) in enumerate(pairs)]
+
+
+def hand_on(act_in, g_in, xi_in, act_out, grad_out, act, g, xi, lsem):
+    ins = [
+        pltpu.make_async_copy(src, dst, lsem.at[k])
+        for k, (src, dst) in enumerate(((xi_in, xi), (g_in, g), (act_in, act)))
+    ]
     outs = [
-        pltpu.make_async_copy(held.at[k], dst, lsem.at[2 + k]) for k, (_, dst) in enumerate(pairs)
+        pltpu.make_async_copy(src, dst, lsem.at[3 + k])
+        for k, (src, dst) in enumerate(((act, act_out), (g, grad_out)))
     ]
     for copy in ins:
         copy.start()
-    for taken, given in zip(ins, outs):
-        taken.wait()
-        given.start()
+    ins[0].wait()
+    x = xi[0].astype(f32)
+    scale = rms_of(x)
+    ins[1].wait()
+    grad = g[...].astype(f32)
+    centred = grad - x * (scale * scale * jnp.mean(grad * x, axis=-1, keepdims=True))
+    g[...] = (xi[1].astype(f32) + scale * centred).astype(bf16)
+    outs[1].start()
+    ins[2].wait()
+    outs[0].start()
     for copy in outs:
         copy.wait()
 
@@ -736,11 +745,12 @@
     smem = pl.BlockSpec(memory_space=pltpu.SMEM)
     V = pltpu.VMEM
     sem = pltpu.SemaphoreType.DMA
-    act, grad = pl.pallas_call(
+    act, g, xi = pl.pallas_call(
         kernel,
-        out_shape=(jax.ShapeDtypeStruct((ROWS, D), bf16),) * 2,
+        out_shape=(jax.ShapeDtypeStruct((ROWS, D), bf16),) * 2
+        + (jax.ShapeDtypeStruct((2, ROWS, D), bf16),),
         in_specs=[smem] + [hbm] * 10,
-        out_specs=(hbm, hbm),
+        out_specs=(hbm,) * 3,
         scratch_shapes=[
             V((2, D, 2 * HD), bf16), V((2, D, HD), bf16), V((2, D, HD), bf16), V((2, 2 * HD, D), bf16),
             V((4, ROWS, D), bf16), V((4, ROWS, D), bf16),
@@ -755,7 +765,7 @@
             V((2, 4, TOK, HD), bf16), V((5, 2, TOK, HD), bf16), V((2, 3, TOK, HD), f32),
             V((8, ROWS, 4 * HD), bf16),
             V((ROWS, D), bf16), V((ROWS, D), bf16), V((TOK, HD // 2), f32), V((TOK, HD // 2), f32),
-            V((2 * 4 * ROWS, D), f32), V((2, ROWS, D), bf16), V((2, ROWS, D), bf16),
+            V((2 * 4 * ROWS, D), f32), V((ROWS, D), bf16),
             V((2, D), f32), V((2, D), f32), V((2, HD), f32), V((2, HD), f32),
             V((2 * TOK, 1), f32), V((2 * TOK, 1), f32),
             sem((15,)), sem((3,)), sem((3, 7)), sem((3, 7)), sem((3, NCH, 4)),
@@ -773,10 +783,10 @@
     act, grad = pl.pallas_call(
         hand_on,
         out_shape=(jax.ShapeDtypeStruct((ROWS, D), bf16),) * 2,
-        in_specs=[hbm, hbm],
+        in_specs=[hbm] * 3,
         out_specs=(hbm, hbm),
-        scratch_shapes=[V((2, ROWS, D), bf16), sem((4,))],
-    )(act, grad)
+        scratch_shapes=[V((ROWS, D), bf16), V((ROWS, D), bf16), V((2, ROWS, D), bf16), sem((5,))],
+    )(act, g, xi)
     return act[None], grad[None]
 
 

time: 108 us -> 105 us (0.972)
  Pallas kernels: 107 us -> 104 us
    pallas_call x1, Pallas kernels: 105 us -> 102 us  [per_device(): pl.pallas_call(kernel, out_shape=(jax.ShapeDtypeStruct((ROWS, D), bf16),)...]
where the time goes in v7:
time: 105 us
  Pallas kernels  104 us (99%)
    pallas_call x1, Pallas kernels, per_device(): pl.pallas_call(kernel, out_shape=(jax.ShapeDtypeStruct((ROWS, D), bf16),)...  102 us
    pallas_call x1, Pallas kernels, per_device(): pl.pallas_call(hand_on, out_shape=(jax.ShapeDtypeStruct((ROWS, D), bf16),...  2.23 us

profile of v7, /device:TPU:72, one launch (start us, length us, event | category | flops | bytes accessed | tf_op | source)
XLA Modules:
  0.0 105.0 jit_solution(9056408272232025745)
XLA Ops:
  0.6 101.9 %shard_map.122 = (bf16[32,3840]{1,0:T(8,128)(2,1)}, bf16[32,3840]{1,0:T(8,128)(2,1)}, bf16[2,32,3840]{2,1,0:T(8,128)(2,1)}) custom-call(s32[1,4]{1,0:T(1,128)} %plan.1, f32[2,3840]{1,0:T(2,128)} %bitcast.18, f32[2,3840]{1,0:T(2,128)} %bitcast.19, f32[2,256]{1,0:T(2,128)} %bitcast.20, f32[2,256]{1,0:T(2,128)} %bitcast.21, bf16[4,32,3840]{2,1,0:T(8,128)(2,1)} %bitcast.16, ...), custom_call_target="tpu_custom_call" | custom-call | tf_op jit(solution)/shard_map/pallas_call | solution.py:748
  102.6 2.2 %shard_map.123 = (bf16[32,3840]{1,0:T(8,128)(2,1)}, bf16[32,3840]{1,0:T(8,128)(2,1)}) custom-call(bf16[32,3840]{1,0:T(8,128)(2,1)} %get-tuple-element.7.act_in, bf16[32,3840]{1,0:T(8,128)(2,1)} %get-tuple-element.8.g_in, bf16[2,32,3840]{2,1,0:T(8,128)(2,1)} %get-tuple-element.9.xi_in), custom_call_target="tpu_custom_call" | custom-call | tf_op jit(solution)/shard_map/pallas_call | solution.py:783

commit v8 on v7

--- a/solution.py
+++ b/solution.py
@@ -16,7 +16,7 @@
 ROWS = 32
 TOK = 256
 HD = 256
-NCH = 5
+NCH = 6
 CW = D // NCH
 BACK, FWD, GRAD = 0, 1, 2
 f32 = jnp.float32
@@ -724,6 +724,8 @@
     for copy in ins:
         copy.start()
     ins[0].wait()
+    ins[2].wait()
+    outs[0].start()
     x = xi[0].astype(f32)
     scale = rms_of(x)
     ins[1].wait()
@@ -731,8 +733,6 @@
     centred = grad - x * (scale * scale * jnp.mean(grad * x, axis=-1, keepdims=True))
     g[...] = (xi[1].astype(f32) + scale * centred).astype(bf16)
     outs[1].start()
-    ins[2].wait()
-    outs[0].start()
     for copy in outs:
         copy.wait()
 

time: 105 us -> 106 us (level)
  no operation moved by 1% of the time
where the time goes in v8:
time: 106 us
  Pallas kernels  105 us (99%)
    pallas_call x1, Pallas kernels, per_device(): pl.pallas_call(kernel, out_shape=(jax.ShapeDtypeStruct((ROWS, D), bf16),)...  102 us
    pallas_call x1, Pallas kernels, per_device(): pl.pallas_call(hand_on, out_shape=(jax.ShapeDtypeStruct((ROWS, D), bf16),...  2.33 us

profile of v8, /device:TPU:72, one launch (start us, length us, event | category | flops | bytes accessed | tf_op | source)
XLA Modules:
  0.0 105.6 jit_solution(8354907190829982238)
XLA Ops:
  0.6 102.5 %shard_map.122 = (bf16[32,3840]{1,0:T(8,128)(2,1)}, bf16[32,3840]{1,0:T(8,128)(2,1)}, bf16[2,32,3840]{2,1,0:T(8,128)(2,1)}) custom-call(s32[1,4]{1,0:T(1,128)} %plan.1, f32[2,3840]{1,0:T(2,128)} %bitcast.18, f32[2,3840]{1,0:T(2,128)} %bitcast.19, f32[2,256]{1,0:T(2,128)} %bitcast.20, f32[2,256]{1,0:T(2,128)} %bitcast.21, bf16[4,32,3840]{2,1,0:T(8,128)(2,1)} %bitcast.16, ...), custom_call_target="tpu_custom_call" | custom-call | tf_op jit(solution)/shard_map/pallas_call | solution.py:748
  103.1 2.3 %shard_map.123 = (bf16[32,3840]{1,0:T(8,128)(2,1)}, bf16[32,3840]{1,0:T(8,128)(2,1)}) custom-call(bf16[32,3840]{1,0:T(8,128)(2,1)} %get-tuple-element.7.act_in, bf16[32,3840]{1,0:T(8,128)(2,1)} %get-tuple-element.8.g_in, bf16[2,32,3840]{2,1,0:T(8,128)(2,1)} %get-tuple-element.9.xi_in), custom_call_target="tpu_custom_call" | custom-call | tf_op jit(solution)/shard_map/pallas_call | solution.py:783
